TPU v7x, 32 devices: a whole 2x2x4 slice. The times are simulated.
32 devices in a mesh: parts: 1, rows: 8 (over z, y), branch: 2 (over core), head: 2 (over x).
Axes of the slice: x: 2, y: 2, z: 4, core: 2. Of those that a mesh axis runs over, the one named last changes fastest.
Arguments:
- lineup_state: bfloat16 [32, 128, 256], P(('parts', 'rows', 'branch')), may hold values from -12 to 12
- pairwise: bfloat16 [128, 128, 128], P(('parts', 'rows', 'branch')), may hold values from -12 to 12
- aligned_residue_bounds: int32 [32, 2], P('parts'), may hold values from 0 to 128, as said below
- residue_valid_mask: int32 [128], P('parts'), may hold values from 0 to 1, as said below
- coupling_offset_weight_map: bfloat16 [128, 8], P(None, 'head'), may hold values from -0.5 to 0.5
- triangle_bias_matrix: bfloat16 [128, 4], P(None, 'head'), may hold values from -0.5 to 0.5
- alignment_projection_matrix: bfloat16 [4, 256, 256], P(None, None, 'head'), may hold values from -1 to 1
- lineup_readout_weight: bfloat16 [256, 256], replicated, may hold values from -4 to 4
- feedfwd_entry_weight: bfloat16 [256, 1024], P(None, 'head'), may hold values from -0.375 to 0.375
- feedfwd_exit_weight: bfloat16 [1024, 256], P('head'), may hold values from -0.1875 to 0.1875
- pair_projection_matrix: bfloat16 [4, 128, 128], P(None, None, 'head'), may hold values from -2 to 2
- pair_output_matrix: bfloat16 [128, 128], P(None, 'head'), may hold values from -6 to 6
- left_right_maps: bfloat16 [2, 256, 32], replicated, may hold values from -0.375 to 0.375
- outer_product_output_matrix: bfloat16 [1024, 128], P(None, 'head'), may hold values from -1.5 to 1.5
Outputs:
- refreshed_lineup_state: bfloat16 [32, 128, 256], P(('parts', 'rows', 'branch'), None, 'head')
- pairwise_out: bfloat16 [128, 128, 128], P(('parts', 'rows', 'branch'), None, 'head')
Inputs may be any that keep to these rules, and one draw needn't show every extreme that they name: `aligned_residue_bounds`: each row holds a start below its end; row 0 covers all 128 residues; every span covers a quarter of the 128 residues or more and starts in the first half. `residue_valid_mask`: 1 on a prefix that holds at least half of the 128 residues, 0 after it; the last residue is always 0.
All inputs are finite; a program needn't handle non-finite values.
Results may differ from a plain program's by a relative error of at most 0.011.
Values may be sent and summed in bfloat16 or wider, within the bound.
No kernel may reach another device: no remote copies, remote signals or barrier semaphores. Data moves between devices by JAX's collectives and lax.ppermute only.
A program may use at most 64 MiB of HBM per device.

v0:
```python
import math

import jax
import jax.numpy as jnp
from jax import lax
from jax.sharding import PartitionSpec as P

PER_FOCUS_DIM = 32


def layer_normalize(values):
    values = values.astype(jnp.float32)
    center = values - jnp.mean(values, -1, keepdims=True)
    spread = jnp.mean(center * center, -1, keepdims=True)
    return center * lax.rsqrt(spread + 1e-05)


def soft_weights(attention_scores):
    row_max = jnp.max(attention_scores, -1, keepdims=True)
    shifted = jnp.exp(attention_scores - row_max)
    return (shifted / jnp.sum(shifted, -1, keepdims=True)).astype(jnp.bfloat16)


def span_mask(aligned_residue_bounds, length_value):
    places = jnp.arange(length_value, dtype=jnp.int32)
    inside = (places[None, :] >= aligned_residue_bounds[:, 0:1]) & (
        places[None, :] < aligned_residue_bounds[:, 1:2]
    )
    return inside.astype(jnp.float32)


def local(
    lineup_state,
    pairwise,
    aligned_residue_bounds,
    residue_valid_mask,
    coupling_offset_weight_map,
    triangle_bias_matrix,
    alignment_projection_matrix,
    lineup_readout_weight,
    feedfwd_entry_weight,
    feedfwd_exit_weight,
    pair_projection_matrix,
    pair_output_matrix,
    left_right_maps,
    outer_product_output_matrix,
):
    sequence_shard_count = lineup_state.shape[0]
    length_value = lineup_state.shape[1]
    residue_shard_count = pairwise.shape[0]
    alignment_heads_sharded = coupling_offset_weight_map.shape[1]
    pairwise_heads_sharded = triangle_bias_matrix.shape[1]
    inv_scale = 1.0 / math.sqrt(PER_FOCUS_DIM)
    row_place = lax.axis_index(("rows", "branch"))
    head_location = lax.axis_index("head")
    seq_start = row_place * sequence_shard_count
    row_start = row_place * residue_shard_count
    mask_full = span_mask(aligned_residue_bounds, length_value)
    mask_own = lax.dynamic_slice_in_dim(mask_full, seq_start, sequence_shard_count, 0)
    key_valid = residue_valid_mask > 0
    alignment_normed = layer_normalize(lineup_state).astype(jnp.bfloat16)
    pair_normed = layer_normalize(pairwise).astype(jnp.bfloat16)
    bias_matrix = jnp.concatenate([coupling_offset_weight_map, triangle_bias_matrix], axis=1)
    bias_local = jnp.einsum(
        "tue,el->ltu", pair_normed, bias_matrix, preferred_element_type=jnp.float32
    ).astype(jnp.bfloat16)
    lineup_mapped = jnp.einsum(
        "tvf,xfp->xtvp",
        alignment_normed,
        alignment_projection_matrix,
        preferred_element_type=jnp.float32,
    )
    lineup_probe_lookup_content = (
        lineup_mapped[:3]
        .astype(jnp.bfloat16)
        .reshape(3, sequence_shard_count, length_value, alignment_heads_sharded, PER_FOCUS_DIM)
    )
    alignment_gate = jax.nn.sigmoid(lineup_mapped[3])
    pair_proj = jnp.einsum(
        "ijc,gcd->gijd", pair_normed, pair_projection_matrix, preferred_element_type=jnp.float32
    )
    pair_qkv = (
        pair_proj[:3]
        .astype(jnp.bfloat16)
        .reshape(3, residue_shard_count, length_value, pairwise_heads_sharded, PER_FOCUS_DIM)
    )
    pair_gate = jax.nn.sigmoid(pair_proj[3])
    bias_portion = lax.all_gather(bias_local, ("rows", "branch"), axis=1, tiled=True)
    row_total_count = bias_portion.shape[1]
    alignment_query = lineup_probe_lookup_content[0]
    attention_scores = (
        jnp.einsum(
            "xtza,xfza->xztf",
            alignment_query,
            lineup_probe_lookup_content[1],
            preferred_element_type=jnp.float32,
        )
        * inv_scale
    )
    attention_scores = (
        attention_scores + bias_portion[:alignment_heads_sharded].astype(jnp.float32)[None]
    )
    attention_scores = jnp.where(mask_own[:, None, None, :] > 0, attention_scores, -1000000000.0)
    softmax_shares = soft_weights(attention_scores)
    alignment_portion = jnp.einsum(
        "fxkc,fcxz->fkxz",
        softmax_shares,
        lineup_probe_lookup_content[2],
        preferred_element_type=jnp.float32,
    )
    alignment_portion = alignment_portion.reshape(
        sequence_shard_count, row_total_count, alignment_heads_sharded * PER_FOCUS_DIM
    )
    alignment_portion = (alignment_portion * alignment_gate).astype(jnp.bfloat16)
    pair_query = pair_qkv[0]
    triangle_scores = (
        jnp.einsum("ijhd,ikhd->ihjk", pair_query, pair_qkv[1], preferred_element_type=jnp.float32)
        * inv_scale
    )
    triangle_scores = (
        triangle_scores + bias_portion[alignment_heads_sharded:].astype(jnp.float32)[None]
    )
    triangle_scores = jnp.where(key_valid[None, None, None, :], triangle_scores, -1000000000.0)
    tri_weights = soft_weights(triangle_scores)
    pair_part = jnp.einsum(
        "ihjk,ikhd->ijhd", tri_weights, pair_qkv[2], preferred_element_type=jnp.float32
    )
    pair_part = pair_part.reshape(
        residue_shard_count, row_total_count, pairwise_heads_sharded * PER_FOCUS_DIM
    )
    pair_part = (pair_part * pair_gate).astype(jnp.bfloat16)
    alignment_flattened = jnp.transpose(alignment_portion, (1, 0, 2)).reshape(
        row_total_count, sequence_shard_count * alignment_heads_sharded * PER_FOCUS_DIM
    )
    pair_flattened = jnp.transpose(pair_part, (1, 0, 2)).reshape(
        row_total_count, residue_shard_count * pairwise_heads_sharded * PER_FOCUS_DIM
    )
    attention_result = jnp.concatenate([alignment_flattened, pair_flattened], axis=1)
    alignment_width = sequence_shard_count * alignment_heads_sharded * PER_FOCUS_DIM
    alignment_local = jnp.transpose(
        attention_result[:, :alignment_width].reshape(
            length_value, sequence_shard_count, alignment_heads_sharded * PER_FOCUS_DIM
        ),
        (1, 0, 2),
    )
    pair_local = jnp.transpose(
        attention_result[:, alignment_width:].reshape(
            length_value, residue_shard_count, pairwise_heads_sharded * PER_FOCUS_DIM
        ),
        (1, 0, 2),
    )
    lineup_focus_split, pairwise_heads = (
        lax.all_gather(alignment_local, "head", axis=2, tiled=True),
        lax.all_gather(pair_local, "head", axis=2, tiled=True),
    )
    outer_factors = jnp.einsum(
        "juf,bfn->bjun", alignment_normed, left_right_maps, preferred_element_type=jnp.float32
    )
    outer_factors = (outer_factors * mask_own[None, :, :, None]).astype(jnp.bfloat16)
    factor_rows = lax.all_to_all(
        outer_factors[0], ("rows", "branch"), split_axis=1, concat_axis=0, tiled=True
    )
    col_factors = lax.all_gather(outer_factors[1], ("rows", "branch"), axis=0, tiled=True)
    mask_rows = lax.dynamic_slice_in_dim(mask_full, row_start, residue_shard_count, 1)
    pair_count = jnp.dot(mask_rows.T, mask_full, precision=lax.Precision.HIGHEST)
    col_block = math.gcd(length_value, 128)

    def outer_block(col_start):
        block_cols = lax.dynamic_slice_in_dim(col_factors, col_start, col_block, 1)
        outer_sum = lax.dot_general(
            factor_rows, block_cols, (((0,), (0,)), ((), ())), preferred_element_type=jnp.float32
        )
        counts = lax.dynamic_slice_in_dim(pair_count, col_start, col_block, 1)
        outer_mean = (outer_sum / counts[:, None, :, None]).astype(jnp.bfloat16)
        outer_mean = jnp.transpose(outer_mean, (0, 2, 1, 3)).reshape(
            residue_shard_count * col_block, -1
        )
        return jnp.dot(
            outer_mean, outer_product_output_matrix, preferred_element_type=jnp.float32
        ).reshape(residue_shard_count, col_block, -1)

    starts = jnp.arange(length_value // col_block, dtype=jnp.int32) * col_block
    opm_blocks = lax.map(outer_block, starts)
    opm_update = jnp.transpose(opm_blocks, (1, 0, 2, 3)).reshape(
        residue_shard_count, length_value, -1
    )
    width_z = pair_output_matrix.shape[1]
    tri_update = jnp.dot(
        pairwise_heads.reshape(residue_shard_count * length_value, -1),
        pair_output_matrix,
        preferred_element_type=jnp.float32,
    ).reshape(residue_shard_count, length_value, width_z)
    pair_own = lax.dynamic_slice_in_dim(pairwise, head_location * width_z, width_z, 2).astype(
        jnp.float32
    )
    pairwise_out = (pair_own + tri_update + opm_update).astype(jnp.bfloat16)
    channels = lineup_state.shape[2]
    lineup_blended = lineup_state.astype(jnp.float32) + jnp.dot(
        lineup_focus_split.reshape(sequence_shard_count * length_value, -1),
        lineup_readout_weight,
        preferred_element_type=jnp.float32,
    ).reshape(sequence_shard_count, length_value, channels)
    feedfwd_standardized = layer_normalize(lineup_blended).astype(jnp.bfloat16)
    head_count = lax.axis_size("head")
    hidden = jax.nn.relu(
        jnp.einsum(
            "src,cf->srf",
            feedfwd_standardized,
            feedfwd_entry_weight,
            preferred_element_type=jnp.float32,
        )
    ).astype(jnp.bfloat16)
    partial_value = jnp.einsum(
        "srf,fc->src", hidden, feedfwd_exit_weight, preferred_element_type=jnp.float32
    )
    summed_result = lax.psum_scatter(
        partial_value.astype(jnp.bfloat16), "head", scatter_dimension=2, tiled=True
    ).astype(jnp.float32)
    alignment_channel_width = channels // head_count
    alignment_owned = lax.dynamic_slice_in_dim(
        lineup_blended, head_location * alignment_channel_width, alignment_channel_width, 2
    )
    refreshed_lineup_state = (alignment_owned + summed_result).astype(jnp.bfloat16)
    return (refreshed_lineup_state, pairwise_out)


def solution(mesh):
    in_specs = (
        P(("parts", "rows", "branch"), None, None),
        P(("parts", "rows", "branch"), None, None),
        P("parts", None),
        P("parts"),
        P(None, "head"),
        P(None, "head"),
        P(None, None, "head"),
        P(),
        P(None, "head"),
        P("head", None),
        P(None, None, "head"),
        P(None, "head"),
        P(),
        P(None, "head"),
    )
    out_specs = (
        P(("parts", "rows", "branch"), None, "head"),
        P(("parts", "rows", "branch"), None, "head"),
    )
    return jax.shard_map(local, mesh=mesh, in_specs=in_specs, out_specs=out_specs, check_vma=False)
```

profile of v0, /device:TPU:0, one launch (start us, length us, event | category | flops | bytes accessed | tf_op | source)
XLA Modules:
  0.0 93.5 jit_solution(9554350493809274063)
XLA Ops:
  7.2 0.0 copy-start
  7.2 0.0 copy-start.2
  7.2 1.1 %convert_reduce_fusion.1 = f32[2,128]{1,0:T(2,128)S(1)} fusion(bf16[2,128,256]{2,1,0:T(8,128)(2,1)} %param.14), kind=kLoop, calls=%fused_computation.38 | loop fusion | flops 130816 | bytes 132096 | tf_op jit(solution)/shard_map/reduce_sum | solution.py:13
  8.3 1.1 %fusion.24 = f32[2,128]{1,0:T(2,128)S(1)} fusion(bf16[2,128,256]{2,1,0:T(8,128)(2,1)} %param.14, f32[2,128]{1,0:T(2,128)S(1)} %broadcast_multiply_fusion.2), kind=kLoop, calls=%fused_computation.41 | loop fusion | flops 261888 | bytes 133120 | tf_op jit(solution)/shard_map/reduce_sum | solution.py:14
  9.4 0.8 slice_bitcast_fusion.2
  10.1 0.1 fusion.62
  10.2 1.2 %fusion.16 = bf16[2,2,128,32]{2,3,0,1:T(8,128)(2,1)S(1)} fusion(bf16[2,128,256]{2,1,0:T(8,128)(2,1)} %param.14, f32[2,128]{1,0:T(2,128)S(1)} %add_rsqrt_fusion.2, f32[2,128]{1,0:T(2,128)S(1)} %broadcast_multiply_fusion.2, bf16[2,256,32]{1,2,0:T(8,128)(2,1)} %param.26, f32[2,128]{1,0:T(2,128)S(1)} %get-tuple-element.28), kind=kOutput, calls=%fused_computation.26 | convolution fusion | flops 8683520 | bytes 199680 | tf_op jit(solution)/shard_map/juf,bfn->bjun/dot_general | solution.py:156
  11.4 0.1 copy.46
  11.6 0.7 reshape.117
  12.3 7.4 %all-to-all-start = ((bf16[16,2,256]{2,1,0:T(2,128)(2,1)}), bf16[16,2,256]{2,1,0:T(2,128)(2,1)S(1)}, u32[]{:S(2)}, u32[]{:S(2)}) async-start(bf16[16,2,256]{2,1,0:T(2,128)(2,1)} %reshape.117), calls=%async_computation | async-start | bytes 32768 | tf_op jit(solution)/shard_map/all_to_all | solution.py:160
  19.7 0.0 reduce-scatter.4.cloned.1.call-start
  19.7 1.1 %convert_reduce_fusion = f32[8,128]{1,0:T(8,128)S(1)} fusion(bf16[8,128,128]{2,1,0:T(8,128)(2,1)} %param.15), kind=kLoop, calls=%fused_computation.30 | loop fusion | flops 261120 | bytes 266240 | tf_op jit(solution)/shard_map/reduce_sum | solution.py:13
  20.9 1.3 %fusion.19 = f32[8,128]{1,0:T(8,128)S(1)} fusion(bf16[8,128,128]{2,1,0:T(8,128)(2,1)} %param.15, f32[8,128]{1,0:T(8,128)S(1)} %broadcast_multiply_fusion), kind=kLoop, calls=%fused_computation.33 | loop fusion | flops 523264 | bytes 270336 | tf_op jit(solution)/shard_map/reduce_sum | solution.py:14
  22.2 1.4 %convolution_convert_fusion = bf16[6,8,128]{2,0,1:T(8,128)(2,1)S(1)} fusion(bf16[8,128,128]{2,1,0:T(8,128)(2,1)} %param.15, f32[8,128]{1,0:T(8,128)S(1)} %add_rsqrt_fusion, f32[8,128]{1,0:T(8,128)S(1)} %broadcast_multiply_fusion, bf16[128,2]{0,1:T(2,128)(2,1)} %param.19, bf16[128,4]{0,1:T(4,128)(2,1)} %param.18), kind=kOutput, calls=%fused_computation.27 | convolution fusion | flops 2106368 | bytes 284160 | tf_op jit(solution)/shard_map/tue,el->ltu/dot_general | solution.py:64
  23.6 22.2 %all_gather.12 = bf16[6,128,128]{2,1,0:T(8,128)(2,1)S(1)} all-gather(bf16[6,8,128]{2,1,0:T(8,128)(2,1)S(1)} %copy.39), channel_id=1, replica_groups=mesh['parts'=1,'rows'=8,'branch'=2,'head'=2] {'rows','branch'}, dimensions={1}, use_global_device_ids=true | all-gather | bytes 208896 | tf_op jit(solution)/shard_map/all_gather | solution.py:88
  45.9 0.1 copy.40
  46.0 0.0 copy-done
  46.1 0.0 copy-done.2
  46.1 0.4 fusion.78
  46.5 0.4 fusion.79
  46.8 0.0 copy-start.3
  46.9 0.0 copy-start.7
  46.9 0.0 copy-start.8
  46.9 0.3 fusion.10
  47.2 0.2 fusion.40
  47.4 0.0 copy-start.9
  47.4 0.0 copy-start.5
  47.5 5.1 %all_gather.13 = bf16[2,128,256]{1,2,0:T(8,128)(2,1)S(1)} all-gather(bf16[2,128,128]{1,2,0:T(8,128)(2,1)S(1)} %fusion.55), channel_id=1, replica_groups=mesh['parts'=1,'rows'=8,'branch'=2,'head'=2] {'head'}, dimensions={2}, use_global_device_ids=true | all-gather | bytes 196608 | tf_op jit(solution)/shard_map/all_gather | solution.py:153
  52.6 0.0 copy-done.3
  52.6 0.3 fusion.80
  53.0 0.2 multiply_reduce_fusion
  53.1 0.0 copy-done.7
  53.2 0.0 copy-done.8
  53.2 0.4 fusion.14
  53.6 0.1 copy.64
  53.7 0.7 copy.76
  54.4 0.0 reduce-scatter.4.cloned.1.call-update
  54.4 0.0 copy-done.9
  54.5 0.1 copy.44
  54.6 0.0 copy-done.1
  54.6 0.0 copy-done.5
  54.6 0.9 fusion.81
  55.5 0.6 fusion.82
  56.1 0.4 fusion.6
  56.4 0.3 fusion.63
  56.7 0.1 constant_dynamic-slice_fusion
  56.9 0.1 copy.66
  57.0 0.0 copy-start.6
  57.0 0.3 fusion.21
  57.4 0.1 fusion.39
  57.4 6.6 %all_gather.14 = bf16[8,128,128]{1,2,0:T(8,128)(2,1)S(1)} all-gather(bf16[8,128,64]{1,2,0:T(8,128)(2,1)S(1)} %fusion.39), channel_id=1, replica_groups=mesh['parts'=1,'rows'=8,'branch'=2,'head'=2] {'head'}, dimensions={2}, use_global_device_ids=true | all-gather | bytes 393216 | tf_op jit(solution)/shard_map/all_gather | solution.py:154
  64.0 0.0 copy-done.6
  64.0 0.2 convolution_add_fusion.1
  64.2 17.8 %all-gather = bf16[1,32,128,32]{2,3,0,1:T(8,128)(2,1)S(1)} all-gather(bf16[1,2,128,32]{2,3,0,1:T(8,128)(2,1)S(1)} %get-tuple-element.27), channel_id=2, replica_groups=mesh['parts'=1,'rows'=8,'branch'=2,'head'=2] {'rows','branch'}, dimensions={1}, use_global_device_ids=true | all-gather | bytes 278528 | tf_op jit(solution)/shard_map/all_gather | solution.py:163
  82.1 0.0 all-to-all-done
  82.1 0.1 reshape.118
  82.2 0.7 fusion.2
  82.9 0.0 copy-start.4
  83.0 0.8 copy.51
  83.8 0.1 copy-done.4
  83.9 1.1 %fusion.13 = bf16[8,128,64]{1,2,0:T(8,128)(2,1)} fusion(f32[8,128,64]{1,2,0:T(8,128)S(1)} %convolution_add_fusion.1, bf16[8,128,1024]{1,2,0:T(8,128)(2,1)S(1)} %bitcast.130, bf16[1024,64]{0,1:T(8,128)(2,1)S(1)} %copy-done.4), kind=kOutput, calls=%fused_computation.22 | convolution fusion | flops 134348800 | bytes 2621440 | tf_op jit(solution)/shard_map/while/body/eval_jaxpr/dot_general | solution.py:178
  85.0 0.9 reshape.116
  85.9 0.1 copy.65
  86.0 0.7 add_convert_fusion
  (19 shorter events, 0.2 us)
Async XLA Ops:
  7.2 38.9 %copy-start = (bf16[4,256,128]{2,1,0:T(8,128)(2,1)S(1)}, bf16[4,256,128]{2,1,0:T(8,128)(2,1)}, u32[]{:S(2)}) copy-start(bf16[4,256,128]{2,1,0:T(8,128)(2,1)} %param.20) | copy-start | bytes 786436
  7.2 38.9 %copy-start.2 = (bf16[2,128,256]{2,1,0:T(8,128)(2,1)S(1)}, bf16[2,128,256]{2,1,0:T(8,128)(2,1)}, u32[]{:S(2)}) copy-start(bf16[2,128,256]{2,1,0:T(8,128)(2,1)} %param.14) | copy-start | bytes 393220
  12.3 69.8 %all-to-all-start = ((bf16[16,2,256]{2,1,0:T(2,128)(2,1)}), bf16[16,2,256]{2,1,0:T(2,128)(2,1)S(1)}, u32[]{:S(2)}, u32[]{:S(2)}) async-start(bf16[16,2,256]{2,1,0:T(2,128)(2,1)} %reshape.117), calls=%async_computation | async-start | bytes 32768 | tf_op jit(solution)/shard_map/all_to_all | solution.py:160
  19.7 65.3 %reduce-scatter.4.cloned.1.call-start = ((), (), s32[]{:S(2)}) async-start(), calls=%async_computation.2 | async-start | bytes 196608
  46.8 5.8 %copy-start.3 = (bf16[256,256]{1,0:T(8,128)(2,1)S(1)}, bf16[256,256]{1,0:T(8,128)(2,1)}, u32[]{:S(2)}) copy-start(bf16[256,256]{1,0:T(8,128)(2,1)} %param.21) | copy-start | bytes 393220
  46.9 6.3 %copy-start.7 = (bf16[512,256]{1,0:T(8,128)(2,1)S(1)}, bf16[512,256]{1,0:T(8,128)(2,1)}, u32[]{:S(2)}) copy-start(bf16[512,256]{1,0:T(8,128)(2,1)} %param.23) | copy-start | bytes 786436
  46.9 6.3 %copy-start.8 = (bf16[256,512]{1,0:T(8,128)(2,1)S(1)}, bf16[256,512]{1,0:T(8,128)(2,1)}, u32[]{:S(2)}) copy-start(bf16[256,512]{1,0:T(8,128)(2,1)} %param.22) | copy-start | bytes 786436
  47.4 7.0 %copy-start.9 = (s32[128]{0:T(128)S(1)}, s32[128]{0:T(128)}, u32[]{:S(2)}) copy-start(s32[128]{0:T(128)} %param.17) | copy-start | bytes 1540
  47.4 7.2 %copy-start.1 = (bf16[8,128,128]{2,1,0:T(8,128)(2,1)S(1)}, bf16[8,128,128]{2,1,0:T(8,128)(2,1)}, u32[]{:S(2)}) copy-start(bf16[8,128,128]{2,1,0:T(8,128)(2,1)} %param.15) | copy-start | bytes 786436
  47.4 7.2 %copy-start.5 = (bf16[4,128,64]{1,2,0:T(8,128)(2,1)S(1)}, bf16[4,128,64]{1,2,0:T(8,128)(2,1)}, u32[]{:S(2)}) copy-start(bf16[4,128,64]{1,2,0:T(8,128)(2,1)} %param.24) | copy-start | bytes 196612
  57.0 7.0 %copy-start.6 = (bf16[128,64]{0,1:T(8,128)(2,1)S(1)}, bf16[128,64]{0,1:T(8,128)(2,1)}, u32[]{:S(2)}) copy-start(bf16[128,64]{0,1:T(8,128)(2,1)} %param.25) | copy-start | bytes 49156
  82.9 0.9 copy-start.4
Sparse Core Ops, SparseCore 0:
  54.5 8.4 reduce-scatter.3
where the time goes:
time: 93.9 us; the launch traced here: 93.5 us
  blocking collectives  51.8 us (55%)
  between operations  14.4 us (15%)
  matrix products  9.08 us (10%)
  starting transfers between devices  7.45 us (8%)
  other arithmetic  5.69 us (6%)
  local copies, waits for them, and re-layouts  4.99 us (5%)
    all_gather x1, blocking collectives, local(): lax.all_gather(bias_local, ('rows', 'branch'), axis=1, tiled=True)  22.2 us
    all_gather x1, blocking collectives, local(): lax.all_gather(outer_factors[1], ('rows', 'branch'), axis=0, tiled=True)  17.8 us
    all_to_all x1, starting transfers between devices, local(): lax.all_to_all(outer_factors[0], ('rows', 'branch'), split_axis=1, concat...  7.41 us
    all_gather x1, blocking collectives, local(): lax.all_gather(pair_local, 'head', axis=2, tiled=True)  6.59 us
    all_gather x1, blocking collectives, local(): lax.all_gather(alignment_local, 'head', axis=2, tiled=True)  5.14 us
    unnamed x27, local copies, waits for them, and re-layouts  2.84 us
    reduce_sum x3, other arithmetic, layer_normalize(): spread = jnp.mean(center * center, -1, keepdims=True)  2.59 us
    reduce_sum x2, other arithmetic, layer_normalize(): center = values - jnp.mean(values, -1, keepdims=True)  2.16 us
  transfers between devices with their start and end apart: 2, of which 0 were waited for; matrix products, arithmetic and copies ran while one was open for 14% of the time, Pallas kernels for 0%

commit v1 on v0

v1 whole, which is shorter than its diff:
```python
import math

import jax
import jax.numpy as jnp
from jax import lax
from jax.sharding import PartitionSpec as P

PER_FOCUS_DIM = 32


def layer_normalize(values):
    values = values.astype(jnp.float32)
    center = values - jnp.mean(values, -1, keepdims=True)
    spread = jnp.mean(center * center, -1, keepdims=True)
    return center * lax.rsqrt(spread + 1e-05)


def soft_weights(attention_scores):
    row_max = jnp.max(attention_scores, -1, keepdims=True)
    shifted = jnp.exp(attention_scores - row_max)
    return (shifted / jnp.sum(shifted, -1, keepdims=True)).astype(jnp.bfloat16)


def span_mask(aligned_residue_bounds, length_value):
    places = jnp.arange(length_value, dtype=jnp.int32)
    inside = (places[None, :] >= aligned_residue_bounds[:, 0:1]) & (
        places[None, :] < aligned_residue_bounds[:, 1:2]
    )
    return inside.astype(jnp.float32)


def gather_head(value, axis):
    if lax.axis_size("head") != 2:
        return lax.all_gather(value, "head", axis=axis, tiled=True)
    other = lax.ppermute(value, "head", [(0, 1), (1, 0)])
    first = lax.axis_index("head") == 0
    return jnp.concatenate(
        [jnp.where(first, value, other), jnp.where(first, other, value)], axis=axis
    )


def sum_to_owner(partial_value):
    count = lax.axis_size("head")
    width = partial_value.shape[-1] // count
    if count != 2:
        return lax.psum_scatter(
            partial_value.astype(jnp.bfloat16),
            "head",
            scatter_dimension=partial_value.ndim - 1,
            tiled=True,
        ).astype(jnp.float32)
    first = lax.axis_index("head") == 0
    low, high = partial_value[..., :width], partial_value[..., width:]
    sent = jnp.where(first, high, low).astype(jnp.bfloat16)
    got = lax.ppermute(sent, "head", [(0, 1), (1, 0)])
    return jnp.where(first, low, high) + got.astype(jnp.float32)


def local(
    lineup_state,
    pairwise,
    aligned_residue_bounds,
    residue_valid_mask,
    coupling_offset_weight_map,
    triangle_bias_matrix,
    alignment_projection_matrix,
    lineup_readout_weight,
    feedfwd_entry_weight,
    feedfwd_exit_weight,
    pair_projection_matrix,
    pair_output_matrix,
    left_right_maps,
    outer_product_output_matrix,
):
    seqs, length, channels = lineup_state.shape
    rows = pairwise.shape[0]
    heads = coupling_offset_weight_map.shape[1]
    pair_heads = triangle_bias_matrix.shape[1]
    depth = left_right_maps.shape[2]
    chips = lax.axis_size("rows")
    cores = lax.axis_size("branch")
    inv_scale = 1.0 / math.sqrt(PER_FOCUS_DIM)
    row_place = lax.axis_index(("rows", "branch"))
    head_location = lax.axis_index("head")
    mask_full = span_mask(aligned_residue_bounds, length)
    mask_own = lax.dynamic_slice_in_dim(mask_full, row_place * seqs, seqs, 0)
    key_valid = residue_valid_mask > 0
    alignment_normed = layer_normalize(lineup_state).astype(jnp.bfloat16)
    pair_normed = layer_normalize(pairwise).astype(jnp.bfloat16)
    bias_matrix = jnp.concatenate([coupling_offset_weight_map, triangle_bias_matrix], axis=1)
    bias_local = jnp.einsum(
        "tue,el->ltu", pair_normed, bias_matrix, preferred_element_type=jnp.float32
    ).astype(jnp.bfloat16)
    factors = jnp.einsum(
        "juf,bfn->bjun", alignment_normed, left_right_maps, preferred_element_type=jnp.float32
    )
    factors = (factors * mask_own[None, :, :, None]).astype(jnp.bfloat16)

    block = cores * rows
    left = jnp.transpose(factors[0].reshape(seqs, chips, block, depth), (1, 0, 2, 3))
    bias_size = bias_local.size
    right_size = seqs * length * depth
    copied = jnp.concatenate([bias_local.reshape(-1), factors[1].reshape(-1)])
    payload = jnp.concatenate(
        [
            jnp.broadcast_to(copied[None], (chips, bias_size + right_size)),
            left.reshape(chips, -1),
        ],
        axis=1,
    )
    payload = payload.reshape(chips, -1, 128)
    got = lax.all_to_all(payload, "rows", 0, 0, tiled=True)
    got = lax.all_gather(got, "branch", axis=1)
    got = got.reshape(chips, cores, -1)
    bias = jnp.transpose(
        got[:, :, :bias_size].reshape(chips, cores, heads + pair_heads, rows, length),
        (2, 0, 1, 3, 4),
    ).reshape(heads + pair_heads, length, length)
    right_all = got[:, :, bias_size : bias_size + right_size].reshape(-1, length, depth)
    left_all = got[:, :, bias_size + right_size :].reshape(-1, cores, rows, depth)
    left_own = lax.dynamic_index_in_dim(left_all, lax.axis_index("branch"), 1, keepdims=False)

    lineup_mapped = jnp.einsum(
        "tvf,xfp->xtvp",
        alignment_normed,
        alignment_projection_matrix,
        preferred_element_type=jnp.float32,
    )
    qkv = lineup_mapped[:3].astype(jnp.bfloat16).reshape(3, seqs, length, heads, PER_FOCUS_DIM)
    alignment_gate = jax.nn.sigmoid(lineup_mapped[3])
    pair_proj = jnp.einsum(
        "ijc,gcd->gijd", pair_normed, pair_projection_matrix, preferred_element_type=jnp.float32
    )
    pair_qkv = pair_proj[:3].astype(jnp.bfloat16)
    pair_qkv = pair_qkv.reshape(3, rows, length, pair_heads, PER_FOCUS_DIM)
    pair_gate = jax.nn.sigmoid(pair_proj[3])

    scores = inv_scale * jnp.einsum(
        "xtza,xfza->xztf", qkv[0], qkv[1], preferred_element_type=jnp.float32
    )
    scores = scores + bias[:heads].astype(jnp.float32)[None]
    scores = jnp.where(mask_own[:, None, None, :] > 0, scores, -1000000000.0)
    mixed = jnp.einsum(
        "fxkc,fcxz->fkxz", soft_weights(scores), qkv[2], preferred_element_type=jnp.float32
    ).reshape(seqs, length, heads * PER_FOCUS_DIM)
    mixed = gather_head((mixed * alignment_gate).astype(jnp.bfloat16), 2)

    tri_scores = inv_scale * jnp.einsum(
        "ijhd,ikhd->ihjk", pair_qkv[0], pair_qkv[1], preferred_element_type=jnp.float32
    )
    tri_scores = tri_scores + bias[heads:].astype(jnp.float32)[None]
    tri_scores = jnp.where(key_valid[None, None, None, :], tri_scores, -1000000000.0)
    pair_mixed = jnp.einsum(
        "ihjk,ikhd->ijhd",
        soft_weights(tri_scores),
        pair_qkv[2],
        preferred_element_type=jnp.float32,
    ).reshape(rows, length, pair_heads * PER_FOCUS_DIM)
    pair_mixed = gather_head((pair_mixed * pair_gate).astype(jnp.bfloat16), 2)

    blended = lineup_state.astype(jnp.float32) + jnp.dot(
        mixed.reshape(seqs * length, -1),
        lineup_readout_weight,
        preferred_element_type=jnp.float32,
    ).reshape(seqs, length, channels)
    standardized = layer_normalize(blended).astype(jnp.bfloat16)
    hidden = jax.nn.relu(
        jnp.einsum(
            "src,cf->srf", standardized, feedfwd_entry_weight, preferred_element_type=jnp.float32
        )
    ).astype(jnp.bfloat16)
    partial_value = jnp.einsum(
        "srf,fc->src", hidden, feedfwd_exit_weight, preferred_element_type=jnp.float32
    )
    summed = sum_to_owner(partial_value)
    own_width = channels // lax.axis_size("head")
    owned = lax.dynamic_slice_in_dim(blended, head_location * own_width, own_width, 2)
    refreshed = (owned + summed).astype(jnp.bfloat16)

    mask_rows = lax.dynamic_slice_in_dim(mask_full, row_place * rows, rows, 1)
    pair_count = jnp.dot(mask_rows.T, mask_full, precision=lax.Precision.HIGHEST)
    col_block = math.gcd(length, 128)

    def outer_block(col_start):
        cols = lax.dynamic_slice_in_dim(right_all, col_start, col_block, 1)
        outer_sum = lax.dot_general(
            left_own, cols, (((0,), (0,)), ((), ())), preferred_element_type=jnp.float32
        )
        counts = lax.dynamic_slice_in_dim(pair_count, col_start, col_block, 1)
        outer_mean = (outer_sum / counts[:, None, :, None]).astype(jnp.bfloat16)
        outer_mean = jnp.transpose(outer_mean, (0, 2, 1, 3)).reshape(rows * col_block, -1)
        return jnp.dot(
            outer_mean, outer_product_output_matrix, preferred_element_type=jnp.float32
        ).reshape(rows, col_block, -1)

    starts = jnp.arange(length // col_block, dtype=jnp.int32) * col_block
    opm_update = jnp.transpose(lax.map(outer_block, starts), (1, 0, 2, 3))
    opm_update = opm_update.reshape(rows, length, -1)
    width_z = pair_output_matrix.shape[1]
    tri_update = jnp.dot(
        pair_mixed.reshape(rows * length, -1),
        pair_output_matrix,
        preferred_element_type=jnp.float32,
    ).reshape(rows, length, width_z)
    pair_own = lax.dynamic_slice_in_dim(pairwise, head_location * width_z, width_z, 2)
    pairwise_out = (pair_own.astype(jnp.float32) + tri_update + opm_update).astype(jnp.bfloat16)
    return (refreshed, pairwise_out)


def solution(mesh):
    in_specs = (
        P(("parts", "rows", "branch"), None, None),
        P(("parts", "rows", "branch"), None, None),
        P("parts", None),
        P("parts"),
        P(None, "head"),
        P(None, "head"),
        P(None, None, "head"),
        P(),
        P(None, "head"),
        P("head", None),
        P(None, None, "head"),
        P(None, "head"),
        P(),
        P(None, "head"),
    )
    out_specs = (
        P(("parts", "rows", "branch"), None, "head"),
        P(("parts", "rows", "branch"), None, "head"),
    )
    return jax.shard_map(local, mesh=mesh, in_specs=in_specs, out_specs=out_specs, check_vma=False)
```

time: 93.9 us -> 54.2 us (0.58)
  blocking collectives: 51.8 us -> 2.15 us
  between operations: 14.4 us -> 1.14 us
  waiting for transfers between devices: 0.02 us -> 7.23 us
  matrix products: 9.08 us -> 16.1 us
  local copies, waits for them, and re-layouts: 4.99 us -> 10.6 us
  starting transfers between devices: 7.45 us -> 11 us
    all_gather x4 -> x1, blocking collectives: 51.8 us -> 2.15 us  [local(): got = lax.all_gather(got, 'branch', axis=1)]
    dot_general x7, matrix products: 2.46 us -> 7.75 us  [the longest x1 2.03 us: outer_block(): lax.dot_general(left_own, cols, (((0,), (0,)), ((), ())), preferred_eleme...]
    all_to_all x1, waiting for transfers between devices: 0.01 us -> 4.93 us  [local(): got = lax.all_to_all(payload, 'rows', 0, 0, tiled=True)]
    ppermute x0 -> x3, starting transfers between devices: none -> 3.64 us  [the longest x2 2.09 us: gather_head(): other = lax.ppermute(value, 'head', [(0, 1), (1, 0)])]
    ppermute x0 -> x3, waiting for transfers between devices: none -> 2.3 us  [the longest x1 2.29 us: sum_to_owner(): got = lax.ppermute(sent, 'head', [(0, 1), (1, 0)])]
    select_n x0 -> x2, other arithmetic: none -> 1.81 us  [gather_head(): jnp.where(first, value, other)]
    sub x2, matrix products: 0.97 us -> 2.77 us  [soft_weights(): shifted = jnp.exp(attention_scores - row_max)]
    convert_element_type x1, local copies, waits for them, and re-layouts: 0.82 us -> 2.46 us  [outer_block(): outer_mean = (outer_sum / counts[:, None, :, None]).astype(jnp.bfloat16)]
  transfers between devices with their start and end apart: 2 -> 4, of which waited for: 0 -> 2; matrix products, arithmetic and copies ran while one was open for 14% -> 29% of each run, Pallas kernels for 0% -> 0%
where the time goes in v1:
time: 54.2 us; the launch traced here: 53.6 us
  matrix products  16.1 us (30%)
  starting transfers between devices  11 us (20%)
  local copies, waits for them, and re-layouts  10.6 us (20%)
  waiting for transfers between devices  7.23 us (13%)
  other arithmetic  5.38 us (10%)
  blocking collectives  2.15 us (4%)
  between operations  1.14 us (2%)
    all_to_all x1, starting transfers between devices, local(): got = lax.all_to_all(payload, 'rows', 0, 0, tiled=True)  7.31 us
    all_to_all x1, waiting for transfers between devices, local(): got = lax.all_to_all(payload, 'rows', 0, 0, tiled=True)  4.93 us
    unnamed x34, local copies, waits for them, and re-layouts  3.38 us
    sub x2, matrix products, soft_weights(): shifted = jnp.exp(attention_scores - row_max)  2.77 us
    convert_element_type x1, local copies, waits for them, and re-layouts, outer_block(): outer_mean = (outer_sum / counts[:, None, :, None]).astype(jnp.bfloat16)  2.46 us
    ppermute x1, waiting for transfers between devices, sum_to_owner(): got = lax.ppermute(sent, 'head', [(0, 1), (1, 0)])  2.29 us
    all_gather x1, blocking collectives, local(): got = lax.all_gather(got, 'branch', axis=1)  2.15 us
    ppermute x2, starting transfers between devices, gather_head(): other = lax.ppermute(value, 'head', [(0, 1), (1, 0)])  2.09 us
  transfers between devices with their start and end apart: 4, of which 2 were waited for; matrix products, arithmetic and copies ran while one was open for 29% of the time, Pallas kernels for 0%

profile of v1, /device:TPU:0, one launch (start us, length us, event | category | flops | bytes accessed | tf_op | source)
XLA Modules:
  0.0 53.6 jit_solution(10248527513812743221)
XLA Ops:
  0.6 0.0 copy-start
  0.6 1.1 %copy.29 = bf16[2,128,256]{1,2,0:T(8,128)(2,1)S(1)} copy(bf16[2,128,256]{2,1,0:T(8,128)(2,1)} %param.14) | data formatting | bytes 262144 | tf_op args[0]
  1.7 0.1 convert_reduce_fusion.1
  1.8 0.1 fusion.24
  1.8 0.8 %slice_bitcast_fusion.1 = (s32[32]{0:T(128)S(1)}, s32[32]{0:T(128)S(1)}) fusion(s32[32,2]{0,1:T(2,128)} %param.16), kind=kLoop, calls=%fused_computation.114 | loop fusion | bytes 512 | tf_op jit(solution)/shard_map/ge | solution.py:26
  2.6 0.1 fusion.68
  2.7 0.9 %fusion.16 = bf16[2,2,128,32]{2,3,0,1:T(8,128)(2,1)S(1)} fusion(bf16[2,128,256]{1,2,0:T(8,128)(2,1)S(1)} %copy.29, f32[2,128]{1,0:T(2,128)S(1)} %add_rsqrt_fusion.2, f32[2,128]{1,0:T(2,128)S(1)} %broadcast_multiply_fusion.2, bf16[2,256,32]{1,2,0:T(8,128)(2,1)} %param.26, f32[2,128]{1,0:T(2,128)S(1)} %get-tuple-element.37), kind=kOutput, calls=%fused_computation.25 | convolution fusion | flops 8683520 | bytes 199680 | tf_op jit(solution)/shard_map/juf,bfn->bjun/dot_general | solution.py:94
  3.6 0.1 copy.35
  3.8 0.0 copy-start.1
  3.8 0.0 copy-start.12
  3.8 0.1 reshape.137
  3.9 0.1 copy.34
  4.1 0.1 reshape_squeeze.6
  4.2 1.1 %convert_reduce_fusion = f32[8,128]{1,0:T(8,128)S(1)} fusion(bf16[8,128,128]{2,1,0:T(8,128)(2,1)} %param.15), kind=kLoop, calls=%fused_computation.29 | loop fusion | flops 261120 | bytes 266240 | tf_op jit(solution)/shard_map/reduce_sum | solution.py:13
  5.3 1.3 %fusion.19 = f32[8,128]{1,0:T(8,128)S(1)} fusion(bf16[8,128,128]{2,1,0:T(8,128)(2,1)} %param.15, f32[8,128]{1,0:T(8,128)S(1)} %broadcast_multiply_fusion), kind=kLoop, calls=%fused_computation.32 | loop fusion | flops 523264 | bytes 270336 | tf_op jit(solution)/shard_map/reduce_sum | solution.py:14
  6.6 1.4 %convolution_convert_fusion = bf16[6,8,128]{2,0,1:T(8,128)(2,1)S(1)} fusion(bf16[8,128,128]{2,1,0:T(8,128)(2,1)} %param.15, f32[8,128]{1,0:T(8,128)S(1)} %add_rsqrt_fusion, f32[8,128]{1,0:T(8,128)S(1)} %broadcast_multiply_fusion, bf16[128,2]{0,1:T(2,128)(2,1)} %param.19, bf16[128,4]{0,1:T(4,128)(2,1)} %param.18), kind=kOutput, calls=%fused_computation.26 | convolution fusion | flops 2106368 | bytes 284160 | tf_op jit(solution)/shard_map/tue,el->ltu/dot_general | solution.py:91
  8.1 0.7 %copy.78 = bf16[1,8,120,128]{3,2,1,0:T(8,128)(2,1)} copy(bf16[1,8,120,128]{3,1,2,0:T(8,128)(2,1)S(1)} %maximum_bitcast_fusion) | data formatting | bytes 491520
  8.8 7.3 %all-to-all-start = ((bf16[8,120,128]{2,1,0:T(8,128)(2,1)}), bf16[8,120,128]{2,1,0:T(8,128)(2,1)S(1)}, u32[]{:S(2)}, u32[]{:S(2)}) async-start(bf16[8,120,128]{2,1,0:T(8,128)(2,1)} %bitcast.133), calls=%async_computation | async-start | bytes 491520 | tf_op jit(solution)/shard_map/all_to_all | solution.py:112
  16.1 0.0 copy-start.14
  16.2 0.3 fusion.87
  16.4 0.7 %fusion.85 = (bf16[1,2,128,128]{2,3,0,1:T(8,128)(2,1)}, bf16[1,2,128,128]{2,3,0,1:T(8,128)(2,1)}, bf16[1,2,128,128]{2,3,0,1:T(8,128)(2,1)}) fusion(bf16[4,2,128,128]{2,3,0,1:T(8,128)(2,1)S(1)} %get-tuple-element.40), kind=kLoop, calls=%fused_computation.127 | loop fusion | bytes 393216 | tf_op jit(solution)/shard_map/slice | solution.py:139
  17.1 0.3 fusion.69
  17.4 0.8 %fusion.90 = (bf16[4,8,128,64]{2,3,0,1:T(8,128)(2,1)S(1)}, f32[4,8,128,64]{2,3,0,1:T(8,128)S(1)}) fusion(bf16[4,128,64]{1,2,0:T(8,128)(2,1)S(1)} %copy-done.12, f32[8,128]{1,0:T(8,128)S(1)} %add_rsqrt_fusion, f32[8,128]{1,0:T(8,128)S(1)} %broadcast_multiply_fusion, bf16[8,128,128]{2,1,0:T(8,128)(2,1)S(1)} %copy-done.1), kind=kOutput, calls=%fused_computation.132 | convolution fusion | flops 67895296 | bytes 1908736 | tf_op jit(solution)/shard_map/ijc,gcd->gijd/dot_general | solution.py:131
  18.2 0.1 constant_dynamic-slice_fusion.1
  18.4 0.8 %copy.73 = bf16[8,128,64]{1,2,0:T(8,128)(2,1)} copy(bf16[8,128,64]{2,1,0:T(8,128)(2,1)S(1)} %constant_dynamic-slice_fusion.1) | data formatting | bytes 262144
  19.1 0.7 %fusion.84 = (bf16[1,8,128,64]{2,3,0,1:T(8,128)(2,1)}, bf16[1,8,128,64]{2,3,0,1:T(8,128)(2,1)}, bf16[1,8,128,64]{2,3,0,1:T(8,128)(2,1)}) fusion(bf16[4,8,128,64]{2,3,0,1:T(8,128)(2,1)S(1)} %get-tuple-element.44), kind=kLoop, calls=%fused_computation.126 | loop fusion | bytes 786432 | tf_op jit(solution)/shard_map/slice | solution.py:149
  19.9 4.9 %all-to-all-done = bf16[8,120,128]{2,1,0:T(8,128)(2,1)S(1)} async-done(((bf16[8,120,128]{2,1,0:T(8,128)(2,1)}), bf16[8,120,128]{2,1,0:T(8,128)(2,1)S(1)}, u32[]{:S(2)}, u32[]{:S(2)}) %all-to-all-start) | async-done | bytes 245792 | tf_op jit(solution)/shard_map/all_to_all | solution.py:112
  24.8 2.1 %all-gather = bf16[8,240,128]{2,1,0:T(8,128)(2,1)S(1)} all-gather(bf16[8,120,128]{2,1,0:T(8,128)(2,1)S(1)} %all-to-all-done), channel_id=2, replica_groups=mesh['parts'=1,'rows'=8,'branch'=2,'head'=2] {'branch'}, dimensions={1}, use_global_device_ids=true | all-gather | bytes 737280 | tf_op jit(solution)/shard_map/all_gather | solution.py:113
  27.0 0.1 reshape.139
  27.1 0.1 slice.99
  27.2 0.1 reshape.163
  27.5 0.1 copy.39
  27.6 1.2 %fusion.88 = f32[2,4,128]{2,1,0:T(4,128)S(1)} fusion(bf16[2,128,4,32]{1,3,2,0:T(8,128)(2,1)} %bitcast.148, bf16[2,128,4,32]{1,3,2,0:T(8,128)(2,1)S(1)} %bitcast.146, f32[4,128,128]{1,2,0:T(8,128)S(1)} %copy.39, pred[2,128]{1,0:T(4,128)(4,1)S(1)} %get-tuple-element.36), kind=kOutput, calls=%fused_computation.130 | convolution fusion | flops 9044095 | bytes 397568 | tf_op jit(solution)/shard_map/sub | solution.py:20
  28.8 1.1 %fusion.10 = f32[2,4,128,128]{2,3,1,0:T(8,128)S(1)} fusion(bf16[2,128,4,32]{1,3,2,0:T(8,128)(2,1)} %bitcast.149, bf16[2,128,4,32]{1,3,2,0:T(8,128)(2,1)S(1)} %bitcast.147, f32[4,128,128]{1,2,0:T(8,128)S(1)} %copy.39, pred[2,128]{1,0:T(4,128)(4,1)S(1)} %get-tuple-element.36), kind=kOutput, calls=%fused_computation.16 | convolution fusion | flops 8781824 | bytes 917760 | tf_op jit(solution)/shard_map/xtza,xfza->xztf/dot_general | solution.py:138
  30.0 0.0 copy-start.4
  30.0 0.1 copy.47
  30.1 1.5 %fusion.91 = f32[8,2,128]{2,1,0:T(2,128)S(1)} fusion(bf16[8,128,2,32]{1,3,2,0:T(8,128)(2,1)} %bitcast.143, bf16[8,128,2,32]{1,3,2,0:T(8,128)(2,1)} %bitcast.141, f32[2,128,128]{1,2,0:T(8,128)S(1)} %copy.47, pred[128]{0:T(512)(128)(4,1)S(1)} %broadcast_compare_fusion.1), kind=kOutput, calls=%fused_computation.133 | convolution fusion | flops 18088064 | bytes 401536 | tf_op jit(solution)/shard_map/sub | solution.py:20
  31.7 1.4 %fusion.6 = f32[8,2,128,128]{2,3,1,0:T(8,128)} fusion(bf16[8,128,2,32]{1,3,2,0:T(8,128)(2,1)S(1)} %bitcast.144, bf16[8,128,2,32]{1,3,2,0:T(8,128)(2,1)S(1)} %bitcast.142, f32[2,128,128]{1,2,0:T(8,128)S(1)} %copy.47, pred[128]{0:T(512)(128)(4,1)S(1)} %broadcast_compare_fusion.1), kind=kOutput, calls=%fused_computation.9 | convolution fusion | flops 17563648 | bytes 1441920 | tf_op jit(solution)/shard_map/ijhd,ikhd->ihjk/dot_general | solution.py:148
  33.1 0.2 fusion.42
  33.3 0.7 %fusion.61 = bf16[2,128,128]{1,2,0:T(8,128)(2,1)} fusion(f32[4,2,128,128]{2,3,0,1:T(8,128)S(1)} %get-tuple-element.41, f32[2,4,32,128]{3,2,1,0:T(8,128)S(1)} %fusion.42), kind=kLoop, calls=%fused_computation.82 | loop fusion | flops 163840 | bytes 327680 | tf_op jit(solution)/shard_map/convert_element_type | solution.py:146
  34.0 1.5 %collective-permute-start = (bf16[2,128,128]{1,2,0:T(8,128)(2,1)}, bf16[2,128,128]{1,2,0:T(8,128)(2,1)}, u32[]{:S(2)}, u32[]{:S(2)}) collective-permute-start(bf16[2,128,128]{1,2,0:T(8,128)(2,1)} %fusion.61), channel_id=1, source_target_pairs={{0,1},{1,0},{2,3},{3,2},{4,5},{5,4},{6,7},{7,6},{8,9},{9,8},{10,11... | collective-permute-start | bytes 196616 | tf_op jit(solution)/shard_map/ppermute | solution.py:35
  35.5 0.5 reshape.144
  36.0 0.5 %copy.51 = bf16[32,128,32]{1,0,2:T(8,128)(2,1)S(1)} copy(bf16[32,128,32]{2,1,0:T(8,128)(2,1)S(1)} %reshape.144) | data formatting | bytes 524288 | tf_op jit(solution)/shard_map/reshape | solution.py:119
  36.5 0.1 reshape.143
  36.7 0.1 copy.50
  36.8 2.0 %fusion.2 = bf16[8,128,32,32]{1,2,3,0:T(8,128)(2,1)} fusion(f32[8,128]{1,0:T(8,128)S(1)} %fusion.69, bf16[32,128,32]{1,0,2:T(8,128)(2,1)S(1)} %copy.51, bf16[32,1,8,32]{0,3,2,1:T(8,128)(2,1)S(1)} %copy.50), kind=kOutput, calls=%fused_computation.3 | convolution fusion | flops 69206016 | bytes 2379776 | tf_op jit(solution)/shard_map/while/body/eval_jaxpr/dot_general | solution.py:186
  38.9 1.9 %fusion.21 = f32[8,2,32,128]{3,2,1,0:T(8,128)S(1)} fusion(bf16[8,128,2,32]{1,3,2,0:T(8,128)(2,1)S(1)} %bitcast.150, f32[8,2,128]{2,1,0:T(2,128)S(1)} %fusion.91, f32[8,2,128,128]{2,3,1,0:T(8,128)} %fusion.6), kind=kOutput, calls=%fused_computation.35 | convolution fusion | flops 17565824 | bytes 1449984 | tf_op jit(solution)/shard_map/ihjk,ikhd->ijhd/dot_general | solution.py:153
  40.8 0.1 fusion.41
  40.9 0.0 copy-start.8
  40.9 0.0 copy-start.7
  40.9 2.5 %copy.52 = bf16[8,128,32,32]{1,3,2,0:T(8,128)(2,1)S(1)} copy(bf16[8,128,32,32]{1,2,3,0:T(8,128)(2,1)} %fusion.2) | data formatting | bytes 4194304 | tf_op jit(solution)/shard_map/while/body/eval_jaxpr/convert_element_type | solution.py:190
  43.3 0.0 copy-start.9
  43.3 0.6 %collective-permute-start.2 = (bf16[8,128,64]{1,2,0:T(8,128)(2,1)S(1)}, bf16[8,128,64]{1,2,0:T(8,128)(2,1)}, u32[]{:S(2)}, u32[]{:S(2)}) collective-permute-start(bf16[8,128,64]{1,2,0:T(8,128)(2,1)S(1)} %fusion.41), channel_id=1, source_target_pairs={{0,1},{1,0},{2,3},{3,2},{4,5},{5,4},{6,7},{7,6},{8,9},{9,8},{10,11... | collective-permute-start | bytes 393224 | tf_op jit(solution)/shard_map/ppermute | solution.py:35
  44.0 0.9 %broadcast_select_fusion.3 = (bf16[2,128,128]{1,2,0:T(8,128)(2,1)S(1)}, bf16[2,128,128]{1,2,0:T(8,128)(2,1)S(1)}) fusion(bf16[2,128,128]{1,2,0:T(8,128)(2,1)} %fusion.61, bf16[2,128,128]{1,2,0:T(8,128)(2,1)} %collective-permute-done, pred[]{:T(512)S(6)} %eq.2), kind=kLoop, calls=%fused_computation.89 | loop fusion | flops 65536 | bytes 262145 | tf_op jit(solution)/shard_map/jit(_where)/select_n | solution.py:38
  44.9 0.3 fusion.89
  45.1 0.1 multiply_reduce_fusion
  45.2 1.4 %fusion.13 = f32[2,128,256]{1,2,0:T(8,128)S(1)} fusion(bf16[512,256]{1,0:T(8,128)(2,1)S(1)} %copy-done.7, bf16[256,512]{1,0:T(8,128)(2,1)} %param.22, f32[2,128,256]{1,2,0:T(8,128)S(1)} %get-tuple-element.43, f32[2,128]{1,0:T(2,128)S(1)} %add_rsqrt_fusion.1, f32[2,128]{1,0:T(2,128)S(1)} %broadcast_multiply_fusion.1), kind=kOutput, calls=%fused_computation.21 | convolution fusion | flops 134676480 | bytes 1050624 | tf_op jit(solution)/shard_map/srf,fc->src/dot_general | solution.py:172
  46.6 0.0 copy-start.13
  46.7 1.6 %collective-permute-start.1 = (bf16[2,128,128]{1,2,0:T(8,128)(2,1)S(1)}, bf16[2,128,128]{1,2,0:T(8,128)(2,1)S(1)}, u32[]{:S(2)}, u32[]{:S(2)}) collective-permute-start(bf16[2,128,128]{1,2,0:T(8,128)(2,1)S(1)} %select_convert_fusion), channel_id=1, source_target_pairs={{0,1},{1,0},{2,3},{3,2},{4,5},{5,4},{6,7},{7,6},{8,9},{9,8},{10,11... | collective-permute-start | bytes 196616 | tf_op jit(solution)/shard_map/ppermute | solution.py:55
  48.2 0.5 fusion.54
  48.7 2.3 %collective-permute-done.1 = bf16[2,128,128]{1,2,0:T(8,128)(2,1)S(1)} collective-permute-done((bf16[2,128,128]{1,2,0:T(8,128)(2,1)S(1)}, bf16[2,128,128]{1,2,0:T(8,128)(2,1)S(1)}, u32[]{:S(2)}, u32[]{:S(2)}) %collective-permute-start.1) | collective-permute-done | bytes 65568 | tf_op jit(solution)/shard_map/ppermute | solution.py:55
  51.0 0.7 %copy.54 = bf16[2,128,128]{2,1,0:T(8,128)(2,1)} copy(bf16[2,128,128]{1,2,0:T(8,128)(2,1)S(1)} %add_convert_fusion) | data formatting | bytes 131072
  51.8 0.9 %broadcast_select_fusion.1 = (bf16[8,128,64]{1,2,0:T(8,128)(2,1)S(1)}, bf16[8,128,64]{1,2,0:T(8,128)(2,1)S(1)}) fusion(bf16[8,128,64]{1,2,0:T(8,128)(2,1)S(1)} %fusion.41, bf16[8,128,64]{1,2,0:T(8,128)(2,1)} %collective-permute-done.2, pred[]{:T(512)S(6)} %eq.2), kind=kLoop, calls=%fused_computation.84 | loop fusion | flops 131072 | bytes 524289 | tf_op jit(solution)/shard_map/jit(_where)/select_n | solution.py:38
  52.7 0.8 %fusion.14 = bf16[8,128,64]{1,2,0:T(8,128)(2,1)} fusion(f32[8,128,64]{1,2,0:T(8,128)S(1)} %fusion.54, bf16[8,128,64]{1,2,0:T(8,128)(2,1)S(1)} %get-tuple-element.28, bf16[8,128,64]{1,2,0:T(8,128)(2,1)S(1)} %get-tuple-element.27, bf16[8,128,64]{1,2,0:T(8,128)(2,1)S(1)} %copy-done.3, bf16[128,64]{0,1:T(8,128)(2,1)S(1)} %copy-done.13), kind=kOutput, calls=%fused_computation.22 | convolution fusion | flops 17563648 | bytes 802816 | tf_op jit(solution)/shard_map/dot_general | solution.py:200
  (48 shorter events, 0.3 us)
Async XLA Ops:
  0.6 15.5 %copy-start = (bf16[4,256,128]{2,1,0:T(8,128)(2,1)S(1)}, bf16[4,256,128]{2,1,0:T(8,128)(2,1)}, u32[]{:S(2)}) copy-start(bf16[4,256,128]{2,1,0:T(8,128)(2,1)} %param.20) | copy-start | bytes 786436
  3.8 13.6 %copy-start.1 = (bf16[8,128,128]{2,1,0:T(8,128)(2,1)S(1)}, bf16[8,128,128]{2,1,0:T(8,128)(2,1)}, u32[]{:S(2)}) copy-start(bf16[8,128,128]{2,1,0:T(8,128)(2,1)} %param.15) | copy-start | bytes 786436
  3.8 13.6 %copy-start.12 = (bf16[4,128,64]{1,2,0:T(8,128)(2,1)S(1)}, bf16[4,128,64]{1,2,0:T(8,128)(2,1)}, u32[]{:S(2)}) copy-start(bf16[4,128,64]{1,2,0:T(8,128)(2,1)} %param.24) | copy-start | bytes 196612
  8.8 16.0 %all-to-all-start = ((bf16[8,120,128]{2,1,0:T(8,128)(2,1)}), bf16[8,120,128]{2,1,0:T(8,128)(2,1)S(1)}, u32[]{:S(2)}, u32[]{:S(2)}) async-start(bf16[8,120,128]{2,1,0:T(8,128)(2,1)} %bitcast.133), calls=%async_computation | async-start | bytes 491520 | tf_op jit(solution)/shard_map/all_to_all | solution.py:112
  16.1 3.0 %copy-start.14 = (s32[128]{0:T(128)S(1)}, s32[128]{0:T(128)}, u32[]{:S(2)}) copy-start(s32[128]{0:T(128)} %param.17) | copy-start | bytes 1540
  19.9 7.7 %copy-start.6 = (bf16[1,2,128,128]{2,3,0,1:T(8,128)(2,1)S(1)}, bf16[1,2,128,128]{2,3,0,1:T(8,128)(2,1)}, u32[]{:S(2)}) copy-start(bf16[1,2,128,128]{2,3,0,1:T(8,128)(2,1)} %get-tuple-element.29) | copy-start | bytes 196612
  27.1 2.9 %copy-start.2 = (bf16[8,2,15360]{2,1,0:T(2,128)(2,1)}, bf16[8,2,15360]{2,1,0:T(2,128)(2,1)S(1)}, u32[]{:S(2)}) copy-start(bf16[8,2,15360]{2,1,0:T(2,128)(2,1)S(1)} %reshape.139) | copy-start | bytes 1474564
  30.0 1.7 %copy-start.4 = (bf16[1,8,128,64]{2,3,0,1:T(8,128)(2,1)S(1)}, bf16[1,8,128,64]{2,3,0,1:T(8,128)(2,1)}, u32[]{:S(2)}) copy-start(bf16[1,8,128,64]{2,3,0,1:T(8,128)(2,1)} %get-tuple-element.24) | copy-start | bytes 393220
  30.0 1.7 %copy-start.5 = (bf16[1,8,128,64]{2,3,0,1:T(8,128)(2,1)S(1)}, bf16[1,8,128,64]{2,3,0,1:T(8,128)(2,1)}, u32[]{:S(2)}) copy-start(bf16[1,8,128,64]{2,3,0,1:T(8,128)(2,1)} %get-tuple-element.25) | copy-start | bytes 393220
  30.0 3.1 %copy-start.11 = (bf16[1,2,128,128]{2,3,0,1:T(8,128)(2,1)S(1)}, bf16[1,2,128,128]{2,3,0,1:T(8,128)(2,1)}, u32[]{:S(2)}) copy-start(bf16[1,2,128,128]{2,3,0,1:T(8,128)(2,1)} %get-tuple-element.31) | copy-start | bytes 196612
  31.7 3.8 %slice-start = ((bf16[8,2,15360]{2,1,0:T(2,128)(2,1)}), bf16[8,2,8192]{2,1,0:T(2,128)(2,1)S(1)}, s32[]{:S(2)}) async-start(bf16[8,2,15360]{2,1,0:T(2,128)(2,1)} %copy-done.2), calls=%async_computation.1 | async-start | bytes 524288 | tf_op jit(solution)/shard_map/slice | solution.py:119
  33.1 3.5 %slice-start.1 = ((bf16[8,2,15360]{2,1,0:T(2,128)(2,1)}), bf16[8,2,1024]{2,1,0:T(2,128)(2,1)S(1)}, s32[]{:S(2)}) async-start(bf16[8,2,15360]{2,1,0:T(2,128)(2,1)} %copy-done.2), calls=%async_computation.2 | async-start | bytes 65536 | tf_op jit(solution)/shard_map/slice | solution.py:120
  34.0 10.0 %collective-permute-start = (bf16[2,128,128]{1,2,0:T(8,128)(2,1)}, bf16[2,128,128]{1,2,0:T(8,128)(2,1)}, u32[]{:S(2)}, u32[]{:S(2)}) collective-permute-start(bf16[2,128,128]{1,2,0:T(8,128)(2,1)} %fusion.61), channel_id=1, source_target_pairs={{0,1},{1,0},{2,3},{3,2},{4,5},{5,4},{6,7},{7,6},{8,9},{9,8},{10,11... | collective-permute-start | bytes 196616 | tf_op jit(solution)/shard_map/ppermute | solution.py:35
  36.8 2.0 %copy-start.10 = (bf16[1,8,128,64]{2,3,0,1:T(8,128)(2,1)S(1)}, bf16[1,8,128,64]{2,3,0,1:T(8,128)(2,1)}, u32[]{:S(2)}) copy-start(bf16[1,8,128,64]{2,3,0,1:T(8,128)(2,1)} %get-tuple-element.26) | copy-start | bytes 393220
  40.9 4.0 %copy-start.8 = (bf16[256,256]{1,0:T(8,128)(2,1)S(1)}, bf16[256,256]{1,0:T(8,128)(2,1)}, u32[]{:S(2)}) copy-start(bf16[256,256]{1,0:T(8,128)(2,1)} %param.21) | copy-start | bytes 393220
  40.9 4.3 %copy-start.7 = (bf16[512,256]{1,0:T(8,128)(2,1)S(1)}, bf16[512,256]{1,0:T(8,128)(2,1)}, u32[]{:S(2)}) copy-start(bf16[512,256]{1,0:T(8,128)(2,1)} %param.23) | copy-start | bytes 786436
  43.3 4.9 %copy-start.9 = (bf16[1024,64]{0,1:T(8,128)(2,1)S(1)}, bf16[1024,64]{0,1:T(8,128)(2,1)}, u32[]{:S(2)}) copy-start(bf16[1024,64]{0,1:T(8,128)(2,1)} %param.27) | copy-start | bytes 393220
  43.3 8.4 %collective-permute-start.2 = (bf16[8,128,64]{1,2,0:T(8,128)(2,1)S(1)}, bf16[8,128,64]{1,2,0:T(8,128)(2,1)}, u32[]{:S(2)}, u32[]{:S(2)}) collective-permute-start(bf16[8,128,64]{1,2,0:T(8,128)(2,1)S(1)} %fusion.41), channel_id=1, source_target_pairs={{0,1},{1,0},{2,3},{3,2},{4,5},{5,4},{6,7},{7,6},{8,9},{9,8},{10,11... | collective-permute-start | bytes 393224 | tf_op jit(solution)/shard_map/ppermute | solution.py:35
  46.6 6.1 %copy-start.3 = (bf16[8,128,64]{1,2,0:T(8,128)(2,1)S(1)}, bf16[8,128,64]{1,2,0:T(8,128)(2,1)}, u32[]{:S(2)}) copy-start(bf16[8,128,64]{1,2,0:T(8,128)(2,1)} %copy.73) | copy-start | bytes 393220
  46.6 6.1 %copy-start.13 = (bf16[128,64]{0,1:T(8,128)(2,1)S(1)}, bf16[128,64]{0,1:T(8,128)(2,1)}, u32[]{:S(2)}) copy-start(bf16[128,64]{0,1:T(8,128)(2,1)} %param.25) | copy-start | bytes 49156
  46.7 4.3 %collective-permute-start.1 = (bf16[2,128,128]{1,2,0:T(8,128)(2,1)S(1)}, bf16[2,128,128]{1,2,0:T(8,128)(2,1)S(1)}, u32[]{:S(2)}, u32[]{:S(2)}) collective-permute-start(bf16[2,128,128]{1,2,0:T(8,128)(2,1)S(1)} %select_convert_fusion), channel_id=1, source_target_pairs={{0,1},{1,0},{2,3},{3,2},{4,5},{5,4},{6,7},{7,6},{8,9},{9,8},{10,11... | collective-permute-start | bytes 196616 | tf_op jit(solution)/shard_map/ppermute | solution.py:55

commit v2 on v1

v2 whole, which is shorter than its diff:
```python
import functools
import math

import jax
import jax.numpy as jnp
from jax import lax
from jax.experimental import pallas as pl
from jax.experimental.pallas import tpu as pltpu
from jax.sharding import PartitionSpec as P


PER_FOCUS_DIM = 32
F32 = jnp.float32
BF16 = jnp.bfloat16
LOG2E = math.log2(math.e)
SCALE = LOG2E / math.sqrt(PER_FOCUS_DIM)
FAR = -1.0e30

VMEM = pl.BlockSpec(memory_space=pltpu.VMEM)
HBM = pl.BlockSpec(memory_space=pltpu.HBM)


def nt(a, b):
    return lax.dot_general(a, b, (((1,), (1,)), ((), ())), preferred_element_type=F32)


def nn(a, b):
    return lax.dot_general(a, b, (((1,), (0,)), ((), ())), preferred_element_type=F32)


def normed(values):
    values = values.astype(F32)
    center = values - jnp.mean(values, -1, keepdims=True)
    spread = jnp.mean(center * center, -1, keepdims=True)
    return center * lax.rsqrt(spread + 1e-05)


def places(shape, axis):
    return lax.broadcasted_iota(jnp.int32, shape, axis)


def place_of(cores):
    return lax.axis_index("rows") * cores + lax.axis_index("branch")


def span_of(bounds_ref, which):
    bounds = bounds_ref[...].astype(F32)
    kept = jnp.where(places(bounds.shape, 1) == which, bounds, 0.0)
    span = jnp.sum(kept, axis=1, keepdims=True)
    return span[0:1], span[1:2]


def within(at, begin, end):
    at = at.astype(F32)
    return (at >= begin) & (at < end)


def fetch(pairs, sem):
    copies = [pltpu.make_async_copy(a, b, sem.at[j]) for j, (a, b) in enumerate(pairs)]
    for copy in copies:
        copy.start()
    return copies


def pre_kernel(cores, *refs):
    pay_ref, sem = refs[6], refs[13]
    copies = fetch(list(zip(refs[:6], refs[7:13])), sem)
    x_ref, p_ref, mb_ref, tb_ref, lr_ref, bounds_ref = refs[7:13]
    seqs, length, _ = x_ref.shape
    rows = p_ref.shape[0]
    chips = pay_ref.shape[0]
    for copy in copies:
        copy.wait()
    bias_w = jnp.concatenate([mb_ref[...].astype(F32), tb_ref[...].astype(F32)], axis=0)
    bias_w = bias_w.astype(BF16)
    heads = bias_w.shape[0]
    depth = lr_ref.shape[1]
    first_seq = place_of(cores) * seqs
    pieces = []
    biases = []
    for i in range(rows):
        pn = normed(p_ref[i]).astype(BF16)
        biases.append(nt(bias_w, pn))
    for h in range(heads):
        pieces.append(jnp.concatenate([b[h : h + 1] for b in biases], axis=0))
    left = None
    zero = jnp.zeros(lr_ref.shape[1:], BF16)
    for s in range(seqs):
        xn = normed(x_ref[s]).astype(BF16)
        begin, end = span_of(bounds_ref, first_seq + s)
        seen = within(places((1, length), 1), begin, end)
        pieces.append(nt(lr_ref[1], xn) * seen.astype(F32))
        weight = jnp.concatenate(
            [lr_ref[0] if other == s else zero for _ in range(cores) for other in range(seqs)],
            axis=0,
        )
        term = nt(xn, weight) * within(places((length, 1), 0), begin, end).astype(F32)
        left = term if left is None else left + term
    width = left.shape[1]
    group = places((rows, width), 1) // (seqs * depth)
    copied = jnp.concatenate(pieces, axis=0).astype(BF16)
    count = copied.shape[0]
    for d in range(chips):
        pay_ref[d, 0:count, :] = copied
        mine = left[d * cores * rows : d * cores * rows + rows]
        for c in range(1, cores):
            begin = (d * cores + c) * rows
            mine = jnp.where(group == c, left[begin : begin + rows], mine)
        if width < length:
            mine = jnp.concatenate([mine, jnp.zeros((rows, length - width), F32)], axis=1)
        pay_ref[d, count : count + rows, :] = mine.astype(BF16)


def proj_kernel(heads, pair_heads, *refs):
    count = 5
    sm_ref, v_ref, g_ref, st_ref, pv_ref, pg_ref, own_ref, lay_ref = refs[count : count + 8]
    held = refs[count + 8 : 2 * count + 8]
    turn_ref, rows_ref, sem = refs[2 * count + 8 :]
    copies = fetch(list(zip(refs[:count], held)), sem)
    x_ref, p_ref, aw_ref, pw_ref, ow_ref = held
    seqs, _, _ = x_ref.shape
    rows = p_ref.shape[0]
    for copy in copies:
        copy.wait()
    for s in range(seqs):
        xn = normed(x_ref[s]).astype(BF16)
        q = nn(xn, aw_ref[0]).astype(BF16)
        k = nn(xn, aw_ref[1]).astype(BF16)
        v_ref[s] = nn(xn, aw_ref[2]).astype(BF16)
        g_ref[s] = jax.nn.sigmoid(nn(xn, aw_ref[3]))
        head = places(q.shape, 1) // PER_FOCUS_DIM
        for h in range(heads):
            sm_ref[s, h] = nt(jnp.where(head == h, q, jnp.zeros_like(q)), k) * SCALE
    qv = jnp.concatenate([pw_ref[0], pw_ref[2]], axis=0)
    kg = jnp.concatenate([pw_ref[1], pw_ref[3]], axis=0)
    width = own_ref.shape[1]
    begin = pl.multiple_of(lax.axis_index("head") * width, width)
    for i in range(rows):
        pn = normed(p_ref[i]).astype(BF16)
        first = nt(pn, qv).astype(BF16)
        second = nt(pn, kg)
        pv_ref[i] = first
        pg_ref[i] = jax.nn.sigmoid(second)
        second = second.astype(BF16)
        head = places(first.shape, 1) // PER_FOCUS_DIM
        for h in range(pair_heads):
            st_ref[i, h] = nt(jnp.where(head == h, first, jnp.zeros_like(first)), second) * SCALE
        turn_ref[...] = p_ref[i].astype(F32).T
        own_ref[i] = turn_ref[pl.ds(begin, width), :].astype(BF16)
    groups = 128 // width
    steps = lay_ref.shape[1] // 128
    depth = steps * groups
    turned = ow_ref[...].astype(F32)
    rows_ref[...] = jnp.concatenate([turned] * groups, axis=0).T
    group = places((depth, 128), 1) // width
    for step in range(steps):
        tile = rows_ref[pl.ds(step, depth, stride=depth), :]
        for g in range(1, groups):
            part = rows_ref[pl.ds(g * steps + step, depth, stride=depth), :]
            tile = jnp.where(group == g, part, tile)
        lay_ref[:, step * 128 : (step + 1) * 128] = tile.astype(BF16)


def gather_bias(bias_ref, mine_ref, other_ref, first, heads, rows, cores):
    chips = mine_ref.shape[0]
    core = lax.axis_index("branch")
    for d in range(chips):
        for ref, c in ((mine_ref, core), (other_ref, 1 - core)):
            begin = pl.multiple_of((d * cores + c) * rows, rows)
            block = ref[d, first * rows : (first + heads) * rows, :].astype(F32) * LOG2E
            for h in range(heads):
                bias_ref[h, pl.ds(begin, rows), :] = block[h * rows : (h + 1) * rows]


def attend(scores, values, gate, offset):
    width = values.shape[1]
    head = (places(values.shape, 1) - offset) // PER_FOCUS_DIM
    inside = places(values.shape, 1) >= offset
    mixed = total = None
    for h, score in enumerate(scores):
        top = jnp.max(score, axis=-1, keepdims=True)
        weights = jnp.exp2(score - top).astype(BF16)
        here = (head == h) & inside
        value = jnp.where(here, values, jnp.zeros_like(values))
        ones = jnp.where(here, jnp.ones_like(values), jnp.zeros_like(values))
        if width % 128 == 0:
            both = nn(weights, jnp.concatenate([value, ones], axis=1))
            part, norm = both[:, :width], both[:, width:]
        else:
            part, norm = nn(weights, value), nn(weights, ones)
        mixed = part if mixed is None else mixed + part
        total = norm if total is None else total + norm
    return gate * mixed / jnp.where(total > 0, total, 1.0)


def align_kernel(cores, rows, mine_ref, other_ref, sm_ref, v_ref, g_ref, bounds_ref, out_ref, bias_ref):
    seqs, heads, length, _ = sm_ref.shape
    gather_bias(bias_ref, mine_ref, other_ref, 0, heads, rows, cores)
    first_seq = place_of(cores) * seqs
    for s in range(seqs):
        begin, end = span_of(bounds_ref, first_seq + s)
        seen = within(places((1, length), 1), begin, end)
        scores = [jnp.where(seen, sm_ref[s, h] + bias_ref[h], FAR) for h in range(heads)]
        out_ref[s] = attend(scores, v_ref[s], g_ref[s], 0).astype(BF16)


def tri_kernel(cores, first, mine_ref, other_ref, st_ref, v_ref, g_ref, valid_ref, out_ref, bias_ref):
    rows, heads, _, _ = st_ref.shape
    offset = heads * PER_FOCUS_DIM
    gather_bias(bias_ref, mine_ref, other_ref, first, heads, rows, cores)
    seen = valid_ref[...] > 0
    for h in range(heads):
        bias_ref[h] = jnp.where(seen, bias_ref[h], FAR)
    for i in range(rows):
        scores = [st_ref[i, h] + bias_ref[h] for h in range(heads)]
        out = attend(scores, v_ref[i], g_ref[i], offset)
        out_ref[i] = out.T[offset : 2 * offset].astype(BF16)


def transition_kernel(parts, *refs):
    heads_refs = refs[:parts]
    x_ref, wo_ref, entry_ref, exit_ref = refs[parts : parts + 4]
    own_ref, sent_ref = refs[parts + 4 :]
    seqs = x_ref.shape[0]
    features = heads_refs[0].shape[2]
    here = lax.axis_index("head")
    for s in range(seqs):
        blended = x_ref[s].astype(F32)
        for j in range(parts):
            which = jnp.where(j == 0, here, 1 - here) if parts == 2 else j
            begin = pl.multiple_of(which * features, features)
            blended = blended + nn(heads_refs[j][s], wo_ref[pl.ds(begin, features), :])
        hidden = jnp.maximum(nn(normed(blended).astype(BF16), entry_ref[...]), 0.0).astype(BF16)
        partial = nn(hidden, exit_ref[...])
        if parts == 2:
            half = partial.shape[1] // 2
            own = here == 0
            kept = jnp.where(own, partial[:, :half], partial[:, half:])
            base = jnp.where(own, blended[:, :half], blended[:, half:])
            own_ref[s] = base + kept
            sent_ref[s] = jnp.where(own, partial[:, half:], partial[:, :half]).astype(BF16)
        else:
            own_ref[s] = blended
            sent_ref[s] = partial.astype(BF16)


def outer_kernel(cores, seqs, heads, mine_ref, other_ref, w_ref, bounds_ref, own_ref, out_ref, a_ref, b_ref):
    rows, width, length = out_ref.shape
    chips = mine_ref.shape[0]
    depth = w_ref.shape[0]
    lanes = depth * cores * seqs
    groups = 128 // width
    steps = depth // groups
    total = chips * cores * seqs
    core = lax.axis_index("branch")
    first = heads * rows
    lane_group = places((rows, lanes), 1) // depth
    for d in range(chips):
        for which, ref in enumerate((mine_ref, other_ref)):
            block = ref[d, first : first + seqs * depth, :].astype(F32)
            left = ref[d, first + seqs * depth : first + seqs * depth + rows, :lanes].astype(F32)
            for s in range(seqs):
                row = (d * cores + which) * seqs + s
                for g in range(groups):
                    begin = s * depth + g * steps
                    for t in range(length // 128):
                        piece = block[begin : begin + steps, t * 128 : (t + 1) * 128]
                        b_ref[g, t, pl.ds(row, steps, stride=total), :] = piece
                kept = jnp.where(lane_group == core * seqs + s, left, 0.0)
                a_ref[pl.ds(row, rows, stride=total), :] = kept
    a = a_ref[...].astype(BF16)
    begin, end = bounds_ref[0:1].astype(F32), bounds_ref[1:2].astype(F32)
    whole = within(places((length, 1), 0), begin, end).astype(BF16)
    owned = within(places((rows, 1), 0) + place_of(cores) * rows, begin, end).astype(BF16)
    count = nt(owned, whole)
    share = 1.0 / count
    gathered = [[] for _ in range(rows)]
    for step in range(steps):
        tile = jnp.concatenate([w_ref[:, step * 128 : (step + 1) * 128]] * (cores * seqs), axis=0)
        g = nn(a, tile).astype(BF16)
        for i in range(rows):
            gathered[i].append(g[i * total : (i + 1) * total])
    b = [[b_ref[g, t].T.astype(BF16) for t in range(length // 128)] for g in range(groups)]
    for i in range(rows):
        g = jnp.concatenate(gathered[i], axis=0)
        for t in range(length // 128):
            acc = None
            for k in range(groups):
                part = nn(b[k][t], g).T[k * width : (k + 1) * width]
                acc = part if acc is None else acc + part
            at = slice(t * 128, (t + 1) * 128)
            out_ref[i, :, at] = acc * share[i : i + 1, at] + own_ref[i, :, at].astype(F32)


def close_kernel(parts, *refs):
    heads_refs = refs[:parts]
    opm_ref, w_ref, base_ref, sum_ref, out_ref, new_ref = refs[parts:]
    new_ref[...] = (base_ref[...] + sum_ref[...].astype(F32)).astype(BF16)
    rows = opm_ref.shape[0]
    features = heads_refs[0].shape[1]
    own = lax.axis_index("head") == 0
    weights = [w_ref[:, j * features : (j + 1) * features].astype(F32) for j in range(parts)]
    if parts == 2:
        weights = [jnp.where(own, weights[0], weights[1]), jnp.where(own, weights[1], weights[0])]
    weights = [w.astype(BF16) for w in weights]
    for i in range(rows):
        out = opm_ref[i]
        for j in range(parts):
            out = out + nn(weights[j], heads_refs[j][i])
        out_ref[i] = out.astype(BF16)


def call(kernel, ins, outs, scratch=(), left=(), flops=0):
    size = sum(a.size * a.dtype.itemsize for a in ins) + sum(
        math.prod(s) * jnp.dtype(d).itemsize for s, d in outs
    )
    held = sum(a.inner_aval.size * 4 for a in scratch)
    limit = min(max((size + held) * 2, 8 << 20), 60 << 20)
    return pl.pallas_call(
        kernel,
        compiler_params=pltpu.CompilerParams(vmem_limit_bytes=limit),
        out_shape=tuple(jax.ShapeDtypeStruct(s, d) for s, d in outs),
        in_specs=[HBM if i in left else VMEM for i in range(len(ins))],
        out_specs=tuple(VMEM for _ in outs),
        scratch_shapes=list(scratch),
        cost_estimate=pl.CostEstimate(flops=flops, bytes_accessed=size, transcendentals=0),
    )(*ins)


def held_copies(arrays):
    return [*(pltpu.VMEM(a.shape, a.dtype) for a in arrays), pltpu.SemaphoreType.DMA((len(arrays),))]


def from_heads(value):
    if lax.axis_size("head") == 2:
        return [value, lax.ppermute(value, "head", [(0, 1), (1, 0)])]
    every = lax.all_gather(value, "head", axis=0)
    return [every[j] for j in range(every.shape[0])]


def local(
    lineup_state,
    pairwise,
    aligned_residue_bounds,
    residue_valid_mask,
    coupling_offset_weight_map,
    triangle_bias_matrix,
    alignment_projection_matrix,
    lineup_readout_weight,
    feedfwd_entry_weight,
    feedfwd_exit_weight,
    pair_projection_matrix,
    pair_output_matrix,
    left_right_maps,
    outer_product_output_matrix,
):
    seqs, length, channels = lineup_state.shape
    rows, _, pair_channels = pairwise.shape
    heads = coupling_offset_weight_map.shape[1]
    pair_heads = triangle_bias_matrix.shape[1]
    every_head = heads + pair_heads
    depth = left_right_maps.shape[2]
    chips = lax.axis_size("rows")
    cores = lax.axis_size("branch")
    parts = lax.axis_size("head")
    width = outer_product_output_matrix.shape[1]
    features = heads * PER_FOCUS_DIM
    pair_features = pair_heads * PER_FOCUS_DIM
    total = chips * cores * seqs
    bounds = aligned_residue_bounds.T

    first = (
        lineup_state,
        pairwise,
        coupling_offset_weight_map.T,
        triangle_bias_matrix.T,
        jnp.swapaxes(left_right_maps, 1, 2),
        bounds,
    )
    (payload,) = call(
        functools.partial(pre_kernel, cores),
        first,
        (((chips, every_head * rows + seqs * depth + rows, length), BF16),),
        scratch=held_copies(first),
        left=range(len(first)),
    )
    mine = lax.all_to_all(payload, "rows", 0, 0, tiled=True)
    other = lax.ppermute(mine, "branch", [(0, 1), (1, 0)])

    groups = 128 // width
    second = (
        lineup_state,
        pairwise,
        alignment_projection_matrix,
        jnp.swapaxes(pair_projection_matrix, 1, 2),
        outer_product_output_matrix.T,
    )
    scores, values, gate, tri_scores, tri_values, tri_gate, own_pair, outer_w = call(
        functools.partial(proj_kernel, heads, pair_heads),
        second,
        (
            ((seqs, heads, length, length), F32),
            ((seqs, length, features), BF16),
            ((seqs, length, features), F32),
            ((rows, pair_heads, length, length), F32),
            ((rows, length, 2 * pair_features), BF16),
            ((rows, length, 2 * pair_features), F32),
            ((rows, width, length), BF16),
            ((depth, depth * width), BF16),
        ),
        scratch=[
            *held_copies(second)[:-1],
            pltpu.VMEM((pair_channels, length), F32),
            pltpu.VMEM((depth * depth, 128), F32),
            held_copies(second)[-1],
        ],
        left=range(len(second)),
        flops=1 << 28,
    )

    (mixed,) = call(
        functools.partial(align_kernel, cores, rows),
        (mine, other, scores, values, gate, bounds),
        (((seqs, length, features), BF16),),
        scratch=[pltpu.VMEM((heads, length, length), F32)],
        flops=1 << 28,
    )
    mixed = from_heads(mixed)
    (pair_mixed,) = call(
        functools.partial(tri_kernel, cores, heads),
        (mine, other, tri_scores, tri_values, tri_gate, residue_valid_mask.reshape(1, -1)),
        (((rows, pair_features, length), BF16),),
        scratch=[pltpu.VMEM((pair_heads, length, length), F32)],
        flops=1 << 28,
    )
    pair_mixed = from_heads(pair_mixed)

    out_channels = channels // 2 if parts == 2 else channels
    owned, partial = call(
        functools.partial(transition_kernel, parts),
        (*mixed, lineup_state, lineup_readout_weight, feedfwd_entry_weight, feedfwd_exit_weight),
        (((seqs, length, out_channels), F32), ((seqs, length, out_channels), BF16)),
        flops=1 << 28,
    )
    if parts == 2:
        received = lax.ppermute(partial, "head", [(0, 1), (1, 0)])
    else:
        own_width = channels // parts
        received = lax.psum_scatter(partial, "head", scatter_dimension=2, tiled=True)
        owned = lax.dynamic_slice_in_dim(owned, lax.axis_index("head") * own_width, own_width, 2)

    (opm,) = call(
        functools.partial(outer_kernel, cores, seqs, every_head),
        (mine, other, outer_w, bounds, own_pair),
        (((rows, width, length), F32),),
        scratch=[
            pltpu.VMEM((rows * total, depth * cores * seqs), F32),
            pltpu.VMEM((groups, length // 128, depth // groups * total, 128), F32),
        ],
        flops=1 << 28,
    )
    pair_out, refreshed = call(
        functools.partial(close_kernel, parts),
        (*pair_mixed, opm, pair_output_matrix.T, owned, received),
        (((rows, width, length), BF16), (owned.shape, BF16)),
        flops=1 << 26,
    )
    return (refreshed, jnp.swapaxes(pair_out, 1, 2))


def solution(mesh):
    in_specs = (
        P(("parts", "rows", "branch"), None, None),
        P(("parts", "rows", "branch"), None, None),
        P("parts", None),
        P("parts"),
        P(None, "head"),
        P(None, "head"),
        P(None, None, "head"),
        P(),
        P(None, "head"),
        P("head", None),
        P(None, None, "head"),
        P(None, "head"),
        P(),
        P(None, "head"),
    )
    out_specs = (
        P(("parts", "rows", "branch"), None, "head"),
        P(("parts", "rows", "branch"), None, "head"),
    )


    return jax.shard_map(local, mesh=mesh, in_specs=in_specs, out_specs=out_specs, check_vma=False)
```

time: 54.2 us -> 35.8 us (0.66)
  matrix products: 16.1 us -> 0 us
  blocking collectives: 2.15 us -> 15.9 us
  Pallas kernels: 0 us -> 8.82 us
  starting transfers between devices: 11 us -> 3.72 us
  local copies, waits for them, and re-layouts: 10.6 us -> 3.98 us
  other arithmetic: 5.38 us -> 0 us
  waiting for transfers between devices: 7.23 us -> 2.32 us
    all_to_all x0 -> x1, blocking collectives: none -> 15.9 us  [local(): mine = lax.all_to_all(payload, 'rows', 0, 0, tiled=True)]
    dot_general x14 -> x0, matrix products: 13.3 us -> none  [the longest x1 2.03 us: outer_block(): lax.dot_general(left_own, cols, (((0,), (0,)), ((), ())), preferred_eleme...]
    pallas_call x0 -> x7, Pallas kernels: none -> 8.82 us  [call(): pl.pallas_call(kernel, compiler_params=pltpu.CompilerParams(vmem_limit_by...]
    all_to_all x1 -> x0, starting transfers between devices: 7.31 us -> none  [local(): got = lax.all_to_all(payload, 'rows', 0, 0, tiled=True)]
    all_to_all x1 -> x0, waiting for transfers between devices: 4.93 us -> none  [local(): got = lax.all_to_all(payload, 'rows', 0, 0, tiled=True)]
    sub x2 -> x0, matrix products: 2.77 us -> none  [soft_weights(): shifted = jnp.exp(attention_scores - row_max)]
    convert_element_type x6 -> x0, local copies, waits for them, and re-layouts: 2.72 us -> none  [the longest x1 2.46 us: outer_block(): outer_mean = (outer_sum / counts[:, None, :, None]).astype(jnp.bfloat16)]
    reduce_sum x5 -> x0, other arithmetic: 2.57 us -> none  [the longest x3 1.43 us: layer_normalize(): spread = jnp.mean(center * center, -1, keepdims=True)]
  transfers between devices with their start and end apart: 4 -> 4, of which waited for: 2 -> 2; matrix products, arithmetic and copies ran while one was open for 29% -> 0% of each run, Pallas kernels for 0% -> 18%
where the time goes in v2:
time: 35.8 us; the launch traced here: 35.5 us
  blocking collectives  15.9 us (44%)
  Pallas kernels  8.82 us (25%)
  local copies, waits for them, and re-layouts  3.98 us (11%)
  starting transfers between devices  3.72 us (10%)
  waiting for transfers between devices  2.32 us (6%)
  between operations  0.78 us (2%)
    all_to_all x1, blocking collectives, local(): mine = lax.all_to_all(payload, 'rows', 0, 0, tiled=True)  15.9 us
    pallas_call x7, Pallas kernels, call(): pl.pallas_call(kernel, compiler_params=pltpu.CompilerParams(vmem_limit_by...  8.82 us
    unnamed x32, local copies, waits for them, and re-layouts  3.98 us
    ppermute x2, starting transfers between devices, from_heads(): return [value, lax.ppermute(value, 'head', [(0, 1), (1, 0)])]  2.16 us
    ppermute x1, starting transfers between devices, local(): received = lax.ppermute(partial, 'head', [(0, 1), (1, 0)])  1.56 us
    ppermute x1, waiting for transfers between devices, local(): received = lax.ppermute(partial, 'head', [(0, 1), (1, 0)])  1.25 us
    ppermute x2, waiting for transfers between devices, from_heads(): return [value, lax.ppermute(value, 'head', [(0, 1), (1, 0)])]  1.06 us
  transfers between devices with their start and end apart: 4, of which 2 were waited for; matrix products, arithmetic and copies ran while one was open for 0% of the time, Pallas kernels for 18%

profile of v2, /device:TPU:0, one launch (start us, length us, event | category | flops | bytes accessed | tf_op | source)
XLA Modules:
  0.0 35.5 jit_solution(9554182801412393225)
XLA Ops:
  0.6 0.0 copy-start.7
  0.6 0.0 copy-start.6
  0.7 0.0 copy-start.8
  0.7 0.7 %copy-done.7 = bf16[128,4]{0,1:T(4,128)(2,1)S(1)} copy-done((bf16[128,4]{0,1:T(4,128)(2,1)S(1)}, bf16[128,4]{0,1:T(4,128)(2,1)}, u32[]{:S(2)}) %copy-start.7) | copy-done | bytes 1048
  1.3 0.0 copy-done.6
  1.3 0.0 copy-done.8
  1.3 0.0 copy-start
  1.3 0.9 %copy-done = bf16[8,128,128]{2,1,0:T(8,128)(2,1)S(1)} copy-done((bf16[8,128,128]{2,1,0:T(8,128)(2,1)S(1)}, bf16[8,128,128]{2,1,0:T(8,128)(2,1)}, u32[]{:S(2)}) %copy-start) | copy-done | bytes 262168
  2.3 0.0 copy-start.2
  2.3 0.9 %copy-done.2 = bf16[2,128,256]{2,1,0:T(8,128)(2,1)S(1)} copy-done((bf16[2,128,256]{2,1,0:T(8,128)(2,1)S(1)}, bf16[2,128,256]{2,1,0:T(8,128)(2,1)}, u32[]{:S(2)}) %copy-start.2) | copy-done | bytes 131096
  3.2 0.0 copy-start.4
  3.2 0.8 %copy-done.4 = bf16[2,256,32]{1,2,0:T(8,128)(2,1)S(1)} copy-done((bf16[2,256,32]{1,2,0:T(8,128)(2,1)S(1)}, bf16[2,256,32]{1,2,0:T(8,128)(2,1)}, u32[]{:S(2)}) %copy-start.4) | copy-done | bytes 32792
  3.9 0.0 copy-start.10
  3.9 0.0 copy-start.13
  3.9 1.0 %shard_map.149 = bf16[8,120,128]{2,1,0:T(8,128)(2,1)S(1)} custom-call(bf16[2,128,256]{2,1,0:T(8,128)(2,1)S(1)} %copy-done.2, bf16[8,128,128]{2,1,0:T(8,128)(2,1)S(1)} %copy-done, bf16[4,128]{1,0:T(4,128)(2,1)S(1)} %bitcast.14, bf16[2,128]{1,0:T(2,128)(2,1)S(1)} %bitcast.15, bf16[2,32,256]{2,1,0:T(8,128)(2,1)S(1)} %bitcast.9, s32[2,32]{1,0:T(2,128)S(1)} %bitcast.11), custom_call_target="tpu_custom_call" | custom-call | bytes 673536 | tf_op jit(solution)/shard_map/pallas_call | solution.py:319
  4.9 0.0 copy-start.1
  4.9 0.0 copy-start.3
  4.9 0.0 copy-start.15
  4.9 15.9 %all_to_all.5.mine_ref = bf16[8,120,128]{2,1,0:T(8,128)(2,1)S(1)} all-to-all(bf16[8,120,128]{2,1,0:T(8,128)(2,1)S(1)} %shard_map.149), channel_id=1, replica_groups=mesh['parts'=1,'rows'=8,'branch'=2,'head'=2] {'rows'}, dimensions={0} | all-to-all | bytes 491520 | tf_op jit(solution)/shard_map/all_to_all | solution.py:387
  20.9 0.0 collective-permute-start
  20.9 0.0 copy-done.10
  20.9 0.0 copy-done.13
  20.9 0.0 copy-done.1
  20.9 0.0 copy-done.3
  20.9 0.0 copy-done.15
  20.9 3.1 %shard_map.150 = (f32[2,4,128,128]{3,2,1,0:T(8,128)S(1)}, bf16[2,128,128]{2,1,0:T(8,128)(2,1)S(1)}, f32[2,128,128]{2,1,0:T(8,128)S(1)}, f32[8,2,128,128]{3,2,1,0...) custom-call(bf16[2,128,256]{2,1,0:T(8,128)(2,1)S(1)} %copy-done.3, ...), custom_call_target="tpu_custom_call" | custom-call | flops 268435456 | bytes 3670016 | tf_op jit(solution)/shard_map/pallas_call | solution.py:319
  24.1 0.0 collective-permute-done.other_ref
  24.1 0.5 %shard_map.153.refs_0_ = bf16[2,128,128]{2,1,0:T(8,128)(2,1)S(1)} custom-call(bf16[8,120,128]{2,1,0:T(8,128)(2,1)S(1)} %all_to_all.5.mine_ref, bf16[8,120,128]{2,1,0:T(8,128)(2,1)S(1)} %collective-permute-done.other_ref, f32[2,4,128,128]{3,2,1,0:T(8,128)S(1)} %get-tuple-element.19.sm_ref, bf16[2,128,128]{2,1,0:T(8,128)(2,1)S(1)} %get-tuple-element.20.v_ref, ...), custom_call_target="tpu_custom_call" | custom-call | flops 268435456 | bytes 1278208 | tf_op jit(solution)/shard_map/pallas_call | solution.py:319
  24.5 1.6 %collective-permute-start.2 = (bf16[2,128,128]{2,1,0:T(8,128)(2,1)S(1)}, bf16[2,128,128]{2,1,0:T(8,128)(2,1)S(1)}, u32[]{:S(2)}, u32[]{:S(2)}) collective-permute-start(bf16[2,128,128]{2,1,0:T(8,128)(2,1)S(1)} %shard_map.153.refs_0_), channel_id=1, source_target_pairs={{0,1},{1,0},{2,3},{3,2},{4,5},{5,4},{6,7},{7,6},{8,9},{9,8},{10,11... | collective-permute-start | bytes 196616 | tf_op jit(solution)/shard_map/ppermute | solution.py:336
  26.1 0.0 copy-start.9
  26.1 0.7 %copy-done.9 = s32[128]{0:T(128)S(1)} copy-done((s32[128]{0:T(128)S(1)}, s32[128]{0:T(128)}, u32[]{:S(2)}) %copy-start.9) | copy-done | bytes 536
  26.8 0.0 copy-start.11
  26.8 0.0 copy-start.12
  26.8 0.0 copy-start.14
  26.8 0.7 %shard_map.151.refs_0_ = bf16[8,64,128]{2,1,0:T(8,128)(2,1)S(1)} custom-call(bf16[8,120,128]{2,1,0:T(8,128)(2,1)S(1)} %all_to_all.5.mine_ref, bf16[8,120,128]{2,1,0:T(8,128)(2,1)S(1)} %collective-permute-done.other_ref, f32[8,2,128,128]{3,2,1,0:T(8,128)S(1)} %get-tuple-element.14.st_ref, bf16[8,128,128]{2,1,0:T(8,128)(2,1)S(1)} %get-tuple-element.15.v_ref, ...), custom_call_target="tpu_custom_call" | custom-call | flops 268435456 | bytes 2458112 | tf_op jit(solution)/shard_map/pallas_call | solution.py:319
  27.4 0.6 %collective-permute-start.1 = (bf16[8,64,128]{2,1,0:T(8,128)(2,1)S(1)}, bf16[8,64,128]{2,1,0:T(8,128)(2,1)S(1)}, u32[]{:S(2)}, u32[]{:S(2)}) collective-permute-start(bf16[8,64,128]{2,1,0:T(8,128)(2,1)S(1)} %shard_map.151.refs_0_), channel_id=1, source_target_pairs={{0,1},{1,0},{2,3},{3,2},{4,5},{5,4},{6,7},{7,6},{8,9},{9,8},{10,11... | collective-permute-start | bytes 393224 | tf_op jit(solution)/shard_map/ppermute | solution.py:336
  28.0 1.1 %collective-permute-done.2.refs_1_ = bf16[2,128,128]{2,1,0:T(8,128)(2,1)S(1)} collective-permute-done((bf16[2,128,128]{2,1,0:T(8,128)(2,1)S(1)}, bf16[2,128,128]{2,1,0:T(8,128)(2,1)S(1)}, u32[]{:S(2)}, u32[]{:S(2)}) %collective-permute-start.2) | collective-permute-done | bytes 65568 | tf_op jit(solution)/shard_map/ppermute | solution.py:336
  29.1 0.0 copy-done.11
  29.1 0.0 copy-done.12
  29.1 0.0 copy-done.14
  29.1 1.0 %shard_map.154 = (f32[2,128,128]{2,1,0:T(8,128)S(1)}, bf16[2,128,128]{2,1,0:T(8,128)(2,1)S(1)}) custom-call(bf16[2,128,128]{2,1,0:T(8,128)(2,1)S(1)} %shard_map.153.refs_0_, bf16[2,128,128]{2,1,0:T(8,128)(2,1)S(1)} %collective-permute-done.2.refs_1_, bf16[2,128,256]{2,1,0:T(8,128)(2,1)S(1)} %copy-done.3, bf16[256,256]{1,0:T(8,128)(2,1)S(1)} %copy-done.14, ...), custom_call_target="tpu_custom_call" | custom-call | flops 268435456 | bytes 1114112 | tf_op jit(solution)/shard_map/pallas_call | solution.py:319
  30.1 1.6 %collective-permute-start.3 = (bf16[2,128,128]{2,1,0:T(8,128)(2,1)S(1)}, bf16[2,128,128]{2,1,0:T(8,128)(2,1)S(1)}, u32[]{:S(2)}, u32[]{:S(2)}) collective-permute-start(bf16[2,128,128]{2,1,0:T(8,128)(2,1)S(1)} %get-tuple-element.23), channel_id=1, source_target_pairs={{0,1},{1,0},{2,3},{3,2},{4,5},{5,4},{6,7},{7,6},{8,9},{9,8},{10,11... | collective-permute-start | bytes 196616 | tf_op jit(solution)/shard_map/ppermute | solution.py:446
  31.7 0.0 copy-start.5
  31.7 1.6 %shard_map.152.refs_2_ = f32[8,64,128]{2,1,0:T(8,128)S(1)} custom-call(bf16[8,120,128]{2,1,0:T(8,128)(2,1)S(1)} %all_to_all.5.mine_ref, bf16[8,120,128]{2,1,0:T(8,128)(2,1)S(1)} %collective-permute-done.other_ref, bf16[32,2048]{1,0:T(8,128)(2,1)S(1)} %get-tuple-element.17.w_ref, s32[2,32]{1,0:T(2,128)S(1)} %bitcast.13, ...), custom_call_target="tpu_custom_call" | custom-call | flops 268435456 | bytes 1016064 | tf_op jit(solution)/shard_map/pallas_call | solution.py:319
  33.3 1.3 %collective-permute-done.3.refs_5_ = bf16[2,128,128]{2,1,0:T(8,128)(2,1)S(1)} collective-permute-done((bf16[2,128,128]{2,1,0:T(8,128)(2,1)S(1)}, bf16[2,128,128]{2,1,0:T(8,128)(2,1)S(1)}, u32[]{:S(2)}, u32[]{:S(2)}) %collective-permute-start.3) | collective-permute-done | bytes 65568 | tf_op jit(solution)/shard_map/ppermute | solution.py:446
  34.5 0.0 collective-permute-done.1.refs_1_
  34.5 0.0 copy-done.5
  34.5 1.0 %shard_map.155 = (bf16[8,64,128]{2,1,0:T(8,128)(2,1)}, bf16[2,128,128]{2,1,0:T(8,128)(2,1)}) custom-call(bf16[8,64,128]{2,1,0:T(8,128)(2,1)S(1)} %shard_map.151.refs_0_, bf16[8,64,128]{2,1,0:T(8,128)(2,1)S(1)} %collective-permute-done.1.refs_1_, f32[8,64,128]{2,1,0:T(8,128)S(1)} %shard_map.152.refs_2_, bf16[64,128]{1,0:T(8,128)(2,1)S(1)} %bitcast.10, ...), custom_call_target="tpu_custom_call" | custom-call | flops 67108864 | bytes 933888 | tf_op jit(solution)/shard_map/pallas_call | solution.py:319
Async XLA Ops:
  0.6 0.7 %copy-start.7 = (bf16[128,4]{0,1:T(4,128)(2,1)S(1)}, bf16[128,4]{0,1:T(4,128)(2,1)}, u32[]{:S(2)}) copy-start(bf16[128,4]{0,1:T(4,128)(2,1)} %param.18) | copy-start | bytes 3076
  0.6 0.7 %copy-start.6 = (s32[32,2]{0,1:T(2,128)S(1)}, s32[32,2]{0,1:T(2,128)}, u32[]{:S(2)}) copy-start(s32[32,2]{0,1:T(2,128)} %param.16) | copy-start | bytes 772
  0.7 0.7 %copy-start.8 = (bf16[128,2]{0,1:T(2,128)(2,1)S(1)}, bf16[128,2]{0,1:T(2,128)(2,1)}, u32[]{:S(2)}) copy-start(bf16[128,2]{0,1:T(2,128)(2,1)} %param.19) | copy-start | bytes 1540
  1.3 1.0 %copy-start = (bf16[8,128,128]{2,1,0:T(8,128)(2,1)S(1)}, bf16[8,128,128]{2,1,0:T(8,128)(2,1)}, u32[]{:S(2)}) copy-start(bf16[8,128,128]{2,1,0:T(8,128)(2,1)} %refs_1_.3) | copy-start | bytes 786436
  2.3 0.9 %copy-start.2 = (bf16[2,128,256]{2,1,0:T(8,128)(2,1)S(1)}, bf16[2,128,256]{2,1,0:T(8,128)(2,1)}, u32[]{:S(2)}) copy-start(bf16[2,128,256]{2,1,0:T(8,128)(2,1)} %refs_2_.3) | copy-start | bytes 393220
  3.2 0.8 %copy-start.4 = (bf16[2,256,32]{1,2,0:T(8,128)(2,1)S(1)}, bf16[2,256,32]{1,2,0:T(8,128)(2,1)}, u32[]{:S(2)}) copy-start(bf16[2,256,32]{1,2,0:T(8,128)(2,1)} %param.26) | copy-start | bytes 98308
  3.9 16.9 %copy-start.10 = (bf16[4,256,128]{2,1,0:T(8,128)(2,1)S(1)}, bf16[4,256,128]{2,1,0:T(8,128)(2,1)}, u32[]{:S(2)}) copy-start(bf16[4,256,128]{2,1,0:T(8,128)(2,1)} %refs_2_.2) | copy-start | bytes 786436
  3.9 16.9 %copy-start.13 = (bf16[1024,64]{0,1:T(8,128)(2,1)S(1)}, bf16[1024,64]{0,1:T(8,128)(2,1)}, u32[]{:S(2)}) copy-start(bf16[1024,64]{0,1:T(8,128)(2,1)} %param.27) | copy-start | bytes 393220
  4.9 16.0 %copy-start.1 = (bf16[8,128,128]{2,1,0:T(8,128)(2,1)S(1)}, bf16[8,128,128]{2,1,0:T(8,128)(2,1)}, u32[]{:S(2)}) copy-start(bf16[8,128,128]{2,1,0:T(8,128)(2,1)} %refs_1_.3) | copy-start | bytes 786436
  4.9 16.0 %copy-start.3 = (bf16[2,128,256]{2,1,0:T(8,128)(2,1)S(1)}, bf16[2,128,256]{2,1,0:T(8,128)(2,1)}, u32[]{:S(2)}) copy-start(bf16[2,128,256]{2,1,0:T(8,128)(2,1)} %refs_2_.3) | copy-start | bytes 393220
  4.9 16.0 %copy-start.15 = (bf16[4,128,64]{1,2,0:T(8,128)(2,1)S(1)}, bf16[4,128,64]{1,2,0:T(8,128)(2,1)}, u32[]{:S(2)}) copy-start(bf16[4,128,64]{1,2,0:T(8,128)(2,1)} %param.24) | copy-start | bytes 196612
  20.9 3.2 %collective-permute-start = (bf16[8,120,128]{2,1,0:T(8,128)(2,1)S(1)}, bf16[8,120,128]{2,1,0:T(8,128)(2,1)S(1)}, u32[]{:S(2)}, u32[]{:S(2)}) collective-permute-start(bf16[8,120,128]{2,1,0:T(8,128)(2,1)S(1)} %all_to_all.5.mine_ref), channel_id=1, source_target_pairs={{0,2},{2,0},{1,3},{3,1},{4,6},{6,4},{5,7},{7,5},{8,10},{10,8},{9,1... | collective-permute-start | bytes 737288 | tf_op jit(solution)/shard_map/ppermute | solution.py:388
  24.5 4.6 %collective-permute-start.2 = (bf16[2,128,128]{2,1,0:T(8,128)(2,1)S(1)}, bf16[2,128,128]{2,1,0:T(8,128)(2,1)S(1)}, u32[]{:S(2)}, u32[]{:S(2)}) collective-permute-start(bf16[2,128,128]{2,1,0:T(8,128)(2,1)S(1)} %shard_map.153.refs_0_), channel_id=1, source_target_pairs={{0,1},{1,0},{2,3},{3,2},{4,5},{5,4},{6,7},{7,6},{8,9},{9,8},{10,11... | collective-permute-start | bytes 196616 | tf_op jit(solution)/shard_map/ppermute | solution.py:336
  26.1 0.7 %copy-start.9 = (s32[128]{0:T(128)S(1)}, s32[128]{0:T(128)}, u32[]{:S(2)}) copy-start(s32[128]{0:T(128)} %param.17) | copy-start | bytes 1540
  26.8 2.3 %copy-start.11 = (bf16[256,512]{1,0:T(8,128)(2,1)S(1)}, bf16[256,512]{1,0:T(8,128)(2,1)}, u32[]{:S(2)}) copy-start(bf16[256,512]{1,0:T(8,128)(2,1)} %refs_4_.1) | copy-start | bytes 786436
  26.8 2.3 %copy-start.12 = (bf16[512,256]{1,0:T(8,128)(2,1)S(1)}, bf16[512,256]{1,0:T(8,128)(2,1)}, u32[]{:S(2)}) copy-start(bf16[512,256]{1,0:T(8,128)(2,1)} %refs_5_.1) | copy-start | bytes 786436
  26.8 2.3 %copy-start.14 = (bf16[256,256]{1,0:T(8,128)(2,1)S(1)}, bf16[256,256]{1,0:T(8,128)(2,1)}, u32[]{:S(2)}) copy-start(bf16[256,256]{1,0:T(8,128)(2,1)} %refs_3_.1) | copy-start | bytes 393220
  27.4 7.1 %collective-permute-start.1 = (bf16[8,64,128]{2,1,0:T(8,128)(2,1)S(1)}, bf16[8,64,128]{2,1,0:T(8,128)(2,1)S(1)}, u32[]{:S(2)}, u32[]{:S(2)}) collective-permute-start(bf16[8,64,128]{2,1,0:T(8,128)(2,1)S(1)} %shard_map.151.refs_0_), channel_id=1, source_target_pairs={{0,1},{1,0},{2,3},{3,2},{4,5},{5,4},{6,7},{7,6},{8,9},{9,8},{10,11... | collective-permute-start | bytes 393224 | tf_op jit(solution)/shard_map/ppermute | solution.py:336
  30.1 4.4 %collective-permute-start.3 = (bf16[2,128,128]{2,1,0:T(8,128)(2,1)S(1)}, bf16[2,128,128]{2,1,0:T(8,128)(2,1)S(1)}, u32[]{:S(2)}, u32[]{:S(2)}) collective-permute-start(bf16[2,128,128]{2,1,0:T(8,128)(2,1)S(1)} %get-tuple-element.23), channel_id=1, source_target_pairs={{0,1},{1,0},{2,3},{3,2},{4,5},{5,4},{6,7},{7,6},{8,9},{9,8},{10,11... | collective-permute-start | bytes 196616 | tf_op jit(solution)/shard_map/ppermute | solution.py:446
  31.7 2.8 %copy-start.5 = (bf16[128,64]{0,1:T(8,128)(2,1)S(1)}, bf16[128,64]{0,1:T(8,128)(2,1)}, u32[]{:S(2)}) copy-start(bf16[128,64]{0,1:T(8,128)(2,1)} %param.25) | copy-start | bytes 49156

commit v3 on v2

--- a/solution.py
+++ b/solution.py
@@ -111,17 +111,28 @@
         pay_ref[d, count : count + rows, :] = mine.astype(BF16)
 
 
-def proj_kernel(heads, pair_heads, *refs):
-    count = 5
-    sm_ref, v_ref, g_ref, st_ref, pv_ref, pg_ref, own_ref, lay_ref = refs[count : count + 8]
-    held = refs[count + 8 : 2 * count + 8]
-    turn_ref, rows_ref, sem = refs[2 * count + 8 :]
+def proj_kernel(cores, heads, pair_heads, *refs):
+    count = 7
+    sm_ref, v_ref, g_ref, st_ref, pv_ref, pg_ref, own_ref, lay_ref, mask_ref, share_ref = refs[
+        count : count + 10
+    ]
+    held = refs[count + 10 : 2 * count + 10]
+    turn_ref, rows_ref, sem = refs[2 * count + 10 :]
     copies = fetch(list(zip(refs[:count], held)), sem)
-    x_ref, p_ref, aw_ref, pw_ref, ow_ref = held
-    seqs, _, _ = x_ref.shape
+    x_ref, p_ref, aw_ref, pw_ref, ow_ref, bounds_ref, valid_ref = held
+    seqs, length, _ = x_ref.shape
     rows = p_ref.shape[0]
     for copy in copies:
         copy.wait()
+    first_seq = place_of(cores) * seqs
+    for s in range(seqs):
+        begin, end = span_of(bounds_ref, first_seq + s)
+        mask_ref[s : s + 1] = jnp.where(within(places((1, length), 1), begin, end), 0.0, FAR)
+    mask_ref[seqs : seqs + 1] = jnp.where(valid_ref[...] > 0, 0.0, FAR)
+    begin, end = bounds_ref[0:1].astype(F32), bounds_ref[1:2].astype(F32)
+    whole = within(places((length, 1), 0), begin, end).astype(BF16)
+    owned = within(places((rows, 1), 0) + place_of(cores) * rows, begin, end).astype(BF16)
+    share_ref[...] = 1.0 / nt(owned, whole)
     for s in range(seqs):
         xn = normed(x_ref[s]).astype(BF16)
         q = nn(xn, aw_ref[0]).astype(BF16)
@@ -131,20 +142,17 @@
         head = places(q.shape, 1) // PER_FOCUS_DIM
         for h in range(heads):
             sm_ref[s, h] = nt(jnp.where(head == h, q, jnp.zeros_like(q)), k) * SCALE
-    qv = jnp.concatenate([pw_ref[0], pw_ref[2]], axis=0)
-    kg = jnp.concatenate([pw_ref[1], pw_ref[3]], axis=0)
     width = own_ref.shape[1]
     begin = pl.multiple_of(lax.axis_index("head") * width, width)
     for i in range(rows):
         pn = normed(p_ref[i]).astype(BF16)
-        first = nt(pn, qv).astype(BF16)
-        second = nt(pn, kg)
-        pv_ref[i] = first
-        pg_ref[i] = jax.nn.sigmoid(second)
-        second = second.astype(BF16)
-        head = places(first.shape, 1) // PER_FOCUS_DIM
+        q = nt(pn, pw_ref[0]).astype(BF16)
+        k = nt(pn, pw_ref[1]).astype(BF16)
+        pv_ref[i] = nt(pw_ref[2], pn).astype(BF16)
+        pg_ref[i] = jax.nn.sigmoid(nt(pw_ref[3], pn))
+        head = places(q.shape, 1) // PER_FOCUS_DIM
         for h in range(pair_heads):
-            st_ref[i, h] = nt(jnp.where(head == h, first, jnp.zeros_like(first)), second) * SCALE
+            st_ref[i, h] = nt(jnp.where(head == h, q, jnp.zeros_like(q)), k) * SCALE
         turn_ref[...] = p_ref[i].astype(F32).T
         own_ref[i] = turn_ref[pl.ds(begin, width), :].astype(BF16)
     groups = 128 // width
@@ -172,15 +180,14 @@
                 bias_ref[h, pl.ds(begin, rows), :] = block[h * rows : (h + 1) * rows]
 
 
-def attend(scores, values, gate, offset):
+def attend(scores, values, gate):
     width = values.shape[1]
-    head = (places(values.shape, 1) - offset) // PER_FOCUS_DIM
-    inside = places(values.shape, 1) >= offset
+    head = places(values.shape, 1) // PER_FOCUS_DIM
     mixed = total = None
     for h, score in enumerate(scores):
         top = jnp.max(score, axis=-1, keepdims=True)
         weights = jnp.exp2(score - top).astype(BF16)
-        here = (head == h) & inside
+        here = head == h
         value = jnp.where(here, values, jnp.zeros_like(values))
         ones = jnp.where(here, jnp.ones_like(values), jnp.zeros_like(values))
         if width % 128 == 0:
@@ -190,61 +197,72 @@
             part, norm = nn(weights, value), nn(weights, ones)
         mixed = part if mixed is None else mixed + part
         total = norm if total is None else total + norm
-    return gate * mixed / jnp.where(total > 0, total, 1.0)
-
-
-def align_kernel(cores, rows, mine_ref, other_ref, sm_ref, v_ref, g_ref, bounds_ref, out_ref, bias_ref):
-    seqs, heads, length, _ = sm_ref.shape
+    return gate * mixed / total
+
+
+def align_kernel(cores, rows, mine_ref, other_ref, sm_ref, v_ref, g_ref, mask_ref, out_ref, bias_ref):
+    seqs, heads, _, _ = sm_ref.shape
     gather_bias(bias_ref, mine_ref, other_ref, 0, heads, rows, cores)
-    first_seq = place_of(cores) * seqs
     for s in range(seqs):
-        begin, end = span_of(bounds_ref, first_seq + s)
-        seen = within(places((1, length), 1), begin, end)
-        scores = [jnp.where(seen, sm_ref[s, h] + bias_ref[h], FAR) for h in range(heads)]
-        out_ref[s] = attend(scores, v_ref[s], g_ref[s], 0).astype(BF16)
-
-
-def tri_kernel(cores, first, mine_ref, other_ref, st_ref, v_ref, g_ref, valid_ref, out_ref, bias_ref):
-    rows, heads, _, _ = st_ref.shape
-    offset = heads * PER_FOCUS_DIM
+        mask = mask_ref[s : s + 1]
+        scores = [sm_ref[s, h] + (bias_ref[h] + mask) for h in range(heads)]
+        out_ref[s] = attend(scores, v_ref[s], g_ref[s]).astype(BF16)
+
+
+def tri_kernel(cores, first, mine_ref, other_ref, st_ref, v_ref, g_ref, mask_ref, out_ref, bias_ref):
+    rows, heads, length, _ = st_ref.shape
     gather_bias(bias_ref, mine_ref, other_ref, first, heads, rows, cores)
-    seen = valid_ref[...] > 0
+    last = mask_ref.shape[0] - 1
     for h in range(heads):
-        bias_ref[h] = jnp.where(seen, bias_ref[h], FAR)
+        bias_ref[h] = bias_ref[h] + mask_ref[last : last + 1]
+    ones = jnp.ones((8, length), BF16)
     for i in range(rows):
-        scores = [st_ref[i, h] + bias_ref[h] for h in range(heads)]
-        out = attend(scores, v_ref[i], g_ref[i], offset)
-        out_ref[i] = out.T[offset : 2 * offset].astype(BF16)
+        for h in range(heads):
+            score = st_ref[i, h] + bias_ref[h]
+            top = jnp.max(score, axis=-1, keepdims=True)
+            weights = jnp.exp2(score - top).astype(BF16)
+            at = slice(h * PER_FOCUS_DIM, (h + 1) * PER_FOCUS_DIM)
+            mixed = nt(v_ref[i, at, :], weights)
+            total = nt(ones, weights)[0:1]
+            out_ref[i, at, :] = (g_ref[i, at, :] * mixed / total).astype(BF16)
 
 
 def transition_kernel(parts, *refs):
     heads_refs = refs[:parts]
-    x_ref, wo_ref, entry_ref, exit_ref = refs[parts : parts + 4]
-    own_ref, sent_ref = refs[parts + 4 :]
+    x_ref, wo_ref = refs[parts : parts + 2]
+    entry_refs = refs[parts + 2 : 2 * parts + 2]
+    exit_refs = refs[2 * parts + 2 : 3 * parts + 2]
+    out_ref, turn_ref = refs[3 * parts + 2 :]
     seqs = x_ref.shape[0]
     features = heads_refs[0].shape[2]
+    width = out_ref.shape[2]
     here = lax.axis_index("head")
-    for s in range(seqs):
-        blended = x_ref[s].astype(F32)
+
+    def owned(value):
+        if parts == 2:
+            return jnp.where(here == 0, value[:, :width], value[:, width:])
+        turn_ref[...] = value.T
+        return turn_ref[pl.ds(pl.multiple_of(here * width, width), width), :].T
+
+    length = x_ref.shape[1]
+    for begin_row in range(0, length, 128):
+        at = slice(begin_row, begin_row + 128)
+        blended = jnp.concatenate([x_ref[s, at, :] for s in range(seqs)], axis=0).astype(F32)
         for j in range(parts):
             which = jnp.where(j == 0, here, 1 - here) if parts == 2 else j
             begin = pl.multiple_of(which * features, features)
-            blended = blended + nn(heads_refs[j][s], wo_ref[pl.ds(begin, features), :])
-        hidden = jnp.maximum(nn(normed(blended).astype(BF16), entry_ref[...]), 0.0).astype(BF16)
-        partial = nn(hidden, exit_ref[...])
-        if parts == 2:
-            half = partial.shape[1] // 2
-            own = here == 0
-            kept = jnp.where(own, partial[:, :half], partial[:, half:])
-            base = jnp.where(own, blended[:, :half], blended[:, half:])
-            own_ref[s] = base + kept
-            sent_ref[s] = jnp.where(own, partial[:, half:], partial[:, :half]).astype(BF16)
-        else:
-            own_ref[s] = blended
-            sent_ref[s] = partial.astype(BF16)
-
-
-def outer_kernel(cores, seqs, heads, mine_ref, other_ref, w_ref, bounds_ref, own_ref, out_ref, a_ref, b_ref):
+            mixed = jnp.concatenate([heads_refs[j][s, at, :] for s in range(seqs)], axis=0)
+            blended = blended + nn(mixed, wo_ref[pl.ds(begin, features), :])
+        standardized = normed(blended).astype(BF16)
+        out = owned(blended)
+        for entry_ref, exit_ref in zip(entry_refs, exit_refs):
+            hidden = jnp.maximum(nn(standardized, entry_ref[...]), 0.0).astype(BF16)
+            out = out + nn(hidden, exit_ref[...])
+        for s in range(seqs):
+            out_ref[s, at, :] = out[s * 128 : (s + 1) * 128].astype(BF16)
+
+
+def outer_kernel(cores, seqs, heads, mine_ref, other_ref, w_ref, share_ref, own_ref, out_ref, a_ref, b_ref):
     rows, width, length = out_ref.shape
     chips = mine_ref.shape[0]
     depth = w_ref.shape[0]
@@ -269,11 +287,7 @@
                 kept = jnp.where(lane_group == core * seqs + s, left, 0.0)
                 a_ref[pl.ds(row, rows, stride=total), :] = kept
     a = a_ref[...].astype(BF16)
-    begin, end = bounds_ref[0:1].astype(F32), bounds_ref[1:2].astype(F32)
-    whole = within(places((length, 1), 0), begin, end).astype(BF16)
-    owned = within(places((rows, 1), 0) + place_of(cores) * rows, begin, end).astype(BF16)
-    count = nt(owned, whole)
-    share = 1.0 / count
+    share = share_ref[...]
     gathered = [[] for _ in range(rows)]
     for step in range(steps):
         tile = jnp.concatenate([w_ref[:, step * 128 : (step + 1) * 128]] * (cores * seqs), axis=0)
@@ -294,29 +308,27 @@
 
 def close_kernel(parts, *refs):
     heads_refs = refs[:parts]
-    opm_ref, w_ref, base_ref, sum_ref, out_ref, new_ref = refs[parts:]
-    new_ref[...] = (base_ref[...] + sum_ref[...].astype(F32)).astype(BF16)
+    opm_ref, w_ref, out_ref = refs[parts:]
     rows = opm_ref.shape[0]
     features = heads_refs[0].shape[1]
     own = lax.axis_index("head") == 0
-    weights = [w_ref[:, j * features : (j + 1) * features].astype(F32) for j in range(parts)]
+    weights = [w_ref[:, j * features : (j + 1) * features] for j in range(parts)]
+    weight = w_ref[...]
     if parts == 2:
-        weights = [jnp.where(own, weights[0], weights[1]), jnp.where(own, weights[1], weights[0])]
-    weights = [w.astype(BF16) for w in weights]
+        turned = jnp.concatenate([weights[1].astype(F32), weights[0].astype(F32)], axis=1)
+        weight = jnp.where(own, weight.astype(F32), turned).astype(BF16)
     for i in range(rows):
-        out = opm_ref[i]
-        for j in range(parts):
-            out = out + nn(weights[j], heads_refs[j][i])
-        out_ref[i] = out.astype(BF16)
-
-
-def call(kernel, ins, outs, scratch=(), left=(), flops=0):
+        every = jnp.concatenate([ref[i] for ref in heads_refs], axis=0)
+        out_ref[i] = (opm_ref[i] + nn(weight, every)).astype(BF16)
+
+
+def call(kernel, ins, outs, scratch=(), left=(), grant=0, flops=0):
     size = sum(a.size * a.dtype.itemsize for a in ins) + sum(
         math.prod(s) * jnp.dtype(d).itemsize for s, d in outs
     )
     held = sum(a.inner_aval.size * 4 for a in scratch)
-    limit = min(max((size + held) * 2, 8 << 20), 60 << 20)
-    return pl.pallas_call(
+    limit = grant or min(max((size + held) * 2, 8 << 20), 60 << 20)
+    run = pl.pallas_call(
         kernel,
         compiler_params=pltpu.CompilerParams(vmem_limit_bytes=limit),
         out_shape=tuple(jax.ShapeDtypeStruct(s, d) for s, d in outs),
@@ -324,7 +336,9 @@
         out_specs=tuple(VMEM for _ in outs),
         scratch_shapes=list(scratch),
         cost_estimate=pl.CostEstimate(flops=flops, bytes_accessed=size, transcendentals=0),
-    )(*ins)
+    )
+    ins = [pltpu.with_memory_space_constraint(a, pltpu.HBM) if i in left else a for i, a in enumerate(ins)]
+    return run(*ins)
 
 
 def held_copies(arrays):
@@ -383,9 +397,23 @@
         (((chips, every_head * rows + seqs * depth + rows, length), BF16),),
         scratch=held_copies(first),
         left=range(len(first)),
+        grant=60 << 20,
     )
     mine = lax.all_to_all(payload, "rows", 0, 0, tiled=True)
     other = lax.ppermute(mine, "branch", [(0, 1), (1, 0)])
+
+    if parts == 2:
+        low, high = feedfwd_exit_weight[:, : channels // 2], feedfwd_exit_weight[:, channels // 2 :]
+        own = lax.axis_index("head") == 0
+        kept, sent = jnp.where(own, low, high), jnp.where(own, high, low)
+        entry = lax.ppermute(feedfwd_entry_weight, "head", [(0, 1), (1, 0)])
+        leave = lax.ppermute(sent, "head", [(0, 1), (1, 0)])
+        entries, exits = [feedfwd_entry_weight, entry], [kept, leave]
+    else:
+        entries = lax.all_gather(feedfwd_entry_weight, "head", axis=0)
+        exits = lax.all_to_all(feedfwd_exit_weight, "head", 1, 0, tiled=True)
+        exits = exits.reshape(parts, -1, exits.shape[1])
+        entries, exits = list(entries), list(exits)
 
     groups = 128 // width
     second = (
@@ -394,19 +422,23 @@
         alignment_projection_matrix,
         jnp.swapaxes(pair_projection_matrix, 1, 2),
         outer_product_output_matrix.T,
-    )
-    scores, values, gate, tri_scores, tri_values, tri_gate, own_pair, outer_w = call(
-        functools.partial(proj_kernel, heads, pair_heads),
+        bounds,
+        residue_valid_mask.reshape(1, -1),
+    )
+    scores, values, gate, tri_scores, tri_values, tri_gate, own_pair, outer_w, masks, shares = call(
+        functools.partial(proj_kernel, cores, heads, pair_heads),
         second,
         (
             ((seqs, heads, length, length), F32),
             ((seqs, length, features), BF16),
             ((seqs, length, features), F32),
             ((rows, pair_heads, length, length), F32),
-            ((rows, length, 2 * pair_features), BF16),
-            ((rows, length, 2 * pair_features), F32),
+            ((rows, pair_features, length), BF16),
+            ((rows, pair_features, length), F32),
             ((rows, width, length), BF16),
             ((depth, depth * width), BF16),
+            ((seqs + 1, length), F32),
+            ((rows, length), F32),
         ),
         scratch=[
             *held_copies(second)[:-1],
@@ -420,7 +452,7 @@
 
     (mixed,) = call(
         functools.partial(align_kernel, cores, rows),
-        (mine, other, scores, values, gate, bounds),
+        (mine, other, scores, values, gate, masks),
         (((seqs, length, features), BF16),),
         scratch=[pltpu.VMEM((heads, length, length), F32)],
         flops=1 << 28,
@@ -428,30 +460,25 @@
     mixed = from_heads(mixed)
     (pair_mixed,) = call(
         functools.partial(tri_kernel, cores, heads),
-        (mine, other, tri_scores, tri_values, tri_gate, residue_valid_mask.reshape(1, -1)),
+        (mine, other, tri_scores, tri_values, tri_gate, masks),
         (((rows, pair_features, length), BF16),),
         scratch=[pltpu.VMEM((pair_heads, length, length), F32)],
         flops=1 << 28,
     )
     pair_mixed = from_heads(pair_mixed)
 
-    out_channels = channels // 2 if parts == 2 else channels
-    owned, partial = call(
+    own_width = channels // parts
+    (refreshed,) = call(
         functools.partial(transition_kernel, parts),
-        (*mixed, lineup_state, lineup_readout_weight, feedfwd_entry_weight, feedfwd_exit_weight),
-        (((seqs, length, out_channels), F32), ((seqs, length, out_channels), BF16)),
+        (*mixed, lineup_state, lineup_readout_weight, *entries, *exits),
+        (((seqs, length, own_width), BF16),),
+        scratch=[pltpu.VMEM((channels, seqs * 128), F32)],
         flops=1 << 28,
     )
-    if parts == 2:
-        received = lax.ppermute(partial, "head", [(0, 1), (1, 0)])
-    else:
-        own_width = channels // parts
-        received = lax.psum_scatter(partial, "head", scatter_dimension=2, tiled=True)
-        owned = lax.dynamic_slice_in_dim(owned, lax.axis_index("head") * own_width, own_width, 2)
 
     (opm,) = call(
         functools.partial(outer_kernel, cores, seqs, every_head),
-        (mine, other, outer_w, bounds, own_pair),
+        (mine, other, outer_w, shares, own_pair),
         (((rows, width, length), F32),),
         scratch=[
             pltpu.VMEM((rows * total, depth * cores * seqs), F32),
@@ -459,10 +486,10 @@
         ],
         flops=1 << 28,
     )
-    pair_out, refreshed = call(
+    (pair_out,) = call(
         functools.partial(close_kernel, parts),
-        (*pair_mixed, opm, pair_output_matrix.T, owned, received),
-        (((rows, width, length), BF16), (owned.shape, BF16)),
+        (*pair_mixed, opm, pair_output_matrix.T),
+        (((rows, width, length), BF16),),
         flops=1 << 26,
     )
     return (refreshed, jnp.swapaxes(pair_out, 1, 2))

time: 35.8 us -> 35.3 us (0.986)
  blocking collectives: 15.9 us -> 0 us
  starting transfers between devices: 3.72 us -> 12.7 us
  waiting for transfers between devices: 2.32 us -> 10 us
  local copies, waits for them, and re-layouts: 3.98 us -> 0.02 us
  Pallas kernels: 8.82 us -> 11.5 us
    all_to_all x1 -> x0, blocking collectives: 15.9 us -> none  [local(): mine = lax.all_to_all(payload, 'rows', 0, 0, tiled=True)]
    all_to_all x0 -> x1, starting transfers between devices: none -> 7.45 us  [local(): mine = lax.all_to_all(payload, 'rows', 0, 0, tiled=True)]
    all_to_all x0 -> x1, waiting for transfers between devices: none -> 7.12 us  [local(): mine = lax.all_to_all(payload, 'rows', 0, 0, tiled=True)]
    unnamed x32 -> x10, local copies, waits for them, and re-layouts: 3.98 us -> 0.02 us
    pallas_call x7, Pallas kernels: 8.82 us -> 11.5 us  [call(): return run(*ins)]
    ppermute x2, waiting for transfers between devices: 1.06 us -> 2.92 us  [from_heads(): return [value, lax.ppermute(value, 'head', [(0, 1), (1, 0)])]]
    ppermute x1 -> x2, starting transfers between devices: 1.56 us -> 3.11 us  [the longest x1 1.56 us: local(): leave = lax.ppermute(sent, 'head', [(0, 1), (1, 0)])]
    ppermute x1 -> x2, waiting for transfers between devices: 1.25 us -> 0.01 us  [the longest x1 0.01 us: local(): entry = lax.ppermute(feedfwd_entry_weight, 'head', [(0, 1), (1, 0)])]
  transfers between devices with their start and end apart: 4 -> 6, of which waited for: 2 -> 2; matrix products, arithmetic and copies ran while one was open for 0% -> 0% of each run, Pallas kernels for 18% -> 23%
where the time goes in v3:
time: 35.3 us; the launch traced here: 35.1 us
  starting transfers between devices  12.7 us (36%)
  Pallas kernels  11.5 us (33%)
  waiting for transfers between devices  10 us (28%)
  between operations  0.72 us (2%)
    pallas_call x7, Pallas kernels, call(): return run(*ins)  11.5 us
    all_to_all x1, starting transfers between devices, local(): mine = lax.all_to_all(payload, 'rows', 0, 0, tiled=True)  7.45 us
    all_to_all x1, waiting for transfers between devices, local(): mine = lax.all_to_all(payload, 'rows', 0, 0, tiled=True)  7.12 us
    ppermute x2, waiting for transfers between devices, from_heads(): return [value, lax.ppermute(value, 'head', [(0, 1), (1, 0)])]  2.92 us
    ppermute x2, starting transfers between devices, from_heads(): return [value, lax.ppermute(value, 'head', [(0, 1), (1, 0)])]  2.16 us
    ppermute x1, starting transfers between devices, local(): leave = lax.ppermute(sent, 'head', [(0, 1), (1, 0)])  1.56 us
    ppermute x1, starting transfers between devices, local(): entry = lax.ppermute(feedfwd_entry_weight, 'head', [(0, 1), (1, 0)])  1.56 us
  transfers between devices with their start and end apart: 6, of which 2 were waited for; matrix products, arithmetic and copies ran while one was open for 0% of the time, Pallas kernels for 23%

profile of v3, /device:TPU:0, one launch (start us, length us, event | category | flops | bytes accessed | tf_op | source)
XLA Modules:
  0.0 35.1 jit_solution(18239542996581444227)
XLA Ops:
  0.6 0.0 copy-start.4
  0.6 2.5 %shard_map.149 = bf16[8,120,128]{2,1,0:T(8,128)(2,1)} custom-call(bf16[2,128,256]{2,1,0:T(8,128)(2,1)} %refs_2_.3, bf16[8,128,128]{2,1,0:T(8,128)(2,1)} %refs_1_.3, bf16[4,128]{1,0:T(4,128)(2,1)} %bitcast.12, bf16[2,128]{1,0:T(2,128)(2,1)} %bitcast.15, bf16[2,32,256]{2,1,0:T(8,128)(2,1)} %bitcast.11, s32[2,32]{1,0:T(2,128)} %bitcast.13), custom_call_target="tpu_custom_call" | custom-call | bytes 673536 | tf_op jit(solution)/shard_map/pallas_call | solution.py:341
  3.1 0.0 copy-start.1
  3.1 7.5 %all-to-all-start = ((bf16[8,120,128]{2,1,0:T(8,128)(2,1)}), bf16[8,120,128]{2,1,0:T(8,128)(2,1)S(1)}, u32[]{:S(2)}, u32[]{:S(2)}) async-start(bf16[8,120,128]{2,1,0:T(8,128)(2,1)} %shard_map.149), calls=%async_computation | async-start | bytes 491520 | tf_op jit(solution)/shard_map/all_to_all | solution.py:402
  10.6 0.0 copy-done.1
  10.6 1.6 %collective-permute-start.2 = (bf16[256,512]{1,0:T(8,128)(2,1)S(1)}, bf16[256,512]{1,0:T(8,128)(2,1)S(1)}, u32[]{:S(2)}, u32[]{:S(2)}) collective-permute-start(bf16[256,512]{1,0:T(8,128)(2,1)S(1)} %copy-done.1), channel_id=1, source_target_pairs={{0,1},{1,0},{2,3},{3,2},{4,5},{5,4},{6,7},{7,6},{8,9},{9,8},{10,11... | collective-permute-start | bytes 786440 | tf_op jit(solution)/shard_map/ppermute | solution.py:409
  12.2 7.1 %all-to-all-done.mine_ref = bf16[8,120,128]{2,1,0:T(8,128)(2,1)S(1)} async-done(((bf16[8,120,128]{2,1,0:T(8,128)(2,1)}), bf16[8,120,128]{2,1,0:T(8,128)(2,1)S(1)}, u32[]{:S(2)}, u32[]{:S(2)}) %all-to-all-start) | async-done | bytes 245792 | tf_op jit(solution)/shard_map/all_to_all | solution.py:402
  19.3 0.0 collective-permute-start
  19.3 0.0 copy-done.4
  19.3 1.6 %collective-permute-start.3 = (bf16[512,128]{1,0:T(8,128)(2,1)S(1)}, bf16[512,128]{1,0:T(8,128)(2,1)S(1)}, u32[]{:S(2)}, u32[]{:S(2)}) collective-permute-start(bf16[512,128]{1,0:T(8,128)(2,1)S(1)} %get-tuple-element.22), channel_id=1, source_target_pairs={{0,1},{1,0},{2,3},{3,2},{4,5},{5,4},{6,7},{7,6},{8,9},{9,8},{10,11... | collective-permute-start | bytes 393224 | tf_op jit(solution)/shard_map/ppermute | solution.py:410
  20.9 3.7 %shard_map.150 = (f32[2,4,128,128]{3,2,1,0:T(8,128)S(1)}, bf16[2,128,128]{2,1,0:T(8,128)(2,1)S(1)}, f32[2,128,128]{2,1,0:T(8,128)S(1)}, f32[8,2,128,128]{3,2,1,0...) custom-call(bf16[2,128,256]{2,1,0:T(8,128)(2,1)} %refs_2_.3, ...), custom_call_target="tpu_custom_call" | custom-call | flops 268435456 | bytes 3283200 | tf_op jit(solution)/shard_map/pallas_call | solution.py:341
  24.6 0.0 collective-permute-done.other_ref
  24.6 0.8 %shard_map.153.refs_0_ = bf16[8,64,128]{2,1,0:T(8,128)(2,1)S(1)} custom-call(bf16[8,120,128]{2,1,0:T(8,128)(2,1)S(1)} %all-to-all-done.mine_ref, bf16[8,120,128]{2,1,0:T(8,128)(2,1)S(1)} %collective-permute-done.other_ref, f32[8,2,128,128]{3,2,1,0:T(8,128)S(1)} %get-tuple-element.16.st_ref, bf16[8,64,128]{2,1,0:T(8,128)(2,1)S(1)} %get-tuple-element.17.v_ref, ...), custom_call_target="tpu_custom_call" | custom-call | flops 268435456 | bytes 2065920 | tf_op jit(solution)/shard_map/pallas_call | solution.py:341
  25.4 0.6 %collective-permute-start.4 = (bf16[8,64,128]{2,1,0:T(8,128)(2,1)S(1)}, bf16[8,64,128]{2,1,0:T(8,128)(2,1)S(1)}, u32[]{:S(2)}, u32[]{:S(2)}) collective-permute-start(bf16[8,64,128]{2,1,0:T(8,128)(2,1)S(1)} %shard_map.153.refs_0_), channel_id=1, source_target_pairs={{0,1},{1,0},{2,3},{3,2},{4,5},{5,4},{6,7},{7,6},{8,9},{9,8},{10,11... | collective-permute-start | bytes 393224 | tf_op jit(solution)/shard_map/ppermute | solution.py:350
  26.0 0.4 %shard_map.151.refs_0_ = bf16[2,128,128]{2,1,0:T(8,128)(2,1)S(1)} custom-call(bf16[8,120,128]{2,1,0:T(8,128)(2,1)S(1)} %all-to-all-done.mine_ref, bf16[8,120,128]{2,1,0:T(8,128)(2,1)S(1)} %collective-permute-done.other_ref, f32[2,4,128,128]{3,2,1,0:T(8,128)S(1)} %get-tuple-element.12.sm_ref, bf16[2,128,128]{2,1,0:T(8,128)(2,1)S(1)} %get-tuple-element.13.v_ref, ...), custom_call_target="tpu_custom_call" | custom-call | flops 268435456 | bytes 1279488 | tf_op jit(solution)/shard_map/pallas_call | solution.py:341
  26.4 1.6 %collective-permute-start.1 = (bf16[2,128,128]{2,1,0:T(8,128)(2,1)S(1)}, bf16[2,128,128]{2,1,0:T(8,128)(2,1)S(1)}, u32[]{:S(2)}, u32[]{:S(2)}) collective-permute-start(bf16[2,128,128]{2,1,0:T(8,128)(2,1)S(1)} %shard_map.151.refs_0_), channel_id=1, source_target_pairs={{0,1},{1,0},{2,3},{3,2},{4,5},{5,4},{6,7},{7,6},{8,9},{9,8},{10,11... | collective-permute-start | bytes 196616 | tf_op jit(solution)/shard_map/ppermute | solution.py:350
  28.0 0.0 copy-start
  28.0 0.0 copy-start.2
  28.0 1.6 %shard_map.154.refs_2_ = f32[8,64,128]{2,1,0:T(8,128)S(1)} custom-call(bf16[8,120,128]{2,1,0:T(8,128)(2,1)S(1)} %all-to-all-done.mine_ref, bf16[8,120,128]{2,1,0:T(8,128)(2,1)S(1)} %collective-permute-done.other_ref, bf16[32,2048]{1,0:T(8,128)(2,1)S(1)} %get-tuple-element.19.w_ref, f32[8,128]{1,0:T(8,128)S(1)} %get-tuple-element.20.share_ref, ...), custom_call_target="tpu_custom_call" | custom-call | flops 268435456 | bytes 1019904 | tf_op jit(solution)/shard_map/pallas_call | solution.py:341
  29.6 0.0 collective-permute-done.3.refs_7_
  29.6 0.0 collective-permute-done.2.refs_5_
  29.6 2.9 %collective-permute-done.1.refs_1_ = bf16[2,128,128]{2,1,0:T(8,128)(2,1)S(1)} collective-permute-done((bf16[2,128,128]{2,1,0:T(8,128)(2,1)S(1)}, bf16[2,128,128]{2,1,0:T(8,128)(2,1)S(1)}, u32[]{:S(2)}, u32[]{:S(2)}) %collective-permute-start.1) | collective-permute-done | bytes 65568 | tf_op jit(solution)/shard_map/ppermute | solution.py:350
  32.5 0.0 copy-done
  32.5 0.0 copy-done.2
  32.5 0.0 copy-start.3
  32.5 1.6 %shard_map.152 = bf16[2,128,128]{2,1,0:T(8,128)(2,1)} custom-call(bf16[2,128,128]{2,1,0:T(8,128)(2,1)S(1)} %shard_map.151.refs_0_, bf16[2,128,128]{2,1,0:T(8,128)(2,1)S(1)} %collective-permute-done.1.refs_1_, bf16[2,128,256]{2,1,0:T(8,128)(2,1)S(1)} %copy-done, bf16[256,256]{1,0:T(8,128)(2,1)S(1)} %copy-done.2, bf16[256,512]{1,0:T(8,128)(2,1)S(1)} %copy-done.1, ...), custom_call_target="tpu_custom_call" | custom-call | flops 268435456 | bytes 1245184 | tf_op jit(solution)/shard_map/pallas_call | solution.py:341
  34.1 0.0 collective-permute-done.4.refs_1_
  34.1 0.0 copy-done.3
  34.1 0.9 %shard_map.155 = bf16[8,64,128]{2,1,0:T(8,128)(2,1)} custom-call(bf16[8,64,128]{2,1,0:T(8,128)(2,1)S(1)} %shard_map.153.refs_0_, bf16[8,64,128]{2,1,0:T(8,128)(2,1)S(1)} %collective-permute-done.4.refs_1_, f32[8,64,128]{2,1,0:T(8,128)S(1)} %shard_map.154.refs_2_, bf16[64,128]{1,0:T(8,128)(2,1)S(1)} %bitcast.9), custom_call_target="tpu_custom_call" | custom-call | flops 67108864 | bytes 671744 | tf_op jit(solution)/shard_map/pallas_call | solution.py:341
  (1 shorter events, 0.0 us)
Async XLA Ops:
  0.6 18.7 %copy-start.4 = (bf16[512,256]{1,0:T(8,128)(2,1)S(1)}, bf16[512,256]{1,0:T(8,128)(2,1)}, u32[]{:S(2)}) copy-start(bf16[512,256]{1,0:T(8,128)(2,1)} %param.23) | copy-start | bytes 786436
  3.1 7.5 %copy-start.1 = (bf16[256,512]{1,0:T(8,128)(2,1)S(1)}, bf16[256,512]{1,0:T(8,128)(2,1)}, u32[]{:S(2)}) copy-start(bf16[256,512]{1,0:T(8,128)(2,1)} %refs_4_.1) | copy-start | bytes 786436
  3.1 16.1 %all-to-all-start = ((bf16[8,120,128]{2,1,0:T(8,128)(2,1)}), bf16[8,120,128]{2,1,0:T(8,128)(2,1)S(1)}, u32[]{:S(2)}, u32[]{:S(2)}) async-start(bf16[8,120,128]{2,1,0:T(8,128)(2,1)} %shard_map.149), calls=%async_computation | async-start | bytes 491520 | tf_op jit(solution)/shard_map/all_to_all | solution.py:402
  10.6 19.0 %collective-permute-start.2 = (bf16[256,512]{1,0:T(8,128)(2,1)S(1)}, bf16[256,512]{1,0:T(8,128)(2,1)S(1)}, u32[]{:S(2)}, u32[]{:S(2)}) collective-permute-start(bf16[256,512]{1,0:T(8,128)(2,1)S(1)} %copy-done.1), channel_id=1, source_target_pairs={{0,1},{1,0},{2,3},{3,2},{4,5},{5,4},{6,7},{7,6},{8,9},{9,8},{10,11... | collective-permute-start | bytes 786440 | tf_op jit(solution)/shard_map/ppermute | solution.py:409
  19.3 5.3 %collective-permute-start = (bf16[8,120,128]{2,1,0:T(8,128)(2,1)S(1)}, bf16[8,120,128]{2,1,0:T(8,128)(2,1)S(1)}, u32[]{:S(2)}, u32[]{:S(2)}) collective-permute-start(bf16[8,120,128]{2,1,0:T(8,128)(2,1)S(1)} %all-to-all-done.mine_ref), channel_id=1, source_target_pairs={{0,2},{2,0},{1,3},{3,1},{4,6},{6,4},{5,7},{7,5},{8,10},{10,8},{9,1... | collective-permute-start | bytes 737288 | tf_op jit(solution)/shard_map/ppermute | solution.py:403
  19.3 10.3 %collective-permute-start.3 = (bf16[512,128]{1,0:T(8,128)(2,1)S(1)}, bf16[512,128]{1,0:T(8,128)(2,1)S(1)}, u32[]{:S(2)}, u32[]{:S(2)}) collective-permute-start(bf16[512,128]{1,0:T(8,128)(2,1)S(1)} %get-tuple-element.22), channel_id=1, source_target_pairs={{0,1},{1,0},{2,3},{3,2},{4,5},{5,4},{6,7},{7,6},{8,9},{9,8},{10,11... | collective-permute-start | bytes 393224 | tf_op jit(solution)/shard_map/ppermute | solution.py:410
  25.4 8.7 %collective-permute-start.4 = (bf16[8,64,128]{2,1,0:T(8,128)(2,1)S(1)}, bf16[8,64,128]{2,1,0:T(8,128)(2,1)S(1)}, u32[]{:S(2)}, u32[]{:S(2)}) collective-permute-start(bf16[8,64,128]{2,1,0:T(8,128)(2,1)S(1)} %shard_map.153.refs_0_), channel_id=1, source_target_pairs={{0,1},{1,0},{2,3},{3,2},{4,5},{5,4},{6,7},{7,6},{8,9},{9,8},{10,11... | collective-permute-start | bytes 393224 | tf_op jit(solution)/shard_map/ppermute | solution.py:350
  26.4 6.1 %collective-permute-start.1 = (bf16[2,128,128]{2,1,0:T(8,128)(2,1)S(1)}, bf16[2,128,128]{2,1,0:T(8,128)(2,1)S(1)}, u32[]{:S(2)}, u32[]{:S(2)}) collective-permute-start(bf16[2,128,128]{2,1,0:T(8,128)(2,1)S(1)} %shard_map.151.refs_0_), channel_id=1, source_target_pairs={{0,1},{1,0},{2,3},{3,2},{4,5},{5,4},{6,7},{7,6},{8,9},{9,8},{10,11... | collective-permute-start | bytes 196616 | tf_op jit(solution)/shard_map/ppermute | solution.py:350
  28.0 4.5 %copy-start = (bf16[2,128,256]{2,1,0:T(8,128)(2,1)S(1)}, bf16[2,128,256]{2,1,0:T(8,128)(2,1)}, u32[]{:S(2)}) copy-start(bf16[2,128,256]{2,1,0:T(8,128)(2,1)} %refs_2_.3) | copy-start | bytes 393220
  28.0 4.5 %copy-start.2 = (bf16[256,256]{1,0:T(8,128)(2,1)S(1)}, bf16[256,256]{1,0:T(8,128)(2,1)}, u32[]{:S(2)}) copy-start(bf16[256,256]{1,0:T(8,128)(2,1)} %refs_3_.1) | copy-start | bytes 393220
  32.5 1.6 %copy-start.3 = (bf16[128,64]{0,1:T(8,128)(2,1)S(1)}, bf16[128,64]{0,1:T(8,128)(2,1)}, u32[]{:S(2)}) copy-start(bf16[128,64]{0,1:T(8,128)(2,1)} %param.25) | copy-start | bytes 49156

commit v4 on v3

--- a/solution.py
+++ b/solution.py
@@ -62,27 +62,34 @@
     return copies
 
 
+def pack_kernel(entry_ref, exit_ref, out_ref, held_ref, sem):
+    units = held_ref.shape[0]
+    width = held_ref.shape[1] - units
+    first = pl.multiple_of(lax.axis_index("branch") * units, units)
+    begin = pl.multiple_of((1 - lax.axis_index("head")) * width, width)
+    pairs = [
+        (entry_ref.at[:, pl.ds(first, units)], held_ref.at[:, pl.ds(0, units)]),
+        (exit_ref.at[pl.ds(first, units), pl.ds(begin, width)], held_ref.at[:, pl.ds(units, width)]),
+    ]
+    for copy in fetch(pairs, sem):
+        copy.wait()
+    copy = pltpu.make_async_copy(held_ref, out_ref, sem.at[0])
+    copy.start()
+    copy.wait()
+
+
 def pre_kernel(cores, *refs):
-    pay_ref, sem = refs[6], refs[13]
-    copies = fetch(list(zip(refs[:6], refs[7:13])), sem)
-    x_ref, p_ref, mb_ref, tb_ref, lr_ref, bounds_ref = refs[7:13]
+    pay_ref, held, (bias_ref, factor_ref, in_sem, out_sem) = refs[6], refs[7:13], refs[13:]
+    copies = fetch(list(zip(refs[:6], held)), in_sem)
+    x_ref, p_ref, mb_ref, tb_ref, lr_ref, bounds_ref = held
     seqs, length, _ = x_ref.shape
     rows = p_ref.shape[0]
     chips = pay_ref.shape[0]
-    for copy in copies:
-        copy.wait()
-    bias_w = jnp.concatenate([mb_ref[...].astype(F32), tb_ref[...].astype(F32)], axis=0)
-    bias_w = bias_w.astype(BF16)
-    heads = bias_w.shape[0]
     depth = lr_ref.shape[1]
     first_seq = place_of(cores) * seqs
+    for j in (0, 4, 5):
+        copies[j].wait()
     pieces = []
-    biases = []
-    for i in range(rows):
-        pn = normed(p_ref[i]).astype(BF16)
-        biases.append(nt(bias_w, pn))
-    for h in range(heads):
-        pieces.append(jnp.concatenate([b[h : h + 1] for b in biases], axis=0))
     left = None
     zero = jnp.zeros(lr_ref.shape[1:], BF16)
     for s in range(seqs):
@@ -96,19 +103,35 @@
         )
         term = nt(xn, weight) * within(places((length, 1), 0), begin, end).astype(F32)
         left = term if left is None else left + term
-    width = left.shape[1]
-    group = places((rows, width), 1) // (seqs * depth)
-    copied = jnp.concatenate(pieces, axis=0).astype(BF16)
-    count = copied.shape[0]
+    right = jnp.concatenate(pieces, axis=0).astype(BF16)
+    lanes = left.shape[1]
+    group = places((rows, lanes), 1) // (seqs * depth)
+    first, count = bias_ref.shape[1], right.shape[0]
     for d in range(chips):
-        pay_ref[d, 0:count, :] = copied
         mine = left[d * cores * rows : d * cores * rows + rows]
         for c in range(1, cores):
             begin = (d * cores + c) * rows
             mine = jnp.where(group == c, left[begin : begin + rows], mine)
-        if width < length:
-            mine = jnp.concatenate([mine, jnp.zeros((rows, length - width), F32)], axis=1)
-        pay_ref[d, count : count + rows, :] = mine.astype(BF16)
+        if lanes < length:
+            mine = jnp.concatenate([mine, jnp.zeros((rows, length - lanes), F32)], axis=1)
+        factor_ref[d, 0:count, :] = right
+        factor_ref[d, count : count + rows, :] = mine.astype(BF16)
+    sends = [pltpu.make_async_copy(factor_ref, pay_ref.at[:, first:], out_sem.at[0])]
+    sends[0].start()
+    for j in (1, 2, 3):
+        copies[j].wait()
+    bias_w = jnp.concatenate([mb_ref[...].astype(F32), tb_ref[...].astype(F32)], axis=0)
+    bias_w = bias_w.astype(BF16)
+    heads = bias_w.shape[0]
+    biases = [nt(bias_w, normed(p_ref[i]).astype(BF16)) for i in range(rows)]
+    pieces = [jnp.concatenate([b[h : h + 1] for b in biases], axis=0) for h in range(heads)]
+    bias = jnp.concatenate(pieces, axis=0).astype(BF16)
+    for d in range(chips):
+        bias_ref[d] = bias
+    sends.append(pltpu.make_async_copy(bias_ref, pay_ref.at[:, 0:first], out_sem.at[1]))
+    sends[1].start()
+    for copy in sends:
+        copy.wait()
 
 
 def proj_kernel(cores, heads, pair_heads, *refs):
@@ -211,8 +234,8 @@
 
 def tri_kernel(cores, first, mine_ref, other_ref, st_ref, v_ref, g_ref, mask_ref, out_ref, bias_ref):
     rows, heads, length, _ = st_ref.shape
+    last = mask_ref.shape[0] - 1
     gather_bias(bias_ref, mine_ref, other_ref, first, heads, rows, cores)
-    last = mask_ref.shape[0] - 1
     for h in range(heads):
         bias_ref[h] = bias_ref[h] + mask_ref[last : last + 1]
     ones = jnp.ones((8, length), BF16)
@@ -227,12 +250,13 @@
             out_ref[i, at, :] = (g_ref[i, at, :] * mixed / total).astype(BF16)
 
 
-def transition_kernel(parts, *refs):
+def transition_kernel(parts, own_only, *refs):
     heads_refs = refs[:parts]
     x_ref, wo_ref = refs[parts : parts + 2]
-    entry_refs = refs[parts + 2 : 2 * parts + 2]
-    exit_refs = refs[2 * parts + 2 : 3 * parts + 2]
-    out_ref, turn_ref = refs[3 * parts + 2 :]
+    count = 1 if own_only else parts
+    entry_refs = refs[parts + 2 : parts + 2 + count]
+    exit_refs = refs[parts + 2 + count : parts + 2 + 2 * count]
+    out_ref, turn_ref = refs[-2:]
     seqs = x_ref.shape[0]
     features = heads_refs[0].shape[2]
     width = out_ref.shape[2]
@@ -244,6 +268,14 @@
         turn_ref[...] = value.T
         return turn_ref[pl.ds(pl.multiple_of(here * width, width), width), :].T
 
+    if own_only:
+        begin = pl.multiple_of(here * width, width)
+        weights = [(entry_refs[0][...], exit_refs[0][:, pl.ds(begin, width)])]
+        for ref in refs[-4:-2]:
+            units = ref.shape[0]
+            weights.append((ref[:, :units], ref[:, units:]))
+    else:
+        weights = [(entry[...], leave[...]) for entry, leave in zip(entry_refs, exit_refs)]
     length = x_ref.shape[1]
     for begin_row in range(0, length, 128):
         at = slice(begin_row, begin_row + 128)
@@ -255,9 +287,9 @@
             blended = blended + nn(mixed, wo_ref[pl.ds(begin, features), :])
         standardized = normed(blended).astype(BF16)
         out = owned(blended)
-        for entry_ref, exit_ref in zip(entry_refs, exit_refs):
-            hidden = jnp.maximum(nn(standardized, entry_ref[...]), 0.0).astype(BF16)
-            out = out + nn(hidden, exit_ref[...])
+        for enter, leave in weights:
+            value = jnp.maximum(nn(standardized, enter), 0.0).astype(BF16)
+            out = out + nn(value, leave)
         for s in range(seqs):
             out_ref[s, at, :] = out[s * 128 : (s + 1) * 128].astype(BF16)
 
@@ -308,32 +340,40 @@
 
 def close_kernel(parts, *refs):
     heads_refs = refs[:parts]
-    opm_ref, w_ref, out_ref = refs[parts:]
+    opm_ref, w_ref, fresh_ref, out_ref, copy_ref, stage_ref, sem = refs[parts:]
+    copies = [
+        pltpu.make_async_copy(fresh_ref, copy_ref, sem.at[0]),
+        pltpu.make_async_copy(stage_ref, out_ref, sem.at[1]),
+    ]
+    copies[0].start()
     rows = opm_ref.shape[0]
     features = heads_refs[0].shape[1]
     own = lax.axis_index("head") == 0
-    weights = [w_ref[:, j * features : (j + 1) * features] for j in range(parts)]
     weight = w_ref[...]
     if parts == 2:
-        turned = jnp.concatenate([weights[1].astype(F32), weights[0].astype(F32)], axis=1)
+        first, second = weight[:, :features].astype(F32), weight[:, features:].astype(F32)
+        turned = jnp.concatenate([second, first], axis=1)
         weight = jnp.where(own, weight.astype(F32), turned).astype(BF16)
     for i in range(rows):
         every = jnp.concatenate([ref[i] for ref in heads_refs], axis=0)
-        out_ref[i] = (opm_ref[i] + nn(weight, every)).astype(BF16)
-
-
-def call(kernel, ins, outs, scratch=(), left=(), grant=0, flops=0):
+        stage_ref[i] = (opm_ref[i] + nn(weight, every)).astype(BF16)
+    copies[1].start()
+    for copy in copies:
+        copy.wait()
+
+
+def call(kernel, ins, outs, scratch=(), left=(), written=(), grant=0, flops=0):
     size = sum(a.size * a.dtype.itemsize for a in ins) + sum(
         math.prod(s) * jnp.dtype(d).itemsize for s, d in outs
     )
-    held = sum(a.inner_aval.size * 4 for a in scratch)
+    held = sum(a.inner_aval.size * 4 for a in scratch )
     limit = grant or min(max((size + held) * 2, 8 << 20), 60 << 20)
     run = pl.pallas_call(
         kernel,
         compiler_params=pltpu.CompilerParams(vmem_limit_bytes=limit),
         out_shape=tuple(jax.ShapeDtypeStruct(s, d) for s, d in outs),
         in_specs=[HBM if i in left else VMEM for i in range(len(ins))],
-        out_specs=tuple(VMEM for _ in outs),
+        out_specs=tuple(HBM if i in written else VMEM for i in range(len(outs))),
         scratch_shapes=list(scratch),
         cost_estimate=pl.CostEstimate(flops=flops, bytes_accessed=size, transcendentals=0),
     )
@@ -391,29 +431,46 @@
         jnp.swapaxes(left_right_maps, 1, 2),
         bounds,
     )
+    bias_rows = every_head * rows
+    right_rows = seqs * depth
+    hidden = feedfwd_entry_weight.shape[1]
     (payload,) = call(
         functools.partial(pre_kernel, cores),
         first,
-        (((chips, every_head * rows + seqs * depth + rows, length), BF16),),
-        scratch=held_copies(first),
+        (((chips, bias_rows + right_rows + rows, length), BF16),),
+        scratch=[
+            *held_copies(first)[:-1],
+            pltpu.VMEM((chips, bias_rows, length), BF16),
+            pltpu.VMEM((chips, right_rows + rows, length), BF16),
+            held_copies(first)[-1],
+            pltpu.SemaphoreType.DMA((2,)),
+        ],
         left=range(len(first)),
+        written=(0,),
         grant=60 << 20,
     )
     mine = lax.all_to_all(payload, "rows", 0, 0, tiled=True)
     other = lax.ppermute(mine, "branch", [(0, 1), (1, 0)])
 
-    if parts == 2:
-        low, high = feedfwd_exit_weight[:, : channels // 2], feedfwd_exit_weight[:, channels // 2 :]
-        own = lax.axis_index("head") == 0
-        kept, sent = jnp.where(own, low, high), jnp.where(own, high, low)
-        entry = lax.ppermute(feedfwd_entry_weight, "head", [(0, 1), (1, 0)])
-        leave = lax.ppermute(sent, "head", [(0, 1), (1, 0)])
-        entries, exits = [feedfwd_entry_weight, entry], [kept, leave]
+    if parts == 2 and cores == 2 and hidden == cores * channels:
+        shape = (channels, hidden // cores + channels // parts)
+        (packed,) = call(
+            pack_kernel,
+            (feedfwd_entry_weight, feedfwd_exit_weight),
+            ((shape, BF16),),
+            scratch=[pltpu.VMEM(shape, BF16), pltpu.SemaphoreType.DMA((2,))],
+            left=(0, 1),
+            written=(0,),
+            flops=1 << 28,
+        )
+        others = [lax.ppermute(packed, "head", [(0, 1), (1, 0)])]
+        others.append(lax.ppermute(others[0], "branch", [(0, 1), (1, 0)]))
+        entries, exits = [feedfwd_entry_weight], [feedfwd_exit_weight]
     else:
         entries = lax.all_gather(feedfwd_entry_weight, "head", axis=0)
         exits = lax.all_to_all(feedfwd_exit_weight, "head", 1, 0, tiled=True)
         exits = exits.reshape(parts, -1, exits.shape[1])
-        entries, exits = list(entries), list(exits)
+        entries, exits, others = list(entries), list(exits), []
 
     groups = 128 // width
     second = (
@@ -468,9 +525,9 @@
     pair_mixed = from_heads(pair_mixed)
 
     own_width = channels // parts
-    (refreshed,) = call(
-        functools.partial(transition_kernel, parts),
-        (*mixed, lineup_state, lineup_readout_weight, *entries, *exits),
+    (fresh,) = call(
+        functools.partial(transition_kernel, parts, bool(others)),
+        (*mixed, lineup_state, lineup_readout_weight, *entries, *exits, *others),
         (((seqs, length, own_width), BF16),),
         scratch=[pltpu.VMEM((channels, seqs * 128), F32)],
         flops=1 << 28,
@@ -486,10 +543,12 @@
         ],
         flops=1 << 28,
     )
-    (pair_out,) = call(
+    pair_out, refreshed = call(
         functools.partial(close_kernel, parts),
-        (*pair_mixed, opm, pair_output_matrix.T),
-        (((rows, width, length), BF16),),
+        (*pair_mixed, opm, pair_output_matrix.T, fresh),
+        (((rows, width, length), BF16), (fresh.shape, BF16)),
+        scratch=[pltpu.VMEM((rows, width, length), BF16), pltpu.SemaphoreType.DMA((2,))],
+        written=(0, 1),
         flops=1 << 26,
     )
     return (refreshed, jnp.swapaxes(pair_out, 1, 2))

time: 35.3 us -> 33.4 us (0.946)
  waiting for transfers between devices: 10 us -> 8.66 us
  starting transfers between devices: 12.7 us -> 11.5 us
  Pallas kernels: 11.5 us -> 12.2 us
    all_to_all x1, waiting for transfers between devices: 7.12 us -> 5.97 us  [local(): mine = lax.all_to_all(payload, 'rows', 0, 0, tiled=True)]
    ppermute x2, starting transfers between devices: 3.11 us -> 2.06 us  [the longest x1 1.56 us: local(): others = [lax.ppermute(packed, 'head', [(0, 1), (1, 0)])]]
    pallas_call x7 -> x8, Pallas kernels: 11.5 us -> 12.2 us  [call(): return run(*ins)]
  transfers between devices with their start and end apart: 6 -> 6, of which waited for: 2 -> 2; matrix products, arithmetic and copies ran while one was open for 0% -> 0% of each run, Pallas kernels for 23% -> 26%
where the time goes in v4:
time: 33.4 us; the launch traced here: 33.1 us
  Pallas kernels  12.2 us (37%)
  starting transfers between devices  11.5 us (34%)
  waiting for transfers between devices  8.66 us (26%)
  between operations  0.74 us (2%)
    pallas_call x8, Pallas kernels, call(): return run(*ins)  12.2 us
    all_to_all x1, starting transfers between devices, local(): mine = lax.all_to_all(payload, 'rows', 0, 0, tiled=True)  7.32 us
    all_to_all x1, waiting for transfers between devices, local(): mine = lax.all_to_all(payload, 'rows', 0, 0, tiled=True)  5.97 us
    ppermute x2, waiting for transfers between devices, from_heads(): return [value, lax.ppermute(value, 'head', [(0, 1), (1, 0)])]  2.68 us
    ppermute x2, starting transfers between devices, from_heads(): return [value, lax.ppermute(value, 'head', [(0, 1), (1, 0)])]  2.15 us
    ppermute x1, starting transfers between devices, local(): others = [lax.ppermute(packed, 'head', [(0, 1), (1, 0)])]  1.56 us
  transfers between devices with their start and end apart: 6, of which 2 were waited for; matrix products, arithmetic and copies ran while one was open for 0% of the time, Pallas kernels for 26%

profile of v4, /device:TPU:0, one launch (start us, length us, event | category | flops | bytes accessed | tf_op | source)
XLA Modules:
  0.0 33.1 jit_solution(10127491888140481812)
XLA Ops:
  0.6 2.6 %shard_map.149 = bf16[8,120,128]{2,1,0:T(8,128)(2,1)} custom-call(bf16[2,128,256]{2,1,0:T(8,128)(2,1)} %refs_2_.3, bf16[8,128,128]{2,1,0:T(8,128)(2,1)} %refs_1_.3, bf16[4,128]{1,0:T(4,128)(2,1)} %bitcast.11, bf16[2,128]{1,0:T(2,128)(2,1)} %bitcast.14, bf16[2,32,256]{2,1,0:T(8,128)(2,1)} %bitcast.10, s32[2,32]{1,0:T(2,128)} %bitcast.12), custom_call_target="tpu_custom_call" | custom-call | bytes 673536 | tf_op jit(solution)/shard_map/pallas_call | solution.py:381
  3.2 7.3 %all-to-all-start = ((bf16[8,120,128]{2,1,0:T(8,128)(2,1)}), bf16[8,120,128]{2,1,0:T(8,128)(2,1)S(1)}, u32[]{:S(2)}, u32[]{:S(2)}) async-start(bf16[8,120,128]{2,1,0:T(8,128)(2,1)} %shard_map.149), calls=%async_computation | async-start | bytes 491520 | tf_op jit(solution)/shard_map/all_to_all | solution.py:452
  10.6 1.1 %shard_map.154 = bf16[256,384]{1,0:T(8,128)(2,1)S(1)} custom-call(bf16[256,512]{1,0:T(8,128)(2,1)} %refs_4_.1, bf16[512,256]{1,0:T(8,128)(2,1)} %refs_5_.1), custom_call_target="tpu_custom_call" | custom-call | flops 268435456 | bytes 720896 | tf_op jit(solution)/shard_map/pallas_call | solution.py:381
  11.7 1.6 %collective-permute-start.3 = (bf16[256,384]{1,0:T(8,128)(2,1)S(1)}, bf16[256,384]{1,0:T(8,128)(2,1)S(1)}, u32[]{:S(2)}, u32[]{:S(2)}) collective-permute-start(bf16[256,384]{1,0:T(8,128)(2,1)S(1)} %shard_map.154), channel_id=1, source_target_pairs={{0,1},{1,0},{2,3},{3,2},{4,5},{5,4},{6,7},{7,6},{8,9},{9,8},{10,11... | collective-permute-start | bytes 589832 | tf_op jit(solution)/shard_map/ppermute | solution.py:466
  13.3 6.0 %all-to-all-done.mine_ref = bf16[8,120,128]{2,1,0:T(8,128)(2,1)S(1)} async-done(((bf16[8,120,128]{2,1,0:T(8,128)(2,1)}), bf16[8,120,128]{2,1,0:T(8,128)(2,1)S(1)}, u32[]{:S(2)}, u32[]{:S(2)}) %all-to-all-start) | async-done | bytes 245792 | tf_op jit(solution)/shard_map/all_to_all | solution.py:452
  19.2 0.0 collective-permute-start
  19.2 0.0 collective-permute-done.3.refs_6_
  19.2 0.5 %collective-permute-start.4 = (bf16[256,384]{1,0:T(8,128)(2,1)S(1)}, bf16[256,384]{1,0:T(8,128)(2,1)S(1)}, u32[]{:S(2)}, u32[]{:S(2)}) collective-permute-start(bf16[256,384]{1,0:T(8,128)(2,1)S(1)} %collective-permute-done.3.refs_6_), channel_id=1, source_target_pairs={{0,2},{2,0},{1,3},{3,1},{4,6},{6,4},{5,7},{7,5},{8,10},{10,8},{9,1... | collective-permute-start | bytes 589832 | tf_op jit(solution)/shard_map/ppermute | solution.py:467
  19.7 3.7 %shard_map.150 = (f32[2,4,128,128]{3,2,1,0:T(8,128)S(1)}, bf16[2,128,128]{2,1,0:T(8,128)(2,1)S(1)}, f32[2,128,128]{2,1,0:T(8,128)S(1)}, f32[8,2,128,128]{3,2,1,0...) custom-call(bf16[2,128,256]{2,1,0:T(8,128)(2,1)} %refs_2_.3, ...), custom_call_target="tpu_custom_call" | custom-call | flops 268435456 | bytes 3283200 | tf_op jit(solution)/shard_map/pallas_call | solution.py:381
  23.5 0.0 collective-permute-done.other_ref
  23.5 0.8 %shard_map.151.refs_0_ = bf16[8,64,128]{2,1,0:T(8,128)(2,1)S(1)} custom-call(bf16[8,120,128]{2,1,0:T(8,128)(2,1)S(1)} %all-to-all-done.mine_ref, bf16[8,120,128]{2,1,0:T(8,128)(2,1)S(1)} %collective-permute-done.other_ref, f32[8,2,128,128]{3,2,1,0:T(8,128)S(1)} %get-tuple-element.14.st_ref, bf16[8,64,128]{2,1,0:T(8,128)(2,1)S(1)} %get-tuple-element.15.v_ref, ...), custom_call_target="tpu_custom_call" | custom-call | flops 268435456 | bytes 2065920 | tf_op jit(solution)/shard_map/pallas_call | solution.py:381
  24.3 1.6 %collective-permute-start.1 = (bf16[8,64,128]{2,1,0:T(8,128)(2,1)S(1)}, bf16[8,64,128]{2,1,0:T(8,128)(2,1)S(1)}, u32[]{:S(2)}, u32[]{:S(2)}) collective-permute-start(bf16[8,64,128]{2,1,0:T(8,128)(2,1)S(1)} %shard_map.151.refs_0_), channel_id=1, source_target_pairs={{0,1},{1,0},{2,3},{3,2},{4,5},{5,4},{6,7},{7,6},{8,9},{9,8},{10,11... | collective-permute-start | bytes 393224 | tf_op jit(solution)/shard_map/ppermute | solution.py:390
  25.8 0.4 %shard_map.153.refs_0_ = bf16[2,128,128]{2,1,0:T(8,128)(2,1)S(1)} custom-call(bf16[8,120,128]{2,1,0:T(8,128)(2,1)S(1)} %all-to-all-done.mine_ref, bf16[8,120,128]{2,1,0:T(8,128)(2,1)S(1)} %collective-permute-done.other_ref, f32[2,4,128,128]{3,2,1,0:T(8,128)S(1)} %get-tuple-element.21.sm_ref, bf16[2,128,128]{2,1,0:T(8,128)(2,1)S(1)} %get-tuple-element.22.v_ref, ...), custom_call_target="tpu_custom_call" | custom-call | flops 268435456 | bytes 1279488 | tf_op jit(solution)/shard_map/pallas_call | solution.py:381
  26.2 0.6 %collective-permute-start.2 = (bf16[2,128,128]{2,1,0:T(8,128)(2,1)S(1)}, bf16[2,128,128]{2,1,0:T(8,128)(2,1)S(1)}, u32[]{:S(2)}, u32[]{:S(2)}) collective-permute-start(bf16[2,128,128]{2,1,0:T(8,128)(2,1)S(1)} %shard_map.153.refs_0_), channel_id=1, source_target_pairs={{0,1},{1,0},{2,3},{3,2},{4,5},{5,4},{6,7},{7,6},{8,9},{9,8},{10,11... | collective-permute-start | bytes 196616 | tf_op jit(solution)/shard_map/ppermute | solution.py:390
  26.8 0.0 copy-start
  26.8 0.0 copy-start.1
  26.9 0.0 copy-start.2
  26.9 0.0 copy-start.3
  26.9 1.6 %shard_map.152.refs_2_ = f32[8,64,128]{2,1,0:T(8,128)S(1)} custom-call(bf16[8,120,128]{2,1,0:T(8,128)(2,1)S(1)} %all-to-all-done.mine_ref, bf16[8,120,128]{2,1,0:T(8,128)(2,1)S(1)} %collective-permute-done.other_ref, bf16[32,2048]{1,0:T(8,128)(2,1)S(1)} %get-tuple-element.18.w_ref, f32[8,128]{1,0:T(8,128)S(1)} %get-tuple-element.19.share_ref, ...), custom_call_target="tpu_custom_call" | custom-call | flops 268435456 | bytes 1019904 | tf_op jit(solution)/shard_map/pallas_call | solution.py:381
  28.4 0.0 copy-start.4
  28.5 0.0 collective-permute-done.4.refs_7_
  28.5 2.7 %collective-permute-done.2.refs_1_ = bf16[2,128,128]{2,1,0:T(8,128)(2,1)S(1)} collective-permute-done((bf16[2,128,128]{2,1,0:T(8,128)(2,1)S(1)}, bf16[2,128,128]{2,1,0:T(8,128)(2,1)S(1)}, u32[]{:S(2)}, u32[]{:S(2)}) %collective-permute-start.2) | collective-permute-done | bytes 65568 | tf_op jit(solution)/shard_map/ppermute | solution.py:390
  31.1 0.0 copy-done
  31.2 0.0 copy-done.1
  31.2 0.0 copy-done.2
  31.2 0.0 copy-done.3
  31.2 1.0 %shard_map.155.refs_4_ = bf16[2,128,128]{2,1,0:T(8,128)(2,1)S(1)} custom-call(bf16[2,128,128]{2,1,0:T(8,128)(2,1)S(1)} %shard_map.153.refs_0_, bf16[2,128,128]{2,1,0:T(8,128)(2,1)S(1)} %collective-permute-done.2.refs_1_, bf16[2,128,256]{2,1,0:T(8,128)(2,1)S(1)} %copy-done, bf16[256,256]{1,0:T(8,128)(2,1)S(1)} %copy-done.3, bf16[256,512]{1,0:T(8,128)(2,1)S(1)} %copy-done.1, ...), custom_call_target="tpu_custom_call" | custom-call | flops 268435456 | bytes 1376256 | tf_op jit(solution)/shard_map/pallas_call | solution.py:381
  32.2 0.0 collective-permute-done.1.refs_1_
  32.2 0.0 copy-done.4
  32.2 0.9 %shard_map.156 = (bf16[8,64,128]{2,1,0:T(8,128)(2,1)}, bf16[2,128,128]{2,1,0:T(8,128)(2,1)}) custom-call(bf16[8,64,128]{2,1,0:T(8,128)(2,1)S(1)} %shard_map.151.refs_0_, bf16[8,64,128]{2,1,0:T(8,128)(2,1)S(1)} %collective-permute-done.1.refs_1_, f32[8,64,128]{2,1,0:T(8,128)S(1)} %shard_map.152.refs_2_, bf16[64,128]{1,0:T(8,128)(2,1)S(1)} %bitcast.9, ...), custom_call_target="tpu_custom_call" | custom-call | flops 67108864 | bytes 802816 | tf_op jit(solution)/shard_map/pallas_call | solution.py:381
Async XLA Ops:
  3.2 16.0 %all-to-all-start = ((bf16[8,120,128]{2,1,0:T(8,128)(2,1)}), bf16[8,120,128]{2,1,0:T(8,128)(2,1)S(1)}, u32[]{:S(2)}, u32[]{:S(2)}) async-start(bf16[8,120,128]{2,1,0:T(8,128)(2,1)} %shard_map.149), calls=%async_computation | async-start | bytes 491520 | tf_op jit(solution)/shard_map/all_to_all | solution.py:452
  11.7 7.5 %collective-permute-start.3 = (bf16[256,384]{1,0:T(8,128)(2,1)S(1)}, bf16[256,384]{1,0:T(8,128)(2,1)S(1)}, u32[]{:S(2)}, u32[]{:S(2)}) collective-permute-start(bf16[256,384]{1,0:T(8,128)(2,1)S(1)} %shard_map.154), channel_id=1, source_target_pairs={{0,1},{1,0},{2,3},{3,2},{4,5},{5,4},{6,7},{7,6},{8,9},{9,8},{10,11... | collective-permute-start | bytes 589832 | tf_op jit(solution)/shard_map/ppermute | solution.py:466
  19.2 4.3 %collective-permute-start = (bf16[8,120,128]{2,1,0:T(8,128)(2,1)S(1)}, bf16[8,120,128]{2,1,0:T(8,128)(2,1)S(1)}, u32[]{:S(2)}, u32[]{:S(2)}) collective-permute-start(bf16[8,120,128]{2,1,0:T(8,128)(2,1)S(1)} %all-to-all-done.mine_ref), channel_id=1, source_target_pairs={{0,2},{2,0},{1,3},{3,1},{4,6},{6,4},{5,7},{7,5},{8,10},{10,8},{9,1... | collective-permute-start | bytes 737288 | tf_op jit(solution)/shard_map/ppermute | solution.py:453
  19.2 9.2 %collective-permute-start.4 = (bf16[256,384]{1,0:T(8,128)(2,1)S(1)}, bf16[256,384]{1,0:T(8,128)(2,1)S(1)}, u32[]{:S(2)}, u32[]{:S(2)}) collective-permute-start(bf16[256,384]{1,0:T(8,128)(2,1)S(1)} %collective-permute-done.3.refs_6_), channel_id=1, source_target_pairs={{0,2},{2,0},{1,3},{3,1},{4,6},{6,4},{5,7},{7,5},{8,10},{10,8},{9,1... | collective-permute-start | bytes 589832 | tf_op jit(solution)/shard_map/ppermute | solution.py:467
  24.3 7.9 %collective-permute-start.1 = (bf16[8,64,128]{2,1,0:T(8,128)(2,1)S(1)}, bf16[8,64,128]{2,1,0:T(8,128)(2,1)S(1)}, u32[]{:S(2)}, u32[]{:S(2)}) collective-permute-start(bf16[8,64,128]{2,1,0:T(8,128)(2,1)S(1)} %shard_map.151.refs_0_), channel_id=1, source_target_pairs={{0,1},{1,0},{2,3},{3,2},{4,5},{5,4},{6,7},{7,6},{8,9},{9,8},{10,11... | collective-permute-start | bytes 393224 | tf_op jit(solution)/shard_map/ppermute | solution.py:390
  26.2 4.9 %collective-permute-start.2 = (bf16[2,128,128]{2,1,0:T(8,128)(2,1)S(1)}, bf16[2,128,128]{2,1,0:T(8,128)(2,1)S(1)}, u32[]{:S(2)}, u32[]{:S(2)}) collective-permute-start(bf16[2,128,128]{2,1,0:T(8,128)(2,1)S(1)} %shard_map.153.refs_0_), channel_id=1, source_target_pairs={{0,1},{1,0},{2,3},{3,2},{4,5},{5,4},{6,7},{7,6},{8,9},{9,8},{10,11... | collective-permute-start | bytes 196616 | tf_op jit(solution)/shard_map/ppermute | solution.py:390
  26.8 4.3 %copy-start = (bf16[2,128,256]{2,1,0:T(8,128)(2,1)S(1)}, bf16[2,128,256]{2,1,0:T(8,128)(2,1)}, u32[]{:S(2)}) copy-start(bf16[2,128,256]{2,1,0:T(8,128)(2,1)} %refs_2_.3) | copy-start | bytes 393220
  26.8 4.3 %copy-start.1 = (bf16[256,512]{1,0:T(8,128)(2,1)S(1)}, bf16[256,512]{1,0:T(8,128)(2,1)}, u32[]{:S(2)}) copy-start(bf16[256,512]{1,0:T(8,128)(2,1)} %refs_4_.1) | copy-start | bytes 786436
  26.9 4.3 %copy-start.2 = (bf16[512,256]{1,0:T(8,128)(2,1)S(1)}, bf16[512,256]{1,0:T(8,128)(2,1)}, u32[]{:S(2)}) copy-start(bf16[512,256]{1,0:T(8,128)(2,1)} %refs_5_.1) | copy-start | bytes 786436
  26.9 4.3 %copy-start.3 = (bf16[256,256]{1,0:T(8,128)(2,1)S(1)}, bf16[256,256]{1,0:T(8,128)(2,1)}, u32[]{:S(2)}) copy-start(bf16[256,256]{1,0:T(8,128)(2,1)} %refs_3_.1) | copy-start | bytes 393220
  28.4 3.7 %copy-start.4 = (bf16[128,64]{0,1:T(8,128)(2,1)S(1)}, bf16[128,64]{0,1:T(8,128)(2,1)}, u32[]{:S(2)}) copy-start(bf16[128,64]{0,1:T(8,128)(2,1)} %param.25) | copy-start | bytes 49156

commit v5 on v4

--- a/solution.py
+++ b/solution.py
@@ -79,12 +79,17 @@
 
 
 def pre_kernel(cores, *refs):
-    pay_ref, held, (bias_ref, factor_ref, in_sem, out_sem) = refs[6], refs[7:13], refs[13:]
+    doubling = len(refs) == 15
+    if doubling:
+        (near_ref, far_ref), held, in_sem = refs[6:8], refs[8:14], refs[14]
+        chips = 8
+    else:
+        pay_ref, held, (bias_ref, factor_ref, in_sem, out_sem) = refs[6], refs[7:13], refs[13:]
+        chips = pay_ref.shape[0]
     copies = fetch(list(zip(refs[:6], held)), in_sem)
     x_ref, p_ref, mb_ref, tb_ref, lr_ref, bounds_ref = held
     seqs, length, _ = x_ref.shape
     rows = p_ref.shape[0]
-    chips = pay_ref.shape[0]
     depth = lr_ref.shape[1]
     first_seq = place_of(cores) * seqs
     for j in (0, 4, 5):
@@ -106,7 +111,8 @@
     right = jnp.concatenate(pieces, axis=0).astype(BF16)
     lanes = left.shape[1]
     group = places((rows, lanes), 1) // (seqs * depth)
-    first, count = bias_ref.shape[1], right.shape[0]
+    first, count = (mb_ref.shape[0] + tb_ref.shape[0]) * rows, right.shape[0]
+    lefts = []
     for d in range(chips):
         mine = left[d * cores * rows : d * cores * rows + rows]
         for c in range(1, cores):
@@ -114,10 +120,21 @@
             mine = jnp.where(group == c, left[begin : begin + rows], mine)
         if lanes < length:
             mine = jnp.concatenate([mine, jnp.zeros((rows, length - lanes), F32)], axis=1)
-        factor_ref[d, 0:count, :] = right
-        factor_ref[d, count : count + rows, :] = mine.astype(BF16)
-    sends = [pltpu.make_async_copy(factor_ref, pay_ref.at[:, first:], out_sem.at[0])]
-    sends[0].start()
+        lefts.append(mine)
+    if doubling:
+        low = lax.axis_index("rows") < chips // 2
+        for k, ref in enumerate((near_ref, far_ref)):
+            ref[first : first + count, :] = right
+            half = chips // 2
+            both = [(lefts[j], lefts[half + j])[:: 1 - 2 * k] for j in range(half)]
+            chosen = jnp.concatenate([jnp.where(low, x, y) for x, y in both], axis=0)
+            ref[first + count : first + count + half * rows, :] = chosen.astype(BF16)
+    else:
+        for d in range(chips):
+            factor_ref[d, 0:count, :] = right
+            factor_ref[d, count : count + rows, :] = lefts[d].astype(BF16)
+        sends = [pltpu.make_async_copy(factor_ref, pay_ref.at[:, first:], out_sem.at[0])]
+        sends[0].start()
     for j in (1, 2, 3):
         copies[j].wait()
     bias_w = jnp.concatenate([mb_ref[...].astype(F32), tb_ref[...].astype(F32)], axis=0)
@@ -126,6 +143,10 @@
     biases = [nt(bias_w, normed(p_ref[i]).astype(BF16)) for i in range(rows)]
     pieces = [jnp.concatenate([b[h : h + 1] for b in biases], axis=0) for h in range(heads)]
     bias = jnp.concatenate(pieces, axis=0).astype(BF16)
+    if doubling:
+        near_ref[0:first, :] = bias
+        far_ref[0:first, :] = bias
+        return
     for d in range(chips):
         bias_ref[d] = bias
     sends.append(pltpu.make_async_copy(bias_ref, pay_ref.at[:, 0:first], out_sem.at[1]))
@@ -192,15 +213,32 @@
         lay_ref[:, step * 128 : (step + 1) * 128] = tile.astype(BF16)
 
 
-def gather_bias(bias_ref, mine_ref, other_ref, first, heads, rows, cores):
-    chips = mine_ref.shape[0]
+def sources(refs):
     core = lax.axis_index("branch")
-    for d in range(chips):
-        for ref, c in ((mine_ref, core), (other_ref, 1 - core)):
-            begin = pl.multiple_of((d * cores + c) * rows, rows)
-            block = ref[d, first * rows : (first + heads) * rows, :].astype(F32) * LOG2E
-            for h in range(heads):
-                bias_ref[h, pl.ds(begin, rows), :] = block[h * rows : (h + 1) * rows]
+    half = len(refs) // 2
+    pairs = list(zip(refs[:half], refs[half:]))
+    found = []
+    if half == 1:
+        for d in range(refs[0].shape[0]):
+            for ref, c in zip(pairs[0], (core, 1 - core)):
+                found.append((lambda lo, hi, ref=ref, d=d: ref[d, lo:hi, :], d, c))
+        return found
+    chip = lax.axis_index("rows")
+    for e, pair in enumerate(pairs):
+        count = pair[0].shape[0] // 2
+        for k in range(2):
+            for ref, c in zip(pair, (core, 1 - core)):
+                read = lambda lo, hi, ref=ref, at=k * count: ref[at + lo : at + hi, :]
+                found.append((read, chip ^ (e + 4 * k), c))
+    return found
+
+
+def gather_bias(bias_ref, refs, first, heads, rows, cores):
+    for read, d, c in sources(refs):
+        begin = pl.multiple_of((d * cores + c) * rows, rows)
+        block = read(first * rows, (first + heads) * rows).astype(F32) * LOG2E
+        for h in range(heads):
+            bias_ref[h, pl.ds(begin, rows), :] = block[h * rows : (h + 1) * rows]
 
 
 def attend(scores, values, gate):
@@ -223,19 +261,21 @@
     return gate * mixed / total
 
 
-def align_kernel(cores, rows, mine_ref, other_ref, sm_ref, v_ref, g_ref, mask_ref, out_ref, bias_ref):
+def align_kernel(cores, rows, *refs):
+    gathered, (sm_ref, v_ref, g_ref, mask_ref, out_ref, bias_ref) = refs[:-6], refs[-6:]
     seqs, heads, _, _ = sm_ref.shape
-    gather_bias(bias_ref, mine_ref, other_ref, 0, heads, rows, cores)
+    gather_bias(bias_ref, gathered, 0, heads, rows, cores)
     for s in range(seqs):
         mask = mask_ref[s : s + 1]
         scores = [sm_ref[s, h] + (bias_ref[h] + mask) for h in range(heads)]
         out_ref[s] = attend(scores, v_ref[s], g_ref[s]).astype(BF16)
 
 
-def tri_kernel(cores, first, mine_ref, other_ref, st_ref, v_ref, g_ref, mask_ref, out_ref, bias_ref):
+def tri_kernel(cores, first, *refs):
+    gathered, (st_ref, v_ref, g_ref, mask_ref, out_ref, bias_ref) = refs[:-6], refs[-6:]
     rows, heads, length, _ = st_ref.shape
     last = mask_ref.shape[0] - 1
-    gather_bias(bias_ref, mine_ref, other_ref, first, heads, rows, cores)
+    gather_bias(bias_ref, gathered, first, heads, rows, cores)
     for h in range(heads):
         bias_ref[h] = bias_ref[h] + mask_ref[last : last + 1]
     ones = jnp.ones((8, length), BF16)
@@ -294,30 +334,36 @@
             out_ref[s, at, :] = out[s * 128 : (s + 1) * 128].astype(BF16)
 
 
-def outer_kernel(cores, seqs, heads, mine_ref, other_ref, w_ref, share_ref, own_ref, out_ref, a_ref, b_ref):
+def outer_kernel(cores, seqs, heads, *refs):
+    found, (w_ref, share_ref, own_ref, out_ref, a_ref, b_ref) = sources(refs[:-6]), refs[-6:]
+    doubling = len(refs) > 8
     rows, width, length = out_ref.shape
-    chips = mine_ref.shape[0]
     depth = w_ref.shape[0]
     lanes = depth * cores * seqs
     groups = 128 // width
     steps = depth // groups
-    total = chips * cores * seqs
+    total = len(found) * seqs
     core = lax.axis_index("branch")
     first = heads * rows
+    last = first + seqs * depth
     lane_group = places((rows, lanes), 1) // depth
-    for d in range(chips):
-        for which, ref in enumerate((mine_ref, other_ref)):
-            block = ref[d, first : first + seqs * depth, :].astype(F32)
-            left = ref[d, first + seqs * depth : first + seqs * depth + rows, :lanes].astype(F32)
-            for s in range(seqs):
-                row = (d * cores + which) * seqs + s
-                for g in range(groups):
-                    begin = s * depth + g * steps
-                    for t in range(length // 128):
-                        piece = block[begin : begin + steps, t * 128 : (t + 1) * 128]
-                        b_ref[g, t, pl.ds(row, steps, stride=total), :] = piece
-                kept = jnp.where(lane_group == core * seqs + s, left, 0.0)
-                a_ref[pl.ds(row, rows, stride=total), :] = kept
+    slot = lax.axis_index("rows") % 4
+    for at_source, (read, _, _) in enumerate(found):
+        block = read(first, last).astype(F32)
+        left = read(last, last + rows)[:, :lanes].astype(F32)
+        if doubling:
+            every = read(last, last + 4 * rows)[:, :lanes].astype(F32)
+            for k in range(1, 4):
+                left = jnp.where(slot == k, every[k * rows : (k + 1) * rows], left)
+        for s in range(seqs):
+            row = at_source * seqs + s
+            for g in range(groups):
+                begin = s * depth + g * steps
+                for t in range(length // 128):
+                    piece = block[begin : begin + steps, t * 128 : (t + 1) * 128]
+                    b_ref[g, t, pl.ds(row, steps, stride=total), :] = piece
+            kept = jnp.where(lane_group == core * seqs + s, left, 0.0)
+            a_ref[pl.ds(row, rows, stride=total), :] = kept
     a = a_ref[...].astype(BF16)
     share = share_ref[...]
     gathered = [[] for _ in range(rows)]
@@ -434,23 +480,42 @@
     bias_rows = every_head * rows
     right_rows = seqs * depth
     hidden = feedfwd_entry_weight.shape[1]
-    (payload,) = call(
-        functools.partial(pre_kernel, cores),
-        first,
-        (((chips, bias_rows + right_rows + rows, length), BF16),),
-        scratch=[
-            *held_copies(first)[:-1],
-            pltpu.VMEM((chips, bias_rows, length), BF16),
-            pltpu.VMEM((chips, right_rows + rows, length), BF16),
-            held_copies(first)[-1],
-            pltpu.SemaphoreType.DMA((2,)),
-        ],
-        left=range(len(first)),
-        written=(0,),
-        grant=60 << 20,
-    )
-    mine = lax.all_to_all(payload, "rows", 0, 0, tiled=True)
-    other = lax.ppermute(mine, "branch", [(0, 1), (1, 0)])
+    swap = [(0, 1), (1, 0)]
+    if chips == 8 and cores == 2:
+        shape = (bias_rows + right_rows + chips // 2 * rows, length)
+        near, far = call(
+            functools.partial(pre_kernel, cores),
+            first,
+            ((shape, BF16), (shape, BF16)),
+            scratch=held_copies(first),
+            left=range(len(first)),
+        )
+        far = lax.ppermute(far, "rows", [(i, i ^ 4) for i in range(8)])
+        both = jnp.concatenate([near, far], axis=0)
+        mine = [both]
+        for e in range(1, 4):
+            mine.append(lax.ppermute(both, "rows", [(i, i ^ e) for i in range(8)]))
+        other = []
+        for e in range(4):
+            other.append(lax.ppermute(mine[e], "branch", swap))
+    else:
+        (payload,) = call(
+            functools.partial(pre_kernel, cores),
+            first,
+            (((chips, bias_rows + right_rows + rows, length), BF16),),
+            scratch=[
+                *held_copies(first)[:-1],
+                pltpu.VMEM((chips, bias_rows, length), BF16),
+                pltpu.VMEM((chips, right_rows + rows, length), BF16),
+                held_copies(first)[-1],
+                pltpu.SemaphoreType.DMA((2,)),
+            ],
+            left=range(len(first)),
+            written=(0,),
+            grant=60 << 20,
+        )
+        mine = [lax.all_to_all(payload, "rows", 0, 0, tiled=True)]
+        other = [lax.ppermute(mine[0], "branch", swap)]
 
     if parts == 2 and cores == 2 and hidden == cores * channels:
         shape = (channels, hidden // cores + channels // parts)
@@ -509,7 +574,7 @@
 
     (mixed,) = call(
         functools.partial(align_kernel, cores, rows),
-        (mine, other, scores, values, gate, masks),
+        (*mine, *other, scores, values, gate, masks),
         (((seqs, length, features), BF16),),
         scratch=[pltpu.VMEM((heads, length, length), F32)],
         flops=1 << 28,
@@ -517,7 +582,7 @@
     mixed = from_heads(mixed)
     (pair_mixed,) = call(
         functools.partial(tri_kernel, cores, heads),
-        (mine, other, tri_scores, tri_values, tri_gate, masks),
+        (*mine, *other, tri_scores, tri_values, tri_gate, masks),
         (((rows, pair_features, length), BF16),),
         scratch=[pltpu.VMEM((pair_heads, length, length), F32)],
         flops=1 << 28,
@@ -535,7 +600,7 @@
 
     (opm,) = call(
         functools.partial(outer_kernel, cores, seqs, every_head),
-        (mine, other, outer_w, shares, own_pair),
+        (*mine, *other, outer_w, shares, own_pair),
         (((rows, width, length), F32),),
         scratch=[
             pltpu.VMEM((rows * total, depth * cores * seqs), F32),

time: 33.4 us -> 31.9 us (0.955)
  waiting for transfers between devices: 8.66 us -> 7.56 us
  Pallas kernels: 12.2 us -> 11.5 us
  starting transfers between devices: 11.5 us -> 11.9 us
    ppermute x1 -> x8, starting transfers between devices: 0.01 us -> 7.69 us  [the longest x1 4.13 us: local(): far = lax.ppermute(far, 'rows', [(i, i ^ 4) for i in range(8)])]
    all_to_all x1 -> x0, starting transfers between devices: 7.32 us -> none  [local(): mine = lax.all_to_all(payload, 'rows', 0, 0, tiled=True)]
    all_to_all x1 -> x0, waiting for transfers between devices: 5.97 us -> none  [local(): mine = lax.all_to_all(payload, 'rows', 0, 0, tiled=True)]
    ppermute x1 -> x8, waiting for transfers between devices: 0.01 us -> 4.86 us  [the longest x3 4.85 us: local(): mine.append(lax.ppermute(both, 'rows', [(i, i ^ e) for i in range(8)]))]
    pallas_call x8, Pallas kernels: 12.2 us -> 11.5 us  [call(): return run(*ins)]
  transfers between devices with their start and end apart: 6 -> 12, of which waited for: 2 -> 4; matrix products, arithmetic and copies ran while one was open for 0% -> 0% of each run, Pallas kernels for 26% -> 27%
where the time goes in v5:
time: 31.9 us; the launch traced here: 31.8 us
  starting transfers between devices  11.9 us (37%)
  Pallas kernels  11.5 us (36%)
  waiting for transfers between devices  7.56 us (24%)
  between operations  0.76 us (2%)
    pallas_call x8, Pallas kernels, call(): return run(*ins)  11.5 us
    ppermute x3, waiting for transfers between devices, local(): mine.append(lax.ppermute(both, 'rows', [(i, i ^ e) for i in range(8)]))  4.85 us
    ppermute x1, starting transfers between devices, local(): far = lax.ppermute(far, 'rows', [(i, i ^ 4) for i in range(8)])  4.13 us
    ppermute x3, starting transfers between devices, local(): mine.append(lax.ppermute(both, 'rows', [(i, i ^ e) for i in range(8)]))  3.55 us
    ppermute x2, waiting for transfers between devices, from_heads(): return [value, lax.ppermute(value, 'head', [(0, 1), (1, 0)])]  2.69 us
    ppermute x2, starting transfers between devices, from_heads(): return [value, lax.ppermute(value, 'head', [(0, 1), (1, 0)])]  2.15 us
    ppermute x1, starting transfers between devices, local(): others = [lax.ppermute(packed, 'head', [(0, 1), (1, 0)])]  1.56 us
  transfers between devices with their start and end apart: 12, of which 4 were waited for; matrix products, arithmetic and copies ran while one was open for 0% of the time, Pallas kernels for 27%

profile of v5, /device:TPU:0, one launch (start us, length us, event | category | flops | bytes accessed | tf_op | source)
XLA Modules:
  0.0 31.8 jit_solution(6123942775733718502)
XLA Ops:
  0.6 1.9 %shard_map.149 = (bf16[144,128]{1,0:T(8,128)(2,1)S(1)}, bf16[144,128]{1,0:T(8,128)(2,1)S(1)}) custom-call(bf16[2,128,256]{2,1,0:T(8,128)(2,1)} %refs_2_.3, bf16[8,128,128]{2,1,0:T(8,128)(2,1)} %refs_1_.3, bf16[4,128]{1,0:T(4,128)(2,1)} %bitcast.11, bf16[2,128]{1,0:T(2,128)(2,1)} %bitcast.14, bf16[2,32,256]{2,1,0:T(8,128)(2,1)} %bitcast.10, s32[2,32]{1,0:T(2,128)} %bitcast.12), custom_call_target="tpu_custom_call" | custom-call | bytes 501504 | tf_op jit(solution)/shard_map/pallas_call | solution.py:427
  2.6 4.1 %collective-permute-start = (bf16[144,128]{1,0:T(8,128)(2,1)S(1)}, bf16[144,128]{1,0:T(8,128)(2,1)S(1)}, u32[]{:S(2)}, u32[]{:S(2)}) collective-permute-start(bf16[144,128]{1,0:T(8,128)(2,1)S(1)} %get-tuple-element.17), channel_id=1, source_target_pairs={{0,16},{4,20},{8,24},{12,28},{16,0},{20,4},{24,8},{28,12},{1,17},{... | collective-permute-start | bytes 110600 | tf_op jit(solution)/shard_map/ppermute | solution.py:493
  6.7 1.1 %shard_map.154 = bf16[256,384]{1,0:T(8,128)(2,1)S(1)} custom-call(bf16[256,512]{1,0:T(8,128)(2,1)} %refs_4_.1, bf16[512,256]{1,0:T(8,128)(2,1)} %refs_5_.1), custom_call_target="tpu_custom_call" | custom-call | flops 268435456 | bytes 720896 | tf_op jit(solution)/shard_map/pallas_call | solution.py:427
  7.9 1.6 %collective-permute-start.10 = (bf16[256,384]{1,0:T(8,128)(2,1)S(1)}, bf16[256,384]{1,0:T(8,128)(2,1)S(1)}, u32[]{:S(2)}, u32[]{:S(2)}) collective-permute-start(bf16[256,384]{1,0:T(8,128)(2,1)S(1)} %shard_map.154), channel_id=1, source_target_pairs={{0,1},{1,0},{2,3},{3,2},{4,5},{5,4},{6,7},{7,6},{8,9},{9,8},{10,11... | collective-permute-start | bytes 589832 | tf_op jit(solution)/shard_map/ppermute | solution.py:531
  9.4 0.0 collective-permute-done
  9.4 1.6 %collective-permute-start.1 = (bf16[288,128]{1,0:T(8,128)(2,1)S(1)}, bf16[288,128]{1,0:T(8,128)(2,1)S(1)}, u32[]{:S(2)}, u32[]{:S(2)}) collective-permute-start(bf16[288,128]{1,0:T(8,128)(2,1)S(1)} %constant_dynamic-update-slice_fusion.refs_0_), channel_id=1, source_target_pairs={{0,4},{4,0},{8,12},{12,8},{16,20},{20,16},{24,28},{28,24},{1,5},{5... | collective-permute-start | bytes 221192 | tf_op jit(solution)/shard_map/ppermute | solution.py:497
  11.0 1.6 %collective-permute-start.2 = (bf16[288,128]{1,0:T(8,128)(2,1)S(1)}, bf16[288,128]{1,0:T(8,128)(2,1)S(1)}, u32[]{:S(2)}, u32[]{:S(2)}) collective-permute-start(bf16[288,128]{1,0:T(8,128)(2,1)S(1)} %constant_dynamic-update-slice_fusion.refs_0_), channel_id=1, source_target_pairs={{0,8},{4,12},{8,0},{12,4},{16,24},{20,28},{24,16},{28,20},{1,9},{5... | collective-permute-start | bytes 221192 | tf_op jit(solution)/shard_map/ppermute | solution.py:497
  12.6 0.4 %collective-permute-start.3 = (bf16[288,128]{1,0:T(8,128)(2,1)S(1)}, bf16[288,128]{1,0:T(8,128)(2,1)S(1)}, u32[]{:S(2)}, u32[]{:S(2)}) collective-permute-start(bf16[288,128]{1,0:T(8,128)(2,1)S(1)} %constant_dynamic-update-slice_fusion.refs_0_), channel_id=1, source_target_pairs={{0,12},{4,8},{8,4},{12,0},{16,28},{20,24},{24,20},{28,16},{1,13},{... | collective-permute-start | bytes 221192 | tf_op jit(solution)/shard_map/ppermute | solution.py:497
  13.0 0.0 collective-permute-start.4
  13.0 0.9 %collective-permute-done.1.refs_1_ = bf16[288,128]{1,0:T(8,128)(2,1)S(1)} collective-permute-done((bf16[288,128]{1,0:T(8,128)(2,1)S(1)}, bf16[288,128]{1,0:T(8,128)(2,1)S(1)}, u32[]{:S(2)}, u32[]{:S(2)}) %collective-permute-start.1) | collective-permute-done | bytes 73760 | tf_op jit(solution)/shard_map/ppermute | solution.py:497
  13.9 0.0 collective-permute-start.5
  13.9 1.6 %collective-permute-done.2.refs_2_ = bf16[288,128]{1,0:T(8,128)(2,1)S(1)} collective-permute-done((bf16[288,128]{1,0:T(8,128)(2,1)S(1)}, bf16[288,128]{1,0:T(8,128)(2,1)S(1)}, u32[]{:S(2)}, u32[]{:S(2)}) %collective-permute-start.2) | collective-permute-done | bytes 73760 | tf_op jit(solution)/shard_map/ppermute | solution.py:497
  15.4 0.0 collective-permute-start.6
  15.4 2.4 %collective-permute-done.3.refs_3_ = bf16[288,128]{1,0:T(8,128)(2,1)S(1)} collective-permute-done((bf16[288,128]{1,0:T(8,128)(2,1)S(1)}, bf16[288,128]{1,0:T(8,128)(2,1)S(1)}, u32[]{:S(2)}, u32[]{:S(2)}) %collective-permute-start.3) | collective-permute-done | bytes 73760 | tf_op jit(solution)/shard_map/ppermute | solution.py:497
  17.8 0.0 collective-permute-start.7
  17.8 0.0 collective-permute-done.10.refs_6_
  17.9 0.5 %collective-permute-start.11 = (bf16[256,384]{1,0:T(8,128)(2,1)S(1)}, bf16[256,384]{1,0:T(8,128)(2,1)S(1)}, u32[]{:S(2)}, u32[]{:S(2)}) collective-permute-start(bf16[256,384]{1,0:T(8,128)(2,1)S(1)} %collective-permute-done.10.refs_6_), channel_id=1, source_target_pairs={{0,2},{2,0},{1,3},{3,1},{4,6},{6,4},{5,7},{7,5},{8,10},{10,8},{9,1... | collective-permute-start | bytes 589832 | tf_op jit(solution)/shard_map/ppermute | solution.py:532
  18.4 3.7 %shard_map.150 = (f32[2,4,128,128]{3,2,1,0:T(8,128)S(1)}, bf16[2,128,128]{2,1,0:T(8,128)(2,1)S(1)}, f32[2,128,128]{2,1,0:T(8,128)S(1)}, f32[8,2,128,128]{3,2,1,0...) custom-call(bf16[2,128,256]{2,1,0:T(8,128)(2,1)} %refs_2_.3, ...), custom_call_target="tpu_custom_call" | custom-call | flops 268435456 | bytes 3283200 | tf_op jit(solution)/shard_map/pallas_call | solution.py:427
  22.1 0.0 collective-permute-done.4.refs_4_
  22.1 0.0 collective-permute-done.5.refs_5_
  22.1 0.0 collective-permute-done.6.refs_6_
  22.1 0.0 collective-permute-done.7.refs_7_
  22.1 0.8 %shard_map.151.refs_0_ = bf16[8,64,128]{2,1,0:T(8,128)(2,1)S(1)} custom-call(bf16[288,128]{1,0:T(8,128)(2,1)S(1)} %constant_dynamic-update-slice_fusion.refs_0_, bf16[288,128]{1,0:T(8,128)(2,1)S(1)} %collective-permute-done.1.refs_1_, bf16[288,128]{1,0:T(8,128)(2,1)S(1)} %collective-permute-done.2.refs_2_, ...), custom_call_target="tpu_custom_call" | custom-call | flops 268435456 | bytes 2164224 | tf_op jit(solution)/shard_map/pallas_call | solution.py:427
  22.9 1.1 %collective-permute-start.8 = (bf16[8,64,128]{2,1,0:T(8,128)(2,1)S(1)}, bf16[8,64,128]{2,1,0:T(8,128)(2,1)S(1)}, u32[]{:S(2)}, u32[]{:S(2)}) collective-permute-start(bf16[8,64,128]{2,1,0:T(8,128)(2,1)S(1)} %shard_map.151.refs_0_), channel_id=1, source_target_pairs={{0,1},{1,0},{2,3},{3,2},{4,5},{5,4},{6,7},{7,6},{8,9},{9,8},{10,11... | collective-permute-start | bytes 393224 | tf_op jit(solution)/shard_map/ppermute | solution.py:436
  24.0 0.4 %shard_map.153.refs_0_ = bf16[2,128,128]{2,1,0:T(8,128)(2,1)S(1)} custom-call(bf16[288,128]{1,0:T(8,128)(2,1)S(1)} %constant_dynamic-update-slice_fusion.refs_0_, bf16[288,128]{1,0:T(8,128)(2,1)S(1)} %collective-permute-done.1.refs_1_, bf16[288,128]{1,0:T(8,128)(2,1)S(1)} %collective-permute-done.2.refs_2_, ...), custom_call_target="tpu_custom_call" | custom-call | flops 268435456 | bytes 1377792 | tf_op jit(solution)/shard_map/pallas_call | solution.py:427
  24.4 1.0 %collective-permute-start.9 = (bf16[2,128,128]{2,1,0:T(8,128)(2,1)S(1)}, bf16[2,128,128]{2,1,0:T(8,128)(2,1)S(1)}, u32[]{:S(2)}, u32[]{:S(2)}) collective-permute-start(bf16[2,128,128]{2,1,0:T(8,128)(2,1)S(1)} %shard_map.153.refs_0_), channel_id=1, source_target_pairs={{0,1},{1,0},{2,3},{3,2},{4,5},{5,4},{6,7},{7,6},{8,9},{9,8},{10,11... | collective-permute-start | bytes 196616 | tf_op jit(solution)/shard_map/ppermute | solution.py:436
  25.5 0.0 copy-start
  25.5 0.0 copy-start.1
  25.5 0.0 copy-start.2
  25.5 0.0 copy-start.3
  25.5 1.6 %shard_map.152.refs_2_ = f32[8,64,128]{2,1,0:T(8,128)S(1)} custom-call(bf16[288,128]{1,0:T(8,128)(2,1)S(1)} %constant_dynamic-update-slice_fusion.refs_0_, bf16[288,128]{1,0:T(8,128)(2,1)S(1)} %collective-permute-done.1.refs_1_, bf16[288,128]{1,0:T(8,128)(2,1)S(1)} %collective-permute-done.2.refs_2_, bf16[288,128]{1,0:T(8,128)(2,1)S(1)} %collective-permute-done.3.refs_3_, ...), custom_call_target="tpu_custom_call" | custom-call | flops 268435456 | bytes 1118208 | tf_op jit(solution)/shard_map/pallas_call | solution.py:427
  27.1 0.0 copy-start.4
  27.1 2.7 %collective-permute-done.9.refs_1_ = bf16[2,128,128]{2,1,0:T(8,128)(2,1)S(1)} collective-permute-done((bf16[2,128,128]{2,1,0:T(8,128)(2,1)S(1)}, bf16[2,128,128]{2,1,0:T(8,128)(2,1)S(1)}, u32[]{:S(2)}, u32[]{:S(2)}) %collective-permute-start.9) | collective-permute-done | bytes 65568 | tf_op jit(solution)/shard_map/ppermute | solution.py:436
  29.8 0.0 collective-permute-done.11.refs_7_
  29.8 0.0 copy-done
  29.8 0.0 copy-done.1
  29.8 0.0 copy-done.2
  29.8 0.0 copy-done.3
  29.8 1.0 %shard_map.155.refs_4_ = bf16[2,128,128]{2,1,0:T(8,128)(2,1)S(1)} custom-call(bf16[2,128,128]{2,1,0:T(8,128)(2,1)S(1)} %shard_map.153.refs_0_, bf16[2,128,128]{2,1,0:T(8,128)(2,1)S(1)} %collective-permute-done.9.refs_1_, bf16[2,128,256]{2,1,0:T(8,128)(2,1)S(1)} %copy-done, bf16[256,256]{1,0:T(8,128)(2,1)S(1)} %copy-done.3, bf16[256,512]{1,0:T(8,128)(2,1)S(1)} %copy-done.1, ...), custom_call_target="tpu_custom_call" | custom-call | flops 268435456 | bytes 1376256 | tf_op jit(solution)/shard_map/pallas_call | solution.py:427
  30.8 0.0 collective-permute-done.8.refs_1_
  30.8 0.0 copy-done.4
  30.8 0.9 %shard_map.156 = (bf16[8,64,128]{2,1,0:T(8,128)(2,1)}, bf16[2,128,128]{2,1,0:T(8,128)(2,1)}) custom-call(bf16[8,64,128]{2,1,0:T(8,128)(2,1)S(1)} %shard_map.151.refs_0_, bf16[8,64,128]{2,1,0:T(8,128)(2,1)S(1)} %collective-permute-done.8.refs_1_, f32[8,64,128]{2,1,0:T(8,128)S(1)} %shard_map.152.refs_2_, bf16[64,128]{1,0:T(8,128)(2,1)S(1)} %bitcast.9, ...), custom_call_target="tpu_custom_call" | custom-call | flops 67108864 | bytes 802816 | tf_op jit(solution)/shard_map/pallas_call | solution.py:427
  (2 shorter events, 0.0 us)
Async XLA Ops:
  2.6 6.8 %collective-permute-start = (bf16[144,128]{1,0:T(8,128)(2,1)S(1)}, bf16[144,128]{1,0:T(8,128)(2,1)S(1)}, u32[]{:S(2)}, u32[]{:S(2)}) collective-permute-start(bf16[144,128]{1,0:T(8,128)(2,1)S(1)} %get-tuple-element.17), channel_id=1, source_target_pairs={{0,16},{4,20},{8,24},{12,28},{16,0},{20,4},{24,8},{28,12},{1,17},{... | collective-permute-start | bytes 110600 | tf_op jit(solution)/shard_map/ppermute | solution.py:493
  7.9 10.0 %collective-permute-start.10 = (bf16[256,384]{1,0:T(8,128)(2,1)S(1)}, bf16[256,384]{1,0:T(8,128)(2,1)S(1)}, u32[]{:S(2)}, u32[]{:S(2)}) collective-permute-start(bf16[256,384]{1,0:T(8,128)(2,1)S(1)} %shard_map.154), channel_id=1, source_target_pairs={{0,1},{1,0},{2,3},{3,2},{4,5},{5,4},{6,7},{7,6},{8,9},{9,8},{10,11... | collective-permute-start | bytes 589832 | tf_op jit(solution)/shard_map/ppermute | solution.py:531
  9.4 4.4 %collective-permute-start.1 = (bf16[288,128]{1,0:T(8,128)(2,1)S(1)}, bf16[288,128]{1,0:T(8,128)(2,1)S(1)}, u32[]{:S(2)}, u32[]{:S(2)}) collective-permute-start(bf16[288,128]{1,0:T(8,128)(2,1)S(1)} %constant_dynamic-update-slice_fusion.refs_0_), channel_id=1, source_target_pairs={{0,4},{4,0},{8,12},{12,8},{16,20},{20,16},{24,28},{28,24},{1,5},{5... | collective-permute-start | bytes 221192 | tf_op jit(solution)/shard_map/ppermute | solution.py:497
  11.0 4.4 %collective-permute-start.2 = (bf16[288,128]{1,0:T(8,128)(2,1)S(1)}, bf16[288,128]{1,0:T(8,128)(2,1)S(1)}, u32[]{:S(2)}, u32[]{:S(2)}) collective-permute-start(bf16[288,128]{1,0:T(8,128)(2,1)S(1)} %constant_dynamic-update-slice_fusion.refs_0_), channel_id=1, source_target_pairs={{0,8},{4,12},{8,0},{12,4},{16,24},{20,28},{24,16},{28,20},{1,9},{5... | collective-permute-start | bytes 221192 | tf_op jit(solution)/shard_map/ppermute | solution.py:497
  12.6 5.3 %collective-permute-start.3 = (bf16[288,128]{1,0:T(8,128)(2,1)S(1)}, bf16[288,128]{1,0:T(8,128)(2,1)S(1)}, u32[]{:S(2)}, u32[]{:S(2)}) collective-permute-start(bf16[288,128]{1,0:T(8,128)(2,1)S(1)} %constant_dynamic-update-slice_fusion.refs_0_), channel_id=1, source_target_pairs={{0,12},{4,8},{8,4},{12,0},{16,28},{20,24},{24,20},{28,16},{1,13},{... | collective-permute-start | bytes 221192 | tf_op jit(solution)/shard_map/ppermute | solution.py:497
  13.0 9.1 %collective-permute-start.4 = (bf16[288,128]{1,0:T(8,128)(2,1)S(1)}, bf16[288,128]{1,0:T(8,128)(2,1)S(1)}, u32[]{:S(2)}, u32[]{:S(2)}) collective-permute-start(bf16[288,128]{1,0:T(8,128)(2,1)S(1)} %constant_dynamic-update-slice_fusion.refs_0_), channel_id=1, source_target_pairs={{0,2},{2,0},{1,3},{3,1},{4,6},{6,4},{5,7},{7,5},{8,10},{10,8},{9,1... | collective-permute-start | bytes 221192 | tf_op jit(solution)/shard_map/ppermute | solution.py:500
  13.9 8.3 %collective-permute-start.5 = (bf16[288,128]{1,0:T(8,128)(2,1)S(1)}, bf16[288,128]{1,0:T(8,128)(2,1)S(1)}, u32[]{:S(2)}, u32[]{:S(2)}) collective-permute-start(bf16[288,128]{1,0:T(8,128)(2,1)S(1)} %collective-permute-done.1.refs_1_), channel_id=1, source_target_pairs={{0,2},{2,0},{1,3},{3,1},{4,6},{6,4},{5,7},{7,5},{8,10},{10,8},{9,1... | collective-permute-start | bytes 221192 | tf_op jit(solution)/shard_map/ppermute | solution.py:500
  15.4 6.7 %collective-permute-start.6 = (bf16[288,128]{1,0:T(8,128)(2,1)S(1)}, bf16[288,128]{1,0:T(8,128)(2,1)S(1)}, u32[]{:S(2)}, u32[]{:S(2)}) collective-permute-start(bf16[288,128]{1,0:T(8,128)(2,1)S(1)} %collective-permute-done.2.refs_2_), channel_id=1, source_target_pairs={{0,2},{2,0},{1,3},{3,1},{4,6},{6,4},{5,7},{7,5},{8,10},{10,8},{9,1... | collective-permute-start | bytes 221192 | tf_op jit(solution)/shard_map/ppermute | solution.py:500
  17.8 4.3 %collective-permute-start.7 = (bf16[288,128]{1,0:T(8,128)(2,1)S(1)}, bf16[288,128]{1,0:T(8,128)(2,1)S(1)}, u32[]{:S(2)}, u32[]{:S(2)}) collective-permute-start(bf16[288,128]{1,0:T(8,128)(2,1)S(1)} %collective-permute-done.3.refs_3_), channel_id=1, source_target_pairs={{0,2},{2,0},{1,3},{3,1},{4,6},{6,4},{5,7},{7,5},{8,10},{10,8},{9,1... | collective-permute-start | bytes 221192 | tf_op jit(solution)/shard_map/ppermute | solution.py:500
  17.9 11.9 %collective-permute-start.11 = (bf16[256,384]{1,0:T(8,128)(2,1)S(1)}, bf16[256,384]{1,0:T(8,128)(2,1)S(1)}, u32[]{:S(2)}, u32[]{:S(2)}) collective-permute-start(bf16[256,384]{1,0:T(8,128)(2,1)S(1)} %collective-permute-done.10.refs_6_), channel_id=1, source_target_pairs={{0,2},{2,0},{1,3},{3,1},{4,6},{6,4},{5,7},{7,5},{8,10},{10,8},{9,1... | collective-permute-start | bytes 589832 | tf_op jit(solution)/shard_map/ppermute | solution.py:532
  22.9 7.9 %collective-permute-start.8 = (bf16[8,64,128]{2,1,0:T(8,128)(2,1)S(1)}, bf16[8,64,128]{2,1,0:T(8,128)(2,1)S(1)}, u32[]{:S(2)}, u32[]{:S(2)}) collective-permute-start(bf16[8,64,128]{2,1,0:T(8,128)(2,1)S(1)} %shard_map.151.refs_0_), channel_id=1, source_target_pairs={{0,1},{1,0},{2,3},{3,2},{4,5},{5,4},{6,7},{7,6},{8,9},{9,8},{10,11... | collective-permute-start | bytes 393224 | tf_op jit(solution)/shard_map/ppermute | solution.py:436
  24.4 5.3 %collective-permute-start.9 = (bf16[2,128,128]{2,1,0:T(8,128)(2,1)S(1)}, bf16[2,128,128]{2,1,0:T(8,128)(2,1)S(1)}, u32[]{:S(2)}, u32[]{:S(2)}) collective-permute-start(bf16[2,128,128]{2,1,0:T(8,128)(2,1)S(1)} %shard_map.153.refs_0_), channel_id=1, source_target_pairs={{0,1},{1,0},{2,3},{3,2},{4,5},{5,4},{6,7},{7,6},{8,9},{9,8},{10,11... | collective-permute-start | bytes 196616 | tf_op jit(solution)/shard_map/ppermute | solution.py:436
  25.5 4.3 %copy-start = (bf16[2,128,256]{2,1,0:T(8,128)(2,1)S(1)}, bf16[2,128,256]{2,1,0:T(8,128)(2,1)}, u32[]{:S(2)}) copy-start(bf16[2,128,256]{2,1,0:T(8,128)(2,1)} %refs_2_.3) | copy-start | bytes 393220
  25.5 4.3 %copy-start.1 = (bf16[256,512]{1,0:T(8,128)(2,1)S(1)}, bf16[256,512]{1,0:T(8,128)(2,1)}, u32[]{:S(2)}) copy-start(bf16[256,512]{1,0:T(8,128)(2,1)} %refs_4_.1) | copy-start | bytes 786436
  25.5 4.3 %copy-start.2 = (bf16[512,256]{1,0:T(8,128)(2,1)S(1)}, bf16[512,256]{1,0:T(8,128)(2,1)}, u32[]{:S(2)}) copy-start(bf16[512,256]{1,0:T(8,128)(2,1)} %refs_5_.1) | copy-start | bytes 786436
  25.5 4.3 %copy-start.3 = (bf16[256,256]{1,0:T(8,128)(2,1)S(1)}, bf16[256,256]{1,0:T(8,128)(2,1)}, u32[]{:S(2)}) copy-start(bf16[256,256]{1,0:T(8,128)(2,1)} %refs_3_.1) | copy-start | bytes 393220
  27.1 3.7 %copy-start.4 = (bf16[128,64]{0,1:T(8,128)(2,1)S(1)}, bf16[128,64]{0,1:T(8,128)(2,1)}, u32[]{:S(2)}) copy-start(bf16[128,64]{0,1:T(8,128)(2,1)} %param.25) | copy-start | bytes 49156
